TPU v7x, 32 devices: a whole 2x2x4 slice. The times are simulated.
32 devices in a mesh: arcs: 2 (over y), seg: 16 (over z, x, core).
Axes of the slice: x: 2, y: 2, z: 4, core: 2. Of those that a mesh axis runs over, the one named last changes fastest.
Arguments:
- pulses: bfloat16 [2, 8192, 256], P(None, ('arcs', 'seg')), parts along dimension 1, may hold values from -6 to 6
- fraction: float32 [8192], P(('arcs', 'seg')), parts along dimension 0, may hold values from 0 to 1
- gate_shift: int32 [8192], P(('arcs', 'seg')), parts along dimension 0, may hold values from 0 to 15
- aperture_start: int32 [4096], P(('arcs', 'seg')), parts along dimension 0, may hold values from 0 to 4095, as said below
- aperture_end: int32 [4096], P(('arcs', 'seg')), parts along dimension 0, may hold values from 257 to 4096, as said below
- doppler: float32 [4096], P(('arcs', 'seg')), parts along dimension 0, may hold values from -2000 to 2000
- chirp_rate: float32 [4096], P(('arcs', 'seg')), parts along dimension 0, may hold values from 2000 to 6000
Outputs:
- focused: bfloat16 [2, 4096, 256], P(None, ('arcs', 'seg')), parts along dimension 1
- multilook: float32 [4096, 256], P(('arcs', 'seg')), parts along dimension 0
There are 2 independent parts, one for each index of `arcs`. A program takes and returns all parts, laid end to end along the dimension named above; each array names one. Nothing has to cross between parts.
Inputs may be any that keep to these rules, and one draw needn't show every extreme that they name: aperture_start[w] >= (w // 128 - 4) * 256, with equality for some waveform; aperture_end[w] - aperture_start[w] >= 257. aperture_end[w] <= (w // 128 + 5) * 256, with equality for some waveform; aperture_start[w] < aperture_end[w].
All inputs are finite; a program needn't handle non-finite values.
Results may differ from a plain program's by a relative error of at most 0.0064.
Values may be sent and summed in bfloat16 or wider, within the bound.
No kernel may reach another device: no remote copies, remote signals or barrier semaphores. Data moves between devices by JAX's collectives and lax.ppermute only.
A program may use at most 64 MiB of HBM per device.

v0:
```python
import jax
import jax.numpy as jnp
from jax import lax
from jax.sharding import PartitionSpec as P

G = 256
P_DEV = 256
REACH = 4
LOOK = 8
SHIFT_MAX = 16


def from_behind(array, axis, by):
    devices = lax.axis_size(axis)
    pairs = [(i, i + by) for i in range(devices) if 0 <= i + by < devices]
    return lax.ppermute(array, axis, pairs)


def padded(array, sides, width):
    for axis, dim in sides:
        devices, length = (lax.axis_size(axis), array.shape[dim])
        up = [(i, (i + 1) % devices) for i in range(devices - 1)]
        down = [(j, i) for i, j in up]
        last = lax.slice_in_dim(array, length - width, length, axis=dim)
        initial = lax.slice_in_dim(array, 0, width, axis=dim)
        before = lax.ppermute(last, axis, up)
        after = lax.ppermute(initial, axis, down)
        array = jnp.concatenate([before, array, after], axis=dim)
    return array


def migrate(pulses, fraction, gate_shift):
    widened = jnp.pad(pulses.astype(jnp.float32), ((0, 0), (0, 0), (0, SHIFT_MAX + 1)))
    blend = fraction[None, :, None]
    shift_col = gate_shift[None, :, None]
    result = jnp.zeros(pulses.shape, jnp.float32)
    for gate_step in range(SHIFT_MAX + 1):
        coeff = jnp.where(shift_col == gate_step, 1.0 - blend, 0.0) + jnp.where(
            shift_col + 1 == gate_step, blend, 0.0
        )
        result = result + coeff * widened[:, :, gate_step : gate_step + G]
    return result.astype(jnp.bfloat16)


def weights(first_pulse, last_pulse, doppler, chirp_rate, pulse_index):
    center = (first_pulse + last_pulse) // 2
    relative = (pulse_index[None, :] - center[:, None]).astype(jnp.float32) / float(REACH * P_DEV)
    phase_angle = chirp_rate[:, None] * relative * relative + doppler[:, None] * relative
    inside = (pulse_index[None, :] >= first_pulse[:, None]) & (
        pulse_index[None, :] < last_pulse[:, None]
    )
    amplitude = lax.rsqrt((last_pulse - first_pulse).astype(jnp.float32))[:, None]
    weight_re = jnp.where(inside, amplitude * jnp.cos(phase_angle), 0.0).astype(jnp.bfloat16)
    weight_im = jnp.where(inside, amplitude * jnp.sin(phase_angle), 0.0).astype(jnp.bfloat16)
    return (weight_re, weight_im)


def focus_block(weight_re, weight_im, block_data):
    real_part = jnp.dot(weight_re, block_data[0], preferred_element_type=jnp.float32) - jnp.dot(
        weight_im, block_data[1], preferred_element_type=jnp.float32
    )
    imag_part = jnp.dot(weight_re, block_data[1], preferred_element_type=jnp.float32) + jnp.dot(
        weight_im, block_data[0], preferred_element_type=jnp.float32
    )
    return jnp.stack([real_part, imag_part])


def settle(term):
    rounded = lax.optimization_barrier(term.astype(jnp.bfloat16))
    return rounded.astype(jnp.float32)


def shards(pulses, fraction, gate_shift, aperture_start, aperture_end, doppler, chirp_rate):
    device = lax.axis_index("seg")
    pulse_count = pulses.shape[1]
    wave_count = aperture_start.shape[0]
    local_index = jnp.arange(pulse_count, dtype=jnp.int32)
    migrated = migrate(pulses, fraction, gate_shift)

    def own_focus(block_data, block_owner):
        weight_re, weight_im = weights(
            aperture_start,
            aperture_end,
            doppler,
            chirp_rate,
            block_owner * pulse_count + local_index,
        )
        return focus_block(weight_re, weight_im, block_data)

    summed = settle(own_focus(migrated, device))
    for offset in range(1, REACH + 1):
        from_lower = from_behind(migrated, "seg", offset)
        from_upper = from_behind(migrated, "seg", -offset)
        summed = (
            summed
            + settle(own_focus(from_lower, device - offset))
            + settle(own_focus(from_upper, device + offset))
        )
    power_sum = summed[0] * summed[0] + summed[1] * summed[1]
    power_pad = padded(power_sum.astype(jnp.bfloat16), (("seg", 0),), LOOK).astype(power_sum.dtype)
    looked = jnp.zeros((wave_count, power_sum.shape[1]), jnp.float32)
    for shift_row in range(2 * LOOK + 1):
        looked = looked + power_pad[shift_row : shift_row + wave_count]
    multilook = looked / float(2 * LOOK + 1)
    return (summed.astype(jnp.bfloat16), multilook)


def solution(mesh):
    return jax.shard_map(
        shards,
        mesh=mesh,
        in_specs=(
            P(None, ("arcs", "seg"), None),
            P(("arcs", "seg")),
            P(("arcs", "seg")),
            P(("arcs", "seg")),
            P(("arcs", "seg")),
            P(("arcs", "seg")),
            P(("arcs", "seg")),
        ),
        out_specs=(P(None, ("arcs", "seg"), None), P(("arcs", "seg"), None)),
        check_vma=False,
    )
```

profile of v0, /device:TPU:3, one launch (start us, length us, event | category | flops | bytes accessed | tf_op | source)
XLA Modules:
  0.0 66.9 jit_solution(14454943047217304032)
XLA Ops:
  0.6 1.0 %convert_element_type.151 = f32[2,256,256]{2,1,0:T(8,128)S(1)} convert(bf16[2,256,256]{2,1,0:T(8,128)(2,1)} %param.7) | non-fusion elementwise | flops 131072 | bytes 786432 | tf_op jit(solution)/shard_map/convert_element_type | solution.py:33
  1.7 3.0 %fusion.68 = bf16[2,256,256]{2,1,0:T(8,128)(2,1)S(1)} fusion(f32[2,256,256]{2,1,0:T(8,128)S(1)} %convert_element_type.151, f32[256]{0:T(256)S(1)} %get-tuple-element.21, f32[256]{0:T(256)S(1)} %get-tuple-element.22, f32[256]{0:T(256)S(1)} %get-tuple-element.20, f32[256]{0:T(256)S(1)} %get-tuple-element.7, f32[256]{0:T(256)S(1)} %get-tuple-element.8, ...), kind=kLoop, calls=%fused_computation.102 | loop fusion | flops 4456448 | bytes 803840 | tf_op jit(solution)/shard_map/convert_element_type | solution.py:42
  4.7 0.0 copy-start.3
  4.7 0.0 copy-start.4
  4.7 3.7 %collective-permute-start = (bf16[2,256,256]{2,1,0:T(8,128)(2,1)S(1)}, bf16[2,256,256]{2,1,0:T(8,128)(2,1)S(1)}, u32[]{:S(2)}, u32[]{:S(2)}) collective-permute-start(bf16[2,256,256]{2,1,0:T(8,128)(2,1)S(1)} %fusion.68), channel_id=1, source_target_pairs={{0,1},{1,2},{2,3},{3,4},{4,5},{5,6},{6,7},{7,8},{8,9},{9,10},{10,1... | collective-permute-start | bytes 786440 | tf_op jit(solution)/shard_map/ppermute | solution.py:16
  8.5 1.9 %collective-permute-start.1 = (bf16[2,256,256]{2,1,0:T(8,128)(2,1)S(1)}, bf16[2,256,256]{2,1,0:T(8,128)(2,1)S(1)}, u32[]{:S(2)}, u32[]{:S(2)}) collective-permute-start(bf16[2,256,256]{2,1,0:T(8,128)(2,1)S(1)} %fusion.68), channel_id=1, source_target_pairs={{1,0},{2,1},{3,2},{4,3},{5,4},{6,5},{7,6},{8,7},{9,8},{10,9},{11,1... | collective-permute-start | bytes 786440 | tf_op jit(solution)/shard_map/ppermute | solution.py:16
  10.4 3.1 %collective-permute-start.2 = (bf16[2,256,256]{2,1,0:T(8,128)(2,1)S(1)}, bf16[2,256,256]{2,1,0:T(8,128)(2,1)S(1)}, u32[]{:S(2)}, u32[]{:S(2)}) collective-permute-start(bf16[2,256,256]{2,1,0:T(8,128)(2,1)S(1)} %fusion.68), channel_id=1, source_target_pairs={{0,2},{1,3},{2,4},{3,5},{4,6},{5,7},{6,8},{7,9},{8,10},{9,11},{10,... | collective-permute-start | bytes 786440 | tf_op jit(solution)/shard_map/ppermute | solution.py:16
  13.5 2.2 %collective-permute-start.3 = (bf16[2,256,256]{2,1,0:T(8,128)(2,1)S(1)}, bf16[2,256,256]{2,1,0:T(8,128)(2,1)S(1)}, u32[]{:S(2)}, u32[]{:S(2)}) collective-permute-start(bf16[2,256,256]{2,1,0:T(8,128)(2,1)S(1)} %fusion.68), channel_id=1, source_target_pairs={{2,0},{3,1},{4,2},{5,3},{6,4},{7,5},{8,6},{9,7},{10,8},{11,9},{12,... | collective-permute-start | bytes 786440 | tf_op jit(solution)/shard_map/ppermute | solution.py:16
  15.7 4.7 %collective-permute-start.4 = (bf16[2,256,256]{2,1,0:T(8,128)(2,1)S(1)}, bf16[2,256,256]{2,1,0:T(8,128)(2,1)S(1)}, u32[]{:S(2)}, u32[]{:S(2)}) collective-permute-start(bf16[2,256,256]{2,1,0:T(8,128)(2,1)S(1)} %fusion.68), channel_id=1, source_target_pairs={{0,3},{1,4},{2,5},{3,6},{4,7},{5,8},{6,9},{7,10},{8,11},{9,12},{10... | collective-permute-start | bytes 786440 | tf_op jit(solution)/shard_map/ppermute | solution.py:16
  20.4 0.0 copy-start.2
  20.4 0.6 copy-done.2
  21.1 0.6 copy-done.5
  21.7 0.7 fusion.73
  22.4 0.7 %fusion.72 = f32[128,256]{1,0:T(8,128)S(1)} fusion(bf16[2,256,256]{2,1,0:T(8,128)(2,1)S(1)} %fusion.68, f32[128]{0:T(128)S(1)} %get-tuple-element.24, f32[128]{0:T(128)S(1)} %broadcast_multiply_fusion.1, s32[128]{0:T(128)S(1)} %and_select_fusion, f32[128]{0:T(128)S(1)} %get-tuple-element.23, s32[256]{0:T(256)S(1)} %iota_add_fusion.8, ...), kind=kOutput, calls=%fused_computation.188 | convolution fusion | flops 17203200 | bytes 266240 | tf_op jit(solution)/shard_map/dot_general | solution.py:59
  23.1 0.7 %fusion.34 = bf16[1,128,256]{2,1,0:T(8,128)(2,1)S(1)} fusion(f32[128,256]{1,0:T(8,128)S(1)} %fusion.73, bf16[2,256,256]{2,1,0:T(8,128)(2,1)S(1)} %fusion.68, f32[128]{0:T(128)S(1)} %get-tuple-element.24, f32[128]{0:T(128)S(1)} %broadcast_multiply_fusion.1, s32[128]{0:T(128)S(1)} %and_select_fusion, f32[128]{0:T(128)S(1)} %get-tuple-element.23, ...), kind=kOutput, calls=%fused_computation.68 | convolution fusion | flops 17268736 | bytes 331776 | tf_op jit(solution)/shard_map/dot_general | solution.py:62
  23.8 0.7 %fusion.35 = bf16[1,128,256]{2,1,0:T(8,128)(2,1)S(1)} fusion(f32[128,256]{1,0:T(8,128)S(1)} %fusion.72, bf16[2,256,256]{2,1,0:T(8,128)(2,1)S(1)} %fusion.68, f32[128]{0:T(128)S(1)} %get-tuple-element.24, f32[128]{0:T(128)S(1)} %broadcast_multiply_fusion.1, s32[128]{0:T(128)S(1)} %and_select_fusion, f32[128]{0:T(128)S(1)} %get-tuple-element.23, ...), kind=kOutput, calls=%fused_computation.69 | convolution fusion | flops 17268736 | bytes 331776 | tf_op jit(solution)/shard_map/dot_general | solution.py:59
  24.5 0.0 collective-permute-done
  24.6 1.9 %collective-permute-start.5 = (bf16[2,256,256]{2,1,0:T(8,128)(2,1)S(1)}, bf16[2,256,256]{2,1,0:T(8,128)(2,1)S(1)}, u32[]{:S(2)}, u32[]{:S(2)}) collective-permute-start(bf16[2,256,256]{2,1,0:T(8,128)(2,1)S(1)} %fusion.68), channel_id=1, source_target_pairs={{3,0},{4,1},{5,2},{6,3},{7,4},{8,5},{9,6},{10,7},{11,8},{12,9},{13... | collective-permute-start | bytes 786440 | tf_op jit(solution)/shard_map/ppermute | solution.py:16
  26.5 0.7 %fusion.74 = f32[128,256]{1,0:T(8,128)S(1)} fusion(bf16[2,256,256]{2,1,0:T(8,128)(2,1)S(1)} %collective-permute-done, s32[256]{0:T(256)S(1)} %iota_add_fusion.7, f32[128]{0:T(128)S(1)} %get-tuple-element.24, f32[128]{0:T(128)S(1)} %broadcast_multiply_fusion.1, s32[128]{0:T(128)S(1)} %and_select_fusion, f32[128]{0:T(128)S(1)} %get-tuple-element.23, ...), kind=kOutput, calls=%fused_computation.190 | convolution fusion | flops 17203200 | bytes 266240 | tf_op jit(solution)/shard_map/dot_general | solution.py:62
  27.2 0.7 %fusion.75 = f32[128,256]{1,0:T(8,128)S(1)} fusion(bf16[2,256,256]{2,1,0:T(8,128)(2,1)S(1)} %collective-permute-done, s32[256]{0:T(256)S(1)} %iota_add_fusion.7, f32[128]{0:T(128)S(1)} %get-tuple-element.24, f32[128]{0:T(128)S(1)} %broadcast_multiply_fusion.1, s32[128]{0:T(128)S(1)} %and_select_fusion, f32[128]{0:T(128)S(1)} %get-tuple-element.23, ...), kind=kOutput, calls=%fused_computation.191 | convolution fusion | flops 17203200 | bytes 266240 | tf_op jit(solution)/shard_map/dot_general | solution.py:59
  27.8 0.0 collective-permute-done.1
  27.8 3.5 %collective-permute-start.6 = (bf16[2,256,256]{2,1,0:T(8,128)(2,1)S(1)}, bf16[2,256,256]{2,1,0:T(8,128)(2,1)S(1)}, u32[]{:S(2)}, u32[]{:S(2)}) collective-permute-start(bf16[2,256,256]{2,1,0:T(8,128)(2,1)S(1)} %fusion.68), channel_id=1, source_target_pairs={{0,4},{1,5},{2,6},{3,7},{4,8},{5,9},{6,10},{7,11},{8,12},{9,13},{1... | collective-permute-start | bytes 786440 | tf_op jit(solution)/shard_map/ppermute | solution.py:16
  31.4 0.7 %fusion.76 = f32[128,256]{1,0:T(8,128)S(1)} fusion(bf16[2,256,256]{2,1,0:T(8,128)(2,1)S(1)} %collective-permute-done.1, s32[256]{0:T(256)S(1)} %iota_add_fusion.6, f32[128]{0:T(128)S(1)} %get-tuple-element.24, f32[128]{0:T(128)S(1)} %broadcast_multiply_fusion.1, s32[128]{0:T(128)S(1)} %and_select_fusion, f32[128]{0:T(128)S(1)} %get-tuple-element.23, ...), kind=kOutput, calls=%fused_computation.192 | convolution fusion | flops 17203200 | bytes 266240 | tf_op jit(solution)/shard_map/dot_general | solution.py:62
  32.1 0.7 %fusion.77 = f32[128,256]{1,0:T(8,128)S(1)} fusion(bf16[2,256,256]{2,1,0:T(8,128)(2,1)S(1)} %collective-permute-done.1, s32[256]{0:T(256)S(1)} %iota_add_fusion.6, f32[128]{0:T(128)S(1)} %get-tuple-element.24, f32[128]{0:T(128)S(1)} %broadcast_multiply_fusion.1, s32[128]{0:T(128)S(1)} %and_select_fusion, f32[128]{0:T(128)S(1)} %get-tuple-element.23, ...), kind=kOutput, calls=%fused_computation.193 | convolution fusion | flops 17203200 | bytes 266240 | tf_op jit(solution)/shard_map/dot_general | solution.py:59
  32.7 0.7 %fusion.32 = bf16[1,128,256]{2,1,0:T(8,128)(2,1)S(1)} fusion(f32[128,256]{1,0:T(8,128)S(1)} %fusion.74, bf16[2,256,256]{2,1,0:T(8,128)(2,1)S(1)} %collective-permute-done, s32[256]{0:T(256)S(1)} %iota_add_fusion.7, f32[128]{0:T(128)S(1)} %get-tuple-element.24, f32[128]{0:T(128)S(1)} %broadcast_multiply_fusion.1, s32[128]{0:T(128)S(1)} %and_select_fusion, ...), kind=kOutput, calls=%fused_computation.66 | convolution fusion | flops 17268736 | bytes 331776 | tf_op jit(solution)/shard_map/dot_general | solution.py:62
  33.4 0.7 %fusion.33 = bf16[1,128,256]{2,1,0:T(8,128)(2,1)S(1)} fusion(f32[128,256]{1,0:T(8,128)S(1)} %fusion.75, bf16[2,256,256]{2,1,0:T(8,128)(2,1)S(1)} %collective-permute-done, s32[256]{0:T(256)S(1)} %iota_add_fusion.7, f32[128]{0:T(128)S(1)} %get-tuple-element.24, f32[128]{0:T(128)S(1)} %broadcast_multiply_fusion.1, s32[128]{0:T(128)S(1)} %and_select_fusion, ...), kind=kOutput, calls=%fused_computation.67 | convolution fusion | flops 17268736 | bytes 331776 | tf_op jit(solution)/shard_map/dot_general | solution.py:59
  34.1 0.7 %fusion.30 = bf16[1,128,256]{2,1,0:T(8,128)(2,1)S(1)} fusion(f32[128,256]{1,0:T(8,128)S(1)} %fusion.76, bf16[2,256,256]{2,1,0:T(8,128)(2,1)S(1)} %collective-permute-done.1, s32[256]{0:T(256)S(1)} %iota_add_fusion.6, f32[128]{0:T(128)S(1)} %get-tuple-element.24, f32[128]{0:T(128)S(1)} %broadcast_multiply_fusion.1, s32[128]{0:T(128)S(1)} %and_select_fusion, ...), kind=kOutput, calls=%fused_computation.64 | convolution fusion | flops 17268736 | bytes 331776 | tf_op jit(solution)/shard_map/dot_general | solution.py:62
  34.8 0.7 %fusion.31 = bf16[1,128,256]{2,1,0:T(8,128)(2,1)S(1)} fusion(f32[128,256]{1,0:T(8,128)S(1)} %fusion.77, bf16[2,256,256]{2,1,0:T(8,128)(2,1)S(1)} %collective-permute-done.1, s32[256]{0:T(256)S(1)} %iota_add_fusion.6, f32[128]{0:T(128)S(1)} %get-tuple-element.24, f32[128]{0:T(128)S(1)} %broadcast_multiply_fusion.1, s32[128]{0:T(128)S(1)} %and_select_fusion, ...), kind=kOutput, calls=%fused_computation.65 | convolution fusion | flops 17268736 | bytes 331776 | tf_op jit(solution)/shard_map/dot_general | solution.py:59
  35.4 0.0 collective-permute-done.2
  35.5 1.5 %collective-permute-start.7 = (bf16[2,256,256]{2,1,0:T(8,128)(2,1)S(1)}, bf16[2,256,256]{2,1,0:T(8,128)(2,1)S(1)}, u32[]{:S(2)}, u32[]{:S(2)}) collective-permute-start(bf16[2,256,256]{2,1,0:T(8,128)(2,1)S(1)} %fusion.68), channel_id=1, source_target_pairs={{4,0},{5,1},{6,2},{7,3},{8,4},{9,5},{10,6},{11,7},{12,8},{13,9},{1... | collective-permute-start | bytes 786440 | tf_op jit(solution)/shard_map/ppermute | solution.py:16
  36.9 0.7 %fusion.78 = f32[128,256]{1,0:T(8,128)S(1)} fusion(bf16[2,256,256]{2,1,0:T(8,128)(2,1)S(1)} %collective-permute-done.2, s32[256]{0:T(256)S(1)} %iota_add_fusion.5, f32[128]{0:T(128)S(1)} %get-tuple-element.24, f32[128]{0:T(128)S(1)} %broadcast_multiply_fusion.1, s32[128]{0:T(128)S(1)} %and_select_fusion, f32[128]{0:T(128)S(1)} %get-tuple-element.23, ...), kind=kOutput, calls=%fused_computation.194 | convolution fusion | flops 17203200 | bytes 266240 | tf_op jit(solution)/shard_map/dot_general | solution.py:62
  37.6 0.7 %fusion.79 = f32[128,256]{1,0:T(8,128)S(1)} fusion(bf16[2,256,256]{2,1,0:T(8,128)(2,1)S(1)} %collective-permute-done.2, s32[256]{0:T(256)S(1)} %iota_add_fusion.5, f32[128]{0:T(128)S(1)} %get-tuple-element.24, f32[128]{0:T(128)S(1)} %broadcast_multiply_fusion.1, s32[128]{0:T(128)S(1)} %and_select_fusion, f32[128]{0:T(128)S(1)} %get-tuple-element.23, ...), kind=kOutput, calls=%fused_computation.195 | convolution fusion | flops 17203200 | bytes 266240 | tf_op jit(solution)/shard_map/dot_general | solution.py:59
  38.3 0.0 collective-permute-done.3
  38.3 0.7 %fusion.80 = f32[128,256]{1,0:T(8,128)S(1)} fusion(bf16[2,256,256]{2,1,0:T(8,128)(2,1)S(1)} %collective-permute-done.3, s32[256]{0:T(256)S(1)} %iota_add_fusion.4, f32[128]{0:T(128)S(1)} %get-tuple-element.24, f32[128]{0:T(128)S(1)} %broadcast_multiply_fusion.1, s32[128]{0:T(128)S(1)} %and_select_fusion, f32[128]{0:T(128)S(1)} %get-tuple-element.23, ...), kind=kOutput, calls=%fused_computation.196 | convolution fusion | flops 17203200 | bytes 266240 | tf_op jit(solution)/shard_map/dot_general | solution.py:62
  39.0 0.7 %fusion.81 = f32[128,256]{1,0:T(8,128)S(1)} fusion(bf16[2,256,256]{2,1,0:T(8,128)(2,1)S(1)} %collective-permute-done.3, s32[256]{0:T(256)S(1)} %iota_add_fusion.4, f32[128]{0:T(128)S(1)} %get-tuple-element.24, f32[128]{0:T(128)S(1)} %broadcast_multiply_fusion.1, s32[128]{0:T(128)S(1)} %and_select_fusion, f32[128]{0:T(128)S(1)} %get-tuple-element.23, ...), kind=kOutput, calls=%fused_computation.197 | convolution fusion | flops 17203200 | bytes 266240 | tf_op jit(solution)/shard_map/dot_general | solution.py:59
  39.7 0.0 collective-permute-done.4
  39.7 0.7 %fusion.82 = f32[128,256]{1,0:T(8,128)S(1)} fusion(bf16[2,256,256]{2,1,0:T(8,128)(2,1)S(1)} %collective-permute-done.4, s32[256]{0:T(256)S(1)} %iota_add_fusion.3, f32[128]{0:T(128)S(1)} %get-tuple-element.24, f32[128]{0:T(128)S(1)} %broadcast_multiply_fusion.1, s32[128]{0:T(128)S(1)} %and_select_fusion, f32[128]{0:T(128)S(1)} %get-tuple-element.23, ...), kind=kOutput, calls=%fused_computation.198 | convolution fusion | flops 17203200 | bytes 266240 | tf_op jit(solution)/shard_map/dot_general | solution.py:62
  40.4 0.7 %fusion.83 = f32[128,256]{1,0:T(8,128)S(1)} fusion(bf16[2,256,256]{2,1,0:T(8,128)(2,1)S(1)} %collective-permute-done.4, s32[256]{0:T(256)S(1)} %iota_add_fusion.3, f32[128]{0:T(128)S(1)} %get-tuple-element.24, f32[128]{0:T(128)S(1)} %broadcast_multiply_fusion.1, s32[128]{0:T(128)S(1)} %and_select_fusion, f32[128]{0:T(128)S(1)} %get-tuple-element.23, ...), kind=kOutput, calls=%fused_computation.199 | convolution fusion | flops 17203200 | bytes 266240 | tf_op jit(solution)/shard_map/dot_general | solution.py:59
  41.0 0.7 %fusion.28 = bf16[1,128,256]{2,1,0:T(8,128)(2,1)S(1)} fusion(f32[128,256]{1,0:T(8,128)S(1)} %fusion.78, bf16[2,256,256]{2,1,0:T(8,128)(2,1)S(1)} %collective-permute-done.2, s32[256]{0:T(256)S(1)} %iota_add_fusion.5, f32[128]{0:T(128)S(1)} %get-tuple-element.24, f32[128]{0:T(128)S(1)} %broadcast_multiply_fusion.1, s32[128]{0:T(128)S(1)} %and_select_fusion, ...), kind=kOutput, calls=%fused_computation.62 | convolution fusion | flops 17268736 | bytes 331776 | tf_op jit(solution)/shard_map/dot_general | solution.py:62
  41.7 0.7 %fusion.29 = bf16[1,128,256]{2,1,0:T(8,128)(2,1)S(1)} fusion(f32[128,256]{1,0:T(8,128)S(1)} %fusion.79, bf16[2,256,256]{2,1,0:T(8,128)(2,1)S(1)} %collective-permute-done.2, s32[256]{0:T(256)S(1)} %iota_add_fusion.5, f32[128]{0:T(128)S(1)} %get-tuple-element.24, f32[128]{0:T(128)S(1)} %broadcast_multiply_fusion.1, s32[128]{0:T(128)S(1)} %and_select_fusion, ...), kind=kOutput, calls=%fused_computation.63 | convolution fusion | flops 17268736 | bytes 331776 | tf_op jit(solution)/shard_map/dot_general | solution.py:59
  42.4 0.7 %fusion.26 = bf16[1,128,256]{2,1,0:T(8,128)(2,1)S(1)} fusion(f32[128,256]{1,0:T(8,128)S(1)} %fusion.80, bf16[2,256,256]{2,1,0:T(8,128)(2,1)S(1)} %collective-permute-done.3, s32[256]{0:T(256)S(1)} %iota_add_fusion.4, f32[128]{0:T(128)S(1)} %get-tuple-element.24, f32[128]{0:T(128)S(1)} %broadcast_multiply_fusion.1, s32[128]{0:T(128)S(1)} %and_select_fusion, ...), kind=kOutput, calls=%fused_computation.60 | convolution fusion | flops 17268736 | bytes 331776 | tf_op jit(solution)/shard_map/dot_general | solution.py:62
  43.1 0.7 %fusion.27 = bf16[1,128,256]{2,1,0:T(8,128)(2,1)S(1)} fusion(f32[128,256]{1,0:T(8,128)S(1)} %fusion.81, bf16[2,256,256]{2,1,0:T(8,128)(2,1)S(1)} %collective-permute-done.3, s32[256]{0:T(256)S(1)} %iota_add_fusion.4, f32[128]{0:T(128)S(1)} %get-tuple-element.24, f32[128]{0:T(128)S(1)} %broadcast_multiply_fusion.1, s32[128]{0:T(128)S(1)} %and_select_fusion, ...), kind=kOutput, calls=%fused_computation.61 | convolution fusion | flops 17268736 | bytes 331776 | tf_op jit(solution)/shard_map/dot_general | solution.py:59
  43.8 0.7 %fusion.24 = bf16[1,128,256]{2,1,0:T(8,128)(2,1)S(1)} fusion(f32[128,256]{1,0:T(8,128)S(1)} %fusion.82, bf16[2,256,256]{2,1,0:T(8,128)(2,1)S(1)} %collective-permute-done.4, s32[256]{0:T(256)S(1)} %iota_add_fusion.3, f32[128]{0:T(128)S(1)} %get-tuple-element.24, f32[128]{0:T(128)S(1)} %broadcast_multiply_fusion.1, s32[128]{0:T(128)S(1)} %and_select_fusion, ...), kind=kOutput, calls=%fused_computation.58 | convolution fusion | flops 17268736 | bytes 331776 | tf_op jit(solution)/shard_map/dot_general | solution.py:62
  44.5 0.7 %fusion.25 = bf16[1,128,256]{2,1,0:T(8,128)(2,1)S(1)} fusion(f32[128,256]{1,0:T(8,128)S(1)} %fusion.83, bf16[2,256,256]{2,1,0:T(8,128)(2,1)S(1)} %collective-permute-done.4, s32[256]{0:T(256)S(1)} %iota_add_fusion.3, f32[128]{0:T(128)S(1)} %get-tuple-element.24, f32[128]{0:T(128)S(1)} %broadcast_multiply_fusion.1, s32[128]{0:T(128)S(1)} %and_select_fusion, ...), kind=kOutput, calls=%fused_computation.59 | convolution fusion | flops 17268736 | bytes 331776 | tf_op jit(solution)/shard_map/dot_general | solution.py:59
  45.2 0.0 collective-permute-done.5
  45.2 0.7 %fusion.84 = f32[128,256]{1,0:T(8,128)S(1)} fusion(bf16[2,256,256]{2,1,0:T(8,128)(2,1)S(1)} %collective-permute-done.5, s32[256]{0:T(256)S(1)} %iota_add_fusion.2, f32[128]{0:T(128)S(1)} %get-tuple-element.24, f32[128]{0:T(128)S(1)} %broadcast_multiply_fusion.1, s32[128]{0:T(128)S(1)} %and_select_fusion, f32[128]{0:T(128)S(1)} %get-tuple-element.23, ...), kind=kOutput, calls=%fused_computation.200 | convolution fusion | flops 17203200 | bytes 266240 | tf_op jit(solution)/shard_map/dot_general | solution.py:62
  45.9 0.7 %fusion.85 = f32[128,256]{1,0:T(8,128)S(1)} fusion(bf16[2,256,256]{2,1,0:T(8,128)(2,1)S(1)} %collective-permute-done.5, s32[256]{0:T(256)S(1)} %iota_add_fusion.2, f32[128]{0:T(128)S(1)} %get-tuple-element.24, f32[128]{0:T(128)S(1)} %broadcast_multiply_fusion.1, s32[128]{0:T(128)S(1)} %and_select_fusion, f32[128]{0:T(128)S(1)} %get-tuple-element.23, ...), kind=kOutput, calls=%fused_computation.201 | convolution fusion | flops 17203200 | bytes 266240 | tf_op jit(solution)/shard_map/dot_general | solution.py:59
  46.5 0.7 %fusion.87 = f32[128,256]{1,0:T(8,128)S(1)} fusion(bf16[2,256,256]{2,1,0:T(8,128)(2,1)S(1)} %collective-permute-done.6, s32[256]{0:T(256)S(1)} %iota_add_fusion.1, f32[128]{0:T(128)S(1)} %get-tuple-element.24, f32[128]{0:T(128)S(1)} %broadcast_multiply_fusion.1, s32[128]{0:T(128)S(1)} %and_select_fusion, f32[128]{0:T(128)S(1)} %get-tuple-element.23, ...), kind=kOutput, calls=%fused_computation.203 | convolution fusion | flops 17203200 | bytes 266240 | tf_op jit(solution)/shard_map/dot_general | solution.py:59
  47.2 0.7 %fusion.86 = f32[128,256]{1,0:T(8,128)S(1)} fusion(bf16[2,256,256]{2,1,0:T(8,128)(2,1)S(1)} %collective-permute-done.6, s32[256]{0:T(256)S(1)} %iota_add_fusion.1, f32[128]{0:T(128)S(1)} %get-tuple-element.24, f32[128]{0:T(128)S(1)} %broadcast_multiply_fusion.1, s32[128]{0:T(128)S(1)} %and_select_fusion, f32[128]{0:T(128)S(1)} %get-tuple-element.23, ...), kind=kOutput, calls=%fused_computation.202 | convolution fusion | flops 17203200 | bytes 266240 | tf_op jit(solution)/shard_map/dot_general | solution.py:62
  47.9 0.7 %fusion.22 = bf16[1,128,256]{2,1,0:T(8,128)(2,1)S(1)} fusion(f32[128,256]{1,0:T(8,128)S(1)} %fusion.84, bf16[2,256,256]{2,1,0:T(8,128)(2,1)S(1)} %collective-permute-done.5, s32[256]{0:T(256)S(1)} %iota_add_fusion.2, f32[128]{0:T(128)S(1)} %get-tuple-element.24, f32[128]{0:T(128)S(1)} %broadcast_multiply_fusion.1, s32[128]{0:T(128)S(1)} %and_select_fusion, ...), kind=kOutput, calls=%fused_computation.56 | convolution fusion | flops 17268736 | bytes 331776 | tf_op jit(solution)/shard_map/dot_general | solution.py:62
  48.6 0.7 %fusion.23 = bf16[1,128,256]{2,1,0:T(8,128)(2,1)S(1)} fusion(f32[128,256]{1,0:T(8,128)S(1)} %fusion.85, bf16[2,256,256]{2,1,0:T(8,128)(2,1)S(1)} %collective-permute-done.5, s32[256]{0:T(256)S(1)} %iota_add_fusion.2, f32[128]{0:T(128)S(1)} %get-tuple-element.24, f32[128]{0:T(128)S(1)} %broadcast_multiply_fusion.1, s32[128]{0:T(128)S(1)} %and_select_fusion, ...), kind=kOutput, calls=%fused_computation.57 | convolution fusion | flops 17268736 | bytes 331776 | tf_op jit(solution)/shard_map/dot_general | solution.py:59
  49.3 0.7 %fusion.21 = bf16[1,128,256]{2,1,0:T(8,128)(2,1)S(1)} fusion(f32[128,256]{1,0:T(8,128)S(1)} %fusion.87, bf16[2,256,256]{2,1,0:T(8,128)(2,1)S(1)} %collective-permute-done.6, s32[256]{0:T(256)S(1)} %iota_add_fusion.1, f32[128]{0:T(128)S(1)} %get-tuple-element.24, f32[128]{0:T(128)S(1)} %broadcast_multiply_fusion.1, s32[128]{0:T(128)S(1)} %and_select_fusion, ...), kind=kOutput, calls=%fused_computation.55 | convolution fusion | flops 17268736 | bytes 331776 | tf_op jit(solution)/shard_map/dot_general | solution.py:59
  50.0 0.7 %fusion.20 = bf16[1,128,256]{2,1,0:T(8,128)(2,1)S(1)} fusion(f32[128,256]{1,0:T(8,128)S(1)} %fusion.86, bf16[2,256,256]{2,1,0:T(8,128)(2,1)S(1)} %collective-permute-done.6, s32[256]{0:T(256)S(1)} %iota_add_fusion.1, f32[128]{0:T(128)S(1)} %get-tuple-element.24, f32[128]{0:T(128)S(1)} %broadcast_multiply_fusion.1, s32[128]{0:T(128)S(1)} %and_select_fusion, ...), kind=kOutput, calls=%fused_computation.54 | convolution fusion | flops 17268736 | bytes 331776 | tf_op jit(solution)/shard_map/dot_general | solution.py:62
  50.6 0.0 collective-permute-done.7
  50.7 0.7 %fusion.89 = f32[128,256]{1,0:T(8,128)S(1)} fusion(bf16[2,256,256]{2,1,0:T(8,128)(2,1)S(1)} %collective-permute-done.7, s32[256]{0:T(256)S(1)} %iota_add_fusion, f32[128]{0:T(128)S(1)} %get-tuple-element.24, f32[128]{0:T(128)S(1)} %broadcast_multiply_fusion.1, s32[128]{0:T(128)S(1)} %and_select_fusion, f32[128]{0:T(128)S(1)} %get-tuple-element.23, ...), kind=kOutput, calls=%fused_computation.205 | convolution fusion | flops 17203200 | bytes 266240 | tf_op jit(solution)/shard_map/dot_general | solution.py:59
  51.3 0.7 %fusion.88 = f32[128,256]{1,0:T(8,128)S(1)} fusion(bf16[2,256,256]{2,1,0:T(8,128)(2,1)S(1)} %collective-permute-done.7, s32[256]{0:T(256)S(1)} %iota_add_fusion, f32[128]{0:T(128)S(1)} %get-tuple-element.24, f32[128]{0:T(128)S(1)} %broadcast_multiply_fusion.1, s32[128]{0:T(128)S(1)} %and_select_fusion, f32[128]{0:T(128)S(1)} %get-tuple-element.23, ...), kind=kOutput, calls=%fused_computation.204 | convolution fusion | flops 17203200 | bytes 266240 | tf_op jit(solution)/shard_map/dot_general | solution.py:62
  52.0 0.7 %fusion.19 = bf16[1,128,256]{2,1,0:T(8,128)(2,1)S(1)} fusion(f32[128,256]{1,0:T(8,128)S(1)} %fusion.89, bf16[2,256,256]{2,1,0:T(8,128)(2,1)S(1)} %collective-permute-done.7, s32[256]{0:T(256)S(1)} %iota_add_fusion, f32[128]{0:T(128)S(1)} %get-tuple-element.24, f32[128]{0:T(128)S(1)} %broadcast_multiply_fusion.1, s32[128]{0:T(128)S(1)} %and_select_fusion, ...), kind=kOutput, calls=%fused_computation.53 | convolution fusion | flops 17268736 | bytes 331776 | tf_op jit(solution)/shard_map/dot_general | solution.py:59
  52.7 0.7 %fusion.18 = bf16[1,128,256]{2,1,0:T(8,128)(2,1)S(1)} fusion(f32[128,256]{1,0:T(8,128)S(1)} %fusion.88, bf16[2,256,256]{2,1,0:T(8,128)(2,1)S(1)} %collective-permute-done.7, s32[256]{0:T(256)S(1)} %iota_add_fusion, f32[128]{0:T(128)S(1)} %get-tuple-element.24, f32[128]{0:T(128)S(1)} %broadcast_multiply_fusion.1, s32[128]{0:T(128)S(1)} %and_select_fusion, ...), kind=kOutput, calls=%fused_computation.52 | convolution fusion | flops 17268736 | bytes 331776 | tf_op jit(solution)/shard_map/dot_general | solution.py:62
  53.4 0.8 %fusion.179 = (bf16[2,128,256]{2,1,0:T(8,128)(2,1)}, f32[2,128,256]{2,1,0:T(8,128)S(1)}) fusion(bf16[2,128,256]{2,1,0:T(8,128)(2,1)S(1)} %pad_maximum_fusion.8, bf16[2,128,256]{2,1,0:T(8,128)(2,1)S(1)} %pad_maximum_fusion.7, bf16[2,128,256]{2,1,0:T(8,128)(2,1)S(1)} %pad_maximum_fusion.6, bf16[2,128,256]{2,1,0:T(8,128)(2,1)S(1)} %pad_maximum_fusion.5, ...), kind=kLoop, calls=%fused_computation.350 | loop fusion | flops 1179648 | bytes 1572864 | tf_op jit(solution)/shard_map/convert_element_type | solution.py:105
  54.2 6.0 %collective-permute-start.8 = (bf16[8,256]{1,0:T(8,128)(2,1)S(1)}, bf16[8,256]{1,0:T(8,128)(2,1)S(1)}, u32[]{:S(2)}, u32[]{:S(2)}) collective-permute-start(bf16[8,256]{1,0:T(8,128)(2,1)S(1)} %get-tuple-element.4), channel_id=1, source_target_pairs={{0,1},{1,2},{2,3},{3,4},{4,5},{5,6},{6,7},{7,8},{8,9},{9,10},{10,1... | collective-permute-start | bytes 12296 | tf_op jit(solution)/shard_map/ppermute | solution.py:26
  60.3 1.9 %collective-permute-start.9 = (bf16[8,256]{1,0:T(8,128)(2,1)S(1)}, bf16[8,256]{1,0:T(8,128)(2,1)S(1)}, u32[]{:S(2)}, u32[]{:S(2)}) collective-permute-start(bf16[8,256]{1,0:T(8,128)(2,1)S(1)} %get-tuple-element.5), channel_id=1, source_target_pairs={{1,0},{2,1},{3,2},{4,3},{5,4},{6,5},{7,6},{8,7},{9,8},{10,9},{11,1... | collective-permute-start | bytes 12296 | tf_op jit(solution)/shard_map/ppermute | solution.py:27
  62.2 0.0 collective-permute-done.8
  62.2 3.9 %collective-permute-done.9 = bf16[8,256]{1,0:T(8,128)(2,1)S(1)} collective-permute-done((bf16[8,256]{1,0:T(8,128)(2,1)S(1)}, bf16[8,256]{1,0:T(8,128)(2,1)S(1)}, u32[]{:S(2)}, u32[]{:S(2)}) %collective-permute-start.9) | collective-permute-done | bytes 4128 | tf_op jit(solution)/shard_map/ppermute | solution.py:27
  66.1 0.8 %fusion.69 = f32[128,256]{1,0:T(8,128)} fusion(f32[144,256]{1,0:T(8,128)S(1)} %maximum_convert_fusion), kind=kLoop, calls=%fused_computation.105 | loop fusion | flops 557056 | bytes 2359296 | tf_op jit(solution)/shard_map/div | solution.py:104
  (34 shorter events, 0.3 us)
Async XLA Ops:
  0.6 1.0 %copy-start.1 = (f32[256]{0:T(256)S(1)}, f32[256]{0:T(256)}, u32[]{:S(2)}) copy-start(f32[256]{0:T(256)} %param.8) | copy-start | bytes 3076
  0.6 1.0 %copy-start = (s32[256]{0:T(256)S(1)}, s32[256]{0:T(256)}, u32[]{:S(2)}) copy-start(s32[256]{0:T(256)} %param.9) | copy-start | bytes 3076
  4.7 15.7 %copy-start.3 = (s32[128]{0:T(128)S(1)}, s32[128]{0:T(128)}, u32[]{:S(2)}) copy-start(s32[128]{0:T(128)} %param.11) | copy-start | bytes 1540
  4.7 15.7 %copy-start.4 = (s32[128]{0:T(128)S(1)}, s32[128]{0:T(128)}, u32[]{:S(2)}) copy-start(s32[128]{0:T(128)} %param.10) | copy-start | bytes 1540
  4.7 19.8 %collective-permute-start = (bf16[2,256,256]{2,1,0:T(8,128)(2,1)S(1)}, bf16[2,256,256]{2,1,0:T(8,128)(2,1)S(1)}, u32[]{:S(2)}, u32[]{:S(2)}) collective-permute-start(bf16[2,256,256]{2,1,0:T(8,128)(2,1)S(1)} %fusion.68), channel_id=1, source_target_pairs={{0,1},{1,2},{2,3},{3,4},{4,5},{5,6},{6,7},{7,8},{8,9},{9,10},{10,1... | collective-permute-start | bytes 786440 | tf_op jit(solution)/shard_map/ppermute | solution.py:16
  8.5 19.4 %collective-permute-start.1 = (bf16[2,256,256]{2,1,0:T(8,128)(2,1)S(1)}, bf16[2,256,256]{2,1,0:T(8,128)(2,1)S(1)}, u32[]{:S(2)}, u32[]{:S(2)}) collective-permute-start(bf16[2,256,256]{2,1,0:T(8,128)(2,1)S(1)} %fusion.68), channel_id=1, source_target_pairs={{1,0},{2,1},{3,2},{4,3},{5,4},{6,5},{7,6},{8,7},{9,8},{10,9},{11,1... | collective-permute-start | bytes 786440 | tf_op jit(solution)/shard_map/ppermute | solution.py:16
  10.4 25.0 %collective-permute-start.2 = (bf16[2,256,256]{2,1,0:T(8,128)(2,1)S(1)}, bf16[2,256,256]{2,1,0:T(8,128)(2,1)S(1)}, u32[]{:S(2)}, u32[]{:S(2)}) collective-permute-start(bf16[2,256,256]{2,1,0:T(8,128)(2,1)S(1)} %fusion.68), channel_id=1, source_target_pairs={{0,2},{1,3},{2,4},{3,5},{4,6},{5,7},{6,8},{7,9},{8,10},{9,11},{10,... | collective-permute-start | bytes 786440 | tf_op jit(solution)/shard_map/ppermute | solution.py:16
  13.5 24.8 %collective-permute-start.3 = (bf16[2,256,256]{2,1,0:T(8,128)(2,1)S(1)}, bf16[2,256,256]{2,1,0:T(8,128)(2,1)S(1)}, u32[]{:S(2)}, u32[]{:S(2)}) collective-permute-start(bf16[2,256,256]{2,1,0:T(8,128)(2,1)S(1)} %fusion.68), channel_id=1, source_target_pairs={{2,0},{3,1},{4,2},{5,3},{6,4},{7,5},{8,6},{9,7},{10,8},{11,9},{12,... | collective-permute-start | bytes 786440 | tf_op jit(solution)/shard_map/ppermute | solution.py:16
  15.7 24.0 %collective-permute-start.4 = (bf16[2,256,256]{2,1,0:T(8,128)(2,1)S(1)}, bf16[2,256,256]{2,1,0:T(8,128)(2,1)S(1)}, u32[]{:S(2)}, u32[]{:S(2)}) collective-permute-start(bf16[2,256,256]{2,1,0:T(8,128)(2,1)S(1)} %fusion.68), channel_id=1, source_target_pairs={{0,3},{1,4},{2,5},{3,6},{4,7},{5,8},{6,9},{7,10},{8,11},{9,12},{10... | collective-permute-start | bytes 786440 | tf_op jit(solution)/shard_map/ppermute | solution.py:16
  20.4 0.7 copy-start.2
  21.1 0.7 copy-start.5
  24.6 20.6 %collective-permute-start.5 = (bf16[2,256,256]{2,1,0:T(8,128)(2,1)S(1)}, bf16[2,256,256]{2,1,0:T(8,128)(2,1)S(1)}, u32[]{:S(2)}, u32[]{:S(2)}) collective-permute-start(bf16[2,256,256]{2,1,0:T(8,128)(2,1)S(1)} %fusion.68), channel_id=1, source_target_pairs={{3,0},{4,1},{5,2},{6,3},{7,4},{8,5},{9,6},{10,7},{11,8},{12,9},{13... | collective-permute-start | bytes 786440 | tf_op jit(solution)/shard_map/ppermute | solution.py:16
  27.8 18.7 %collective-permute-start.6 = (bf16[2,256,256]{2,1,0:T(8,128)(2,1)S(1)}, bf16[2,256,256]{2,1,0:T(8,128)(2,1)S(1)}, u32[]{:S(2)}, u32[]{:S(2)}) collective-permute-start(bf16[2,256,256]{2,1,0:T(8,128)(2,1)S(1)} %fusion.68), channel_id=1, source_target_pairs={{0,4},{1,5},{2,6},{3,7},{4,8},{5,9},{6,10},{7,11},{8,12},{9,13},{1... | collective-permute-start | bytes 786440 | tf_op jit(solution)/shard_map/ppermute | solution.py:16
  35.5 15.2 %collective-permute-start.7 = (bf16[2,256,256]{2,1,0:T(8,128)(2,1)S(1)}, bf16[2,256,256]{2,1,0:T(8,128)(2,1)S(1)}, u32[]{:S(2)}, u32[]{:S(2)}) collective-permute-start(bf16[2,256,256]{2,1,0:T(8,128)(2,1)S(1)} %fusion.68), channel_id=1, source_target_pairs={{4,0},{5,1},{6,2},{7,3},{8,4},{9,5},{10,6},{11,7},{12,8},{13,9},{1... | collective-permute-start | bytes 786440 | tf_op jit(solution)/shard_map/ppermute | solution.py:16
  54.2 8.0 %collective-permute-start.8 = (bf16[8,256]{1,0:T(8,128)(2,1)S(1)}, bf16[8,256]{1,0:T(8,128)(2,1)S(1)}, u32[]{:S(2)}, u32[]{:S(2)}) collective-permute-start(bf16[8,256]{1,0:T(8,128)(2,1)S(1)} %get-tuple-element.4), channel_id=1, source_target_pairs={{0,1},{1,2},{2,3},{3,4},{4,5},{5,6},{6,7},{7,8},{8,9},{9,10},{10,1... | collective-permute-start | bytes 12296 | tf_op jit(solution)/shard_map/ppermute | solution.py:26
  60.3 5.8 %collective-permute-start.9 = (bf16[8,256]{1,0:T(8,128)(2,1)S(1)}, bf16[8,256]{1,0:T(8,128)(2,1)S(1)}, u32[]{:S(2)}, u32[]{:S(2)}) collective-permute-start(bf16[8,256]{1,0:T(8,128)(2,1)S(1)} %get-tuple-element.5), channel_id=1, source_target_pairs={{1,0},{2,1},{3,2},{4,3},{5,4},{6,5},{7,6},{8,7},{9,8},{10,9},{11,1... | collective-permute-start | bytes 12296 | tf_op jit(solution)/shard_map/ppermute | solution.py:27
where the time goes:
time: 67.3 us; the launch traced here: 66.9 us
  starting transfers between devices  30.5 us (45%)
  matrix products  24.4 us (36%)
  other arithmetic  5.89 us (9%)
  waiting for transfers between devices  3.88 us (6%)
  local copies, waits for them, and re-layouts  1.31 us (2%)
  between operations  1.01 us (2%)
    ppermute x8, starting transfers between devices, from_behind(): return lax.ppermute(array, axis, pairs)  22.5 us
    dot_general x9, matrix products, focus_block(): jnp.dot(weight_im, block_data[0], preferred_element_type=jnp.float32)  6.11 us
    dot_general x9, matrix products, focus_block(): jnp.dot(weight_im, block_data[1], preferred_element_type=jnp.float32)  6.1 us
    dot_general x9, matrix products, focus_block(): jnp.dot(weight_re, block_data[0], preferred_element_type=jnp.float32)  6.08 us
    dot_general x9, matrix products, focus_block(): jnp.dot(weight_re, block_data[1], preferred_element_type=jnp.float32)  6.07 us
    ppermute x1, starting transfers between devices, padded(): before = lax.ppermute(last, axis, up)  6.01 us
    ppermute x1, waiting for transfers between devices, padded(): after = lax.ppermute(initial, axis, down)  3.86 us
    convert_element_type x1, other arithmetic, migrate(): return result.astype(jnp.bfloat16)  3.01 us
  transfers between devices with their start and end apart: 10, of which 1 were waited for; matrix products, arithmetic and copies ran while one was open for 33% of the time, Pallas kernels for 0%

commit v1 on v0

v1 whole, which is shorter than its diff:
```python
import functools

import jax
import jax.numpy as jnp
from jax import lax
from jax.experimental import pallas as pl
from jax.experimental.pallas import tpu as pltpu
from jax.sharding import PartitionSpec as P

REACH = 4
LOOK = 8
SHIFT_MAX = 16
F32 = jnp.float32
BF16 = jnp.bfloat16

SIN = (1.0, -0.16666658222675323, 0.008333050645887852, -0.0001980901142815128, 2.605078407214023e-06)
COS = (1.0, -0.5, 0.04166663438081741, -0.0013888359535485506, 2.476008012308739e-05, -2.605002862310357e-07)
PI_HI = 3.140625
PI_LO = 0.0009676536
INV_PI = 0.3183098861837907


PARAMS = pltpu.CompilerParams(vmem_limit_bytes=16 * 2**20)


def neighbour(i, by, odd, devices):
    up = (i // by) % 2 == (1 if odd else 0)
    j = i + by if up else i - by
    return j if 0 <= j < devices else i ^ 1


def swap(array, by, odd):
    devices = lax.axis_size("seg")
    return lax.ppermute(array, "seg", [(i, neighbour(i, by, odd, devices)) for i in range(devices)])


def ring(array):
    devices = lax.axis_size("seg")
    pairs = []
    for i in range(devices):
        j = i + 2 if i % 2 == 0 else i - 2
        pairs.append((i, j if 0 <= j < devices else i ^ 1))
    return lax.ppermute(array, "seg", pairs)


def column(row):
    return jnp.transpose(jnp.broadcast_to(row, (8, row.shape[1])))[:, :1]


def migrate_kernel(pulses_ref, fraction_ref, shift_ref, start_ref, end_ref, doppler_ref, chirp_ref, out_ref, params_ref):
    gates = pulses_ref.shape[2]
    count = pulses_ref.shape[1]
    shape = (count, gates)
    fraction = jnp.broadcast_to(column(fraction_ref[...]), shape)
    shift = jnp.broadcast_to(column(shift_ref[...].astype(F32)), shape).astype(jnp.int32)
    reach = lax.broadcasted_iota(jnp.int32, shape, 1) + shift
    first = jnp.where(reach < gates, 1.0 - fraction, 0.0)
    second = jnp.where(reach + 1 < gates, fraction, 0.0)
    for part in range(2):
        moved = pulses_ref[part].astype(F32)
        bit = 1
        while bit < SHIFT_MAX:
            moved = jnp.where((shift & bit) != 0, pltpu.roll(moved, gates - bit, 1), moved)
            bit *= 2
        out_ref[part] = (first * moved + second * pltpu.roll(moved, gates - 1, 1)).astype(BF16)
    params_ref[0:1, :] = start_ref[...].astype(F32)
    params_ref[1:2, :] = end_ref[...].astype(F32)
    params_ref[2:3, :] = doppler_ref[...]
    params_ref[3:4, :] = chirp_ref[...]
    params_ref[4:8, :] = jnp.zeros((4, params_ref.shape[1]), F32)


def poly(coefs, z):
    total = coefs[-1] * z + coefs[-2]
    for c in coefs[-3::-1]:
        total = total * z + c
    return total


def spread(params_ref, other_ref, cols):
    waves = params_ref.shape[1]
    for half, ref in enumerate((params_ref, other_ref)):
        start, end = ref[0:1, :], ref[1:2, :]
        center = jnp.floor((start + end) * 0.5)
        scale = lax.rsqrt(end - start)
        stack = jnp.concatenate([center, start, end, ref[2:3, :], ref[3:4, :], scale, scale, scale], 0)
        turned = jnp.transpose(stack)
        for k in range(6):
            cols[k, half * waves : (half + 1) * waves, :] = jnp.broadcast_to(turned[:, k : k + 1], (waves, 128))


def weigh(cols, base, pulse_count, rows, put):
    total_rows = cols.shape[1]

    def step(k, carry):
        r = pl.multiple_of(k * rows, rows)
        center, start, end, doppler, chirp, scale = (cols[j, pl.ds(r, rows), :] for j in range(6))
        for lane in range(0, pulse_count, 128):
            pulse = (lax.broadcasted_iota(jnp.int32, (rows, 128), 1) + (base + lane)).astype(F32)
            relative = (pulse - center) * (1.0 / (REACH * pulse_count))
            phase = chirp * relative * relative + doppler * relative
            turns = jnp.round(phase * INV_PI)
            rest = (phase - turns * PI_HI) - turns * PI_LO
            square = rest * rest
            signed = jnp.where((turns.astype(jnp.int32) & 1) != 0, -scale, scale)
            signed = jnp.where((pulse >= start) & (pulse < end), signed, 0.0)
            put(r, lane, signed * poly(COS, square), signed * rest * poly(SIN, square))
        return carry

    lax.fori_loop(0, total_rows // rows, step, 0, unroll=2)


def owner_of(slot, device):
    by, odd = ((2, 0), (2, 1), (4, 0), (4, 1))[slot]
    return jnp.where((device // by) % 2 == odd, device + by, device - by)


def weights_kernel(params_ref, other_ref, own_ref, partial_ref, weights_ref, cols, own_w):
    device = lax.axis_index("seg")
    count = own_ref.shape[1]
    spread(params_ref, other_ref, cols)

    def put_own(r, lane, re, im):
        own_w[0, pl.ds(r, 16), lane : lane + 128] = re.astype(BF16)
        own_w[1, pl.ds(r, 16), lane : lane + 128] = im.astype(BF16)

    weigh(cols, device * count, count, 16, put_own)
    dot = functools.partial(jnp.dot, preferred_element_type=F32)
    partial_ref[0] = dot(own_w[0], own_ref[0]) - dot(own_w[1], own_ref[1])
    partial_ref[1] = dot(own_w[0], own_ref[1]) + dot(own_w[1], own_ref[0])
    for slot in range(4):

        def put(r, lane, re, im, slot=slot):
            weights_ref[0, pl.ds(r, 16), slot * count + lane : slot * count + lane + 128] = re.astype(BF16)
            weights_ref[1, pl.ds(r, 16), slot * count + lane : slot * count + lane + 128] = im.astype(BF16)

        weigh(cols, owner_of(slot, device) * count, count, 16, put)


def focus_kernel(partial_ref, weights_ref, b0, b1, b2, b3, keep_ref, message_ref):
    count = b0.shape[1]
    waves = partial_ref.shape[1] // 2
    dot = functools.partial(jnp.dot, preferred_element_type=F32)
    re, im = partial_ref[0], partial_ref[1]
    minus = jnp.zeros_like(re)
    for slot, ref in enumerate((b0, b1, b2, b3)):
        w_re = weights_ref[0, :, slot * count : (slot + 1) * count]
        w_im = weights_ref[1, :, slot * count : (slot + 1) * count]
        re += dot(w_re, ref[0])
        minus += dot(w_im, ref[1])
        im += dot(w_re, ref[1])
        im += dot(w_im, ref[0])
    re = re - minus
    for part, value in enumerate((re, im)):
        keep_ref[part, :waves] = value[:waves]
        keep_ref[part, waves : waves + LOOK] = value[waves : waves + LOOK]
        keep_ref[part, waves + LOOK :] = value[2 * waves - LOOK :]
        message_ref[part, :waves] = value[waves:].astype(BF16)
        edges = jnp.concatenate([value[:LOOK], value[waves - LOOK : waves]], 0)
        message_ref[part, waves:] = edges.astype(BF16)


def power_kernel(keep_ref, got_ref, focused_ref, looked_ref, edge_ref, ext):
    waves = focused_ref.shape[1]
    core = lax.axis_index("seg") % 2
    total = keep_ref[...] + got_ref[...].astype(F32)
    focused_ref[...] = total[:, :waves].astype(BF16)
    power = total[0] * total[0] + total[1] * total[1]
    initial, last = power[waves : waves + LOOK], power[waves + LOOK :]
    edge_ref[...] = jnp.where(core == 0, last, initial)
    ext[:LOOK] = jnp.where(core == 1, last, 0.0)
    ext[LOOK : LOOK + waves] = power[:waves]
    ext[LOOK + waves :] = jnp.where(core == 0, initial, 0.0)
    rows = waves + 2 * LOOK
    span, window = 1, ext[...]
    while span < 2 * LOOK:
        rows -= span
        window = window[:rows] + window[span : span + rows]
        span *= 2
    looked = window[:waves] + ext[2 * LOOK :]
    looked_ref[...] = looked * (1.0 / (2 * LOOK + 1))


def edge_kernel(devices, looked_ref, edge_ref, out_ref):
    step = pl.program_id(0)
    device = lax.axis_index("seg")
    core = device % 2
    from_chip = device + 4 * core - 2
    here = (step == core) & (from_chip >= 0) & (from_chip < devices)
    scale = jnp.where(here, 1.0 / (2 * LOOK + 1), 0.0)
    row = lax.broadcasted_iota(jnp.int32, edge_ref.shape, 0)
    total = jnp.zeros(edge_ref.shape, F32)
    for h in range(LOOK):
        total += jnp.where((row - h) * (2 * core - 1) >= 0, edge_ref[h : h + 1, :], 0.0)
    out_ref[...] = looked_ref[...] + total * scale


def shards(pulses, fraction, gate_shift, aperture_start, aperture_end, doppler, chirp_rate):
    _, count, gates = pulses.shape
    waves = aperture_start.shape[0]
    devices = lax.axis_size("seg")
    shape = jax.ShapeDtypeStruct
    vmem = pl.BlockSpec(memory_space=pltpu.VMEM)

    migrated, params = pl.pallas_call(
        migrate_kernel,
        out_shape=(shape((2, count, gates), BF16), shape((8, waves), F32)),
        in_specs=[vmem] * 7,
        out_specs=(vmem, vmem),
        compiler_params=PARAMS,
        name="migrate",
    )(
        pulses,
        fraction.reshape(1, count),
        gate_shift.reshape(1, count),
        aperture_start.reshape(1, waves),
        aperture_end.reshape(1, waves),
        doppler.reshape(1, waves),
        chirp_rate.reshape(1, waves),
    )
    blocks = [swap(migrated, by, odd) for by, odd in ((2, 0), (2, 1), (4, 0), (4, 1))]
    other = swap(params, 1, 0)
    partial, weights = pl.pallas_call(
        weights_kernel,
        out_shape=(shape((2, 2 * waves, gates), F32), shape((2, 2 * waves, 4 * count), BF16)),
        in_specs=[vmem] * 3,
        out_specs=(vmem, vmem),
        scratch_shapes=[pltpu.VMEM((6, 2 * waves, 128), F32), pltpu.VMEM((2, 2 * waves, count), BF16)],
        compiler_params=PARAMS,
        name="weights",
    )(params, other, migrated)
    rows = waves + 2 * LOOK
    keep, message = pl.pallas_call(
        focus_kernel,
        out_shape=(shape((2, rows, gates), F32), shape((2, rows, gates), BF16)),
        in_specs=[vmem] * 6,
        out_specs=(vmem, vmem),
        compiler_params=PARAMS,
        name="focus",
    )(partial, weights, *blocks)
    got = swap(message, 1, 0)
    focused, looked, edge = pl.pallas_call(
        power_kernel,
        out_shape=(shape((2, waves, gates), BF16), shape((waves, gates), F32), shape((LOOK, gates), F32)),
        in_specs=[vmem] * 2,
        out_specs=(vmem, vmem, vmem),
        scratch_shapes=[pltpu.VMEM((rows, gates), F32)],
        compiler_params=PARAMS,
        name="power",
    )(keep, got)
    far = ring(edge)
    block = pl.BlockSpec((LOOK, gates), lambda g: (g * (waves // LOOK - 1), 0))
    multilook = pl.pallas_call(
        functools.partial(edge_kernel, devices),
        grid=(2,),
        out_shape=shape((waves, gates), F32),
        in_specs=[block, pl.BlockSpec((LOOK, gates), lambda g: (0, 0))],
        out_specs=block,
        input_output_aliases={0: 0},
        compiler_params=PARAMS,
        name="edge",
    )(looked, far)
    return (focused, multilook)


def solution(mesh):
    part = P(("arcs", "seg"))
    return jax.shard_map(
        shards,
        mesh=mesh,
        in_specs=(P(None, ("arcs", "seg"), None),) + (part,) * 6,
        out_specs=(P(None, ("arcs", "seg"), None), P(("arcs", "seg"), None)),
        check_vma=False,
    )
```

time: 67.3 us -> 29.9 us (0.44)
  the two profiles are of different devices: /device:TPU:3 before, /device:TPU:8 now
where the time goes in v1:
time: 29.9 us; the launch traced here: 29.7 us
  waiting for transfers between devices  14.5 us (48%)
  Pallas kernels  6.93 us (23%)
  starting transfers between devices  5.87 us (20%)
  local copies, waits for them, and re-layouts  1.65 us (6%)
  between operations  0.72 us (2%)
    ppermute x6, waiting for transfers between devices, swap(): lax.ppermute(array, 'seg', [(i, neighbour(i, by, odd, devices)) for i in...  11 us
    ppermute x6, starting transfers between devices, swap(): lax.ppermute(array, 'seg', [(i, neighbour(i, by, odd, devices)) for i in...  4.83 us
    ppermute x1, waiting for transfers between devices, ring(): return lax.ppermute(array, 'seg', pairs)  3.51 us
    pallas_call x1, Pallas kernels, shards(): pl.pallas_call(weights_kernel, out_shape=(shape((2, 2 * waves, gates), F3...  2.98 us
    unnamed x14, local copies, waits for them, and re-layouts  1.65 us
    pallas_call x1, Pallas kernels, shards(): pl.pallas_call(functools.partial(edge_kernel, devices), grid=(2,), out_sh...  1.36 us
    pallas_call x1, Pallas kernels, shards(): pl.pallas_call(migrate_kernel, out_shape=(shape((2, count, gates), BF16),...  1.13 us
    ppermute x1, starting transfers between devices, ring(): return lax.ppermute(array, 'seg', pairs)  1.04 us
  transfers between devices with their start and end apart: 7, of which 7 were waited for; matrix products, arithmetic and copies ran while one was open for 0% of the time, Pallas kernels for 10%

profile of v1, /device:TPU:8, one launch (start us, length us, event | category | flops | bytes accessed | tf_op | source)
XLA Modules:
  0.0 29.7 jit_solution(430483922669251990)
XLA Ops:
  0.6 0.0 copy-start.6
  0.6 0.0 copy-start.2
  0.7 0.0 copy-start.4
  0.7 0.0 copy-start.5
  0.7 0.0 copy-start.1
  0.7 0.0 copy-start.3
  0.7 0.6 %copy-done.6 = f32[128]{0:T(128)S(1)} copy-done((f32[128]{0:T(128)S(1)}, f32[128]{0:T(128)}, u32[]{:S(2)}) %copy-start.6) | copy-done | bytes 536
  1.3 0.0 copy-done.2
  1.3 0.0 copy-done.4
  1.3 0.0 copy-done.5
  1.3 0.0 copy-done.1
  1.4 0.0 copy-done.3
  1.4 0.0 copy-start
  1.4 0.9 %copy-done = bf16[2,256,256]{2,1,0:T(8,128)(2,1)S(1)} copy-done((bf16[2,256,256]{2,1,0:T(8,128)(2,1)S(1)}, bf16[2,256,256]{2,1,0:T(8,128)(2,1)}, u32[]{:S(2)}) %copy-start) | copy-done | bytes 262168
  2.3 1.1 %migrate.1 = (bf16[2,256,256]{2,1,0:T(8,128)(2,1)S(1)}, f32[8,128]{1,0:T(8,128)S(1)}) custom-call(bf16[2,256,256]{2,1,0:T(8,128)(2,1)S(1)} %copy-done, f32[1,256]{1,0:T(1,128)S(1)} %bitcast.6, s32[1,256]{1,0:T(1,128)S(1)} %bitcast.7, s32[1,128]{1,0:T(1,128)S(1)} %bitcast.8, s32[1,128]{1,0:T(1,128)S(1)} %bitcast.9, f32[1,128]{1,0:T(1,128)S(1)} %bitcast.10, ...), custom_call_target="tpu_custom_call" | custom-call | tf_op jit(solution)/shard_map/migrate/pallas_call | solution.py:205
  3.5 1.6 %collective-permute-start.4 = (bf16[2,256,256]{2,1,0:T(8,128)(2,1)S(1)}, bf16[2,256,256]{2,1,0:T(8,128)(2,1)S(1)}, u32[]{:S(2)}, u32[]{:S(2)}) collective-permute-start(bf16[2,256,256]{2,1,0:T(8,128)(2,1)S(1)} %get-tuple-element.12.own_ref), channel_id=1, source_target_pairs={{0,1},{1,0},{2,3},{3,2},{4,8},{5,9},{6,10},{7,11},{8,4},{9,5},{10,... | collective-permute-start | bytes 786440 | tf_op jit(solution)/shard_map/ppermute | solution.py:34
  5.1 0.0 collective-permute-start.3
  5.1 3.0 %collective-permute-start.2 = (bf16[2,256,256]{2,1,0:T(8,128)(2,1)S(1)}, bf16[2,256,256]{2,1,0:T(8,128)(2,1)S(1)}, u32[]{:S(2)}, u32[]{:S(2)}) collective-permute-start(bf16[2,256,256]{2,1,0:T(8,128)(2,1)S(1)} %get-tuple-element.12.own_ref), channel_id=1, source_target_pairs={{0,1},{1,0},{2,4},{3,5},{4,2},{5,3},{6,8},{7,9},{8,6},{9,7},{10,12... | collective-permute-start | bytes 786440 | tf_op jit(solution)/shard_map/ppermute | solution.py:34
  8.1 0.2 collective-permute-start.1
  8.2 0.0 collective-permute-start
  8.2 1.2 %collective-permute-done.other_ref = f32[8,128]{1,0:T(8,128)S(1)} collective-permute-done((f32[8,128]{1,0:T(8,128)S(1)}, f32[8,128]{1,0:T(8,128)S(1)}, u32[]{:S(2)}, u32[]{:S(2)}) %collective-permute-start) | collective-permute-done | bytes 4128 | tf_op jit(solution)/shard_map/ppermute | solution.py:34
  9.4 3.0 %weights.1 = (f32[2,256,256]{2,1,0:T(8,128)S(1)}, bf16[2,256,1024]{2,1,0:T(8,128)(2,1)S(1)}) custom-call(f32[8,128]{1,0:T(8,128)S(1)} %get-tuple-element.11.params_ref, f32[8,128]{1,0:T(8,128)S(1)} %collective-permute-done.other_ref, bf16[2,256,256]{2,1,0:T(8,128)(2,1)S(1)} %get-tuple-element.12.own_ref), custom_call_target="tpu_custom_call" | custom-call | tf_op jit(solution)/shard_map/weights/pallas_call | solution.py:223
  12.4 0.3 %collective-permute-done.4.b3 = bf16[2,256,256]{2,1,0:T(8,128)(2,1)S(1)} collective-permute-done((bf16[2,256,256]{2,1,0:T(8,128)(2,1)S(1)}, bf16[2,256,256]{2,1,0:T(8,128)(2,1)S(1)}, u32[]{:S(2)}, u32[]{:S(2)}) %collective-permute-start.4) | collective-permute-done | bytes 262176 | tf_op jit(solution)/shard_map/ppermute | solution.py:34
  12.7 0.2 collective-permute-done.3.b2
  12.9 6.6 %collective-permute-done.2.b1 = bf16[2,256,256]{2,1,0:T(8,128)(2,1)S(1)} collective-permute-done((bf16[2,256,256]{2,1,0:T(8,128)(2,1)S(1)}, bf16[2,256,256]{2,1,0:T(8,128)(2,1)S(1)}, u32[]{:S(2)}, u32[]{:S(2)}) %collective-permute-start.2) | collective-permute-done | bytes 262176 | tf_op jit(solution)/shard_map/ppermute | solution.py:34
  19.5 1.4 %collective-permute-done.1.b0 = bf16[2,256,256]{2,1,0:T(8,128)(2,1)S(1)} collective-permute-done((bf16[2,256,256]{2,1,0:T(8,128)(2,1)S(1)}, bf16[2,256,256]{2,1,0:T(8,128)(2,1)S(1)}, u32[]{:S(2)}, u32[]{:S(2)}) %collective-permute-start.1) | collective-permute-done | bytes 262176 | tf_op jit(solution)/shard_map/ppermute | solution.py:34
  20.9 0.7 %focus.1 = (f32[2,144,256]{2,1,0:T(8,128)S(1)}, bf16[2,144,256]{2,1,0:T(8,128)(2,1)S(1)}) custom-call(f32[2,256,256]{2,1,0:T(8,128)S(1)} %get-tuple-element.13.partial_ref, bf16[2,256,1024]{2,1,0:T(8,128)(2,1)S(1)} %get-tuple-element.14.weights_ref, bf16[2,256,256]{2,1,0:T(8,128)(2,1)S(1)} %collective-permute-done.1.b0, ...), custom_call_target="tpu_custom_call" | custom-call | tf_op jit(solution)/shard_map/focus/pallas_call | solution.py:233
  21.6 0.1 collective-permute-start.5
  21.7 1.4 %collective-permute-done.5.got_ref = bf16[2,144,256]{2,1,0:T(8,128)(2,1)S(1)} collective-permute-done((bf16[2,144,256]{2,1,0:T(8,128)(2,1)S(1)}, bf16[2,144,256]{2,1,0:T(8,128)(2,1)S(1)}, u32[]{:S(2)}, u32[]{:S(2)}) %collective-permute-start.5) | collective-permute-done | bytes 147488 | tf_op jit(solution)/shard_map/ppermute | solution.py:34
  23.0 0.8 %power.1 = (bf16[2,128,256]{2,1,0:T(8,128)(2,1)}, f32[128,256]{1,0:T(8,128)}, f32[8,256]{1,0:T(8,128)S(1)}) custom-call(f32[2,144,256]{2,1,0:T(8,128)S(1)} %get-tuple-element.15.keep_ref, bf16[2,144,256]{2,1,0:T(8,128)(2,1)S(1)} %collective-permute-done.5.got_ref), custom_call_target="tpu_custom_call" | custom-call | tf_op jit(solution)/shard_map/power/pallas_call | solution.py:242
  23.8 1.0 %collective-permute-start.6 = (f32[8,256]{1,0:T(8,128)S(1)}, f32[8,256]{1,0:T(8,128)S(1)}, u32[]{:S(2)}, u32[]{:S(2)}) collective-permute-start(f32[8,256]{1,0:T(8,128)S(1)} %get-tuple-element.19), channel_id=1, source_target_pairs={{0,2},{1,0},{2,4},{3,1},{4,6},{5,3},{6,8},{7,5},{8,10},{9,7},{10,1... | collective-permute-start | bytes 24584 | tf_op jit(solution)/shard_map/ppermute | solution.py:43
  24.8 3.5 %collective-permute-done.6.edge_ref = f32[8,256]{1,0:T(8,128)S(1)} collective-permute-done((f32[8,256]{1,0:T(8,128)S(1)}, f32[8,256]{1,0:T(8,128)S(1)}, u32[]{:S(2)}, u32[]{:S(2)}) %collective-permute-start.6) | collective-permute-done | bytes 8224 | tf_op jit(solution)/shard_map/ppermute | solution.py:43
  28.4 1.4 %edge.1 = f32[128,256]{1,0:T(8,128)} custom-call(f32[128,256]{1,0:T(8,128)} %get-tuple-element.18.looked_ref, f32[8,256]{1,0:T(8,128)S(1)} %collective-permute-done.6.edge_ref), custom_call_target="tpu_custom_call", output_to_operand_aliasing={{}: (0, {})} | custom-call | tf_op jit(solution)/shard_map/edge/pallas_call | solution.py:253
Async XLA Ops:
  0.6 0.7 %copy-start.6 = (f32[128]{0:T(128)S(1)}, f32[128]{0:T(128)}, u32[]{:S(2)}) copy-start(f32[128]{0:T(128)} %param.13) | copy-start | bytes 1540
  0.6 0.7 %copy-start.2 = (s32[256]{0:T(256)S(1)}, s32[256]{0:T(256)}, u32[]{:S(2)}) copy-start(s32[256]{0:T(256)} %param.9) | copy-start | bytes 3076
  0.7 0.7 %copy-start.4 = (s32[128]{0:T(128)S(1)}, s32[128]{0:T(128)}, u32[]{:S(2)}) copy-start(s32[128]{0:T(128)} %param.11) | copy-start | bytes 1540
  0.7 0.7 %copy-start.5 = (f32[128]{0:T(128)S(1)}, f32[128]{0:T(128)}, u32[]{:S(2)}) copy-start(f32[128]{0:T(128)} %param.12) | copy-start | bytes 1540
  0.7 0.7 %copy-start.1 = (f32[256]{0:T(256)S(1)}, f32[256]{0:T(256)}, u32[]{:S(2)}) copy-start(f32[256]{0:T(256)} %param.8) | copy-start | bytes 3076
  0.7 0.7 %copy-start.3 = (s32[128]{0:T(128)S(1)}, s32[128]{0:T(128)}, u32[]{:S(2)}) copy-start(s32[128]{0:T(128)} %param.10) | copy-start | bytes 1540
  1.4 1.0 %copy-start = (bf16[2,256,256]{2,1,0:T(8,128)(2,1)S(1)}, bf16[2,256,256]{2,1,0:T(8,128)(2,1)}, u32[]{:S(2)}) copy-start(bf16[2,256,256]{2,1,0:T(8,128)(2,1)} %pulses_ref.1) | copy-start | bytes 786436
  3.5 9.2 %collective-permute-start.4 = (bf16[2,256,256]{2,1,0:T(8,128)(2,1)S(1)}, bf16[2,256,256]{2,1,0:T(8,128)(2,1)S(1)}, u32[]{:S(2)}, u32[]{:S(2)}) collective-permute-start(bf16[2,256,256]{2,1,0:T(8,128)(2,1)S(1)} %get-tuple-element.12.own_ref), channel_id=1, source_target_pairs={{0,1},{1,0},{2,3},{3,2},{4,8},{5,9},{6,10},{7,11},{8,4},{9,5},{10,... | collective-permute-start | bytes 786440 | tf_op jit(solution)/shard_map/ppermute | solution.py:34
  5.1 7.8 %collective-permute-start.3 = (bf16[2,256,256]{2,1,0:T(8,128)(2,1)S(1)}, bf16[2,256,256]{2,1,0:T(8,128)(2,1)S(1)}, u32[]{:S(2)}, u32[]{:S(2)}) collective-permute-start(bf16[2,256,256]{2,1,0:T(8,128)(2,1)S(1)} %get-tuple-element.12.own_ref), channel_id=1, source_target_pairs={{0,4},{1,5},{2,6},{3,7},{4,0},{5,1},{6,2},{7,3},{8,12},{9,13},{10,... | collective-permute-start | bytes 786440 | tf_op jit(solution)/shard_map/ppermute | solution.py:34
  5.1 14.4 %collective-permute-start.2 = (bf16[2,256,256]{2,1,0:T(8,128)(2,1)S(1)}, bf16[2,256,256]{2,1,0:T(8,128)(2,1)S(1)}, u32[]{:S(2)}, u32[]{:S(2)}) collective-permute-start(bf16[2,256,256]{2,1,0:T(8,128)(2,1)S(1)} %get-tuple-element.12.own_ref), channel_id=1, source_target_pairs={{0,1},{1,0},{2,4},{3,5},{4,2},{5,3},{6,8},{7,9},{8,6},{9,7},{10,12... | collective-permute-start | bytes 786440 | tf_op jit(solution)/shard_map/ppermute | solution.py:34
  8.1 12.8 %collective-permute-start.1 = (bf16[2,256,256]{2,1,0:T(8,128)(2,1)S(1)}, bf16[2,256,256]{2,1,0:T(8,128)(2,1)S(1)}, u32[]{:S(2)}, u32[]{:S(2)}) collective-permute-start(bf16[2,256,256]{2,1,0:T(8,128)(2,1)S(1)} %get-tuple-element.12.own_ref), channel_id=1, source_target_pairs={{0,2},{1,3},{2,0},{3,1},{4,6},{5,7},{6,4},{7,5},{8,10},{9,11},{10,... | collective-permute-start | bytes 786440 | tf_op jit(solution)/shard_map/ppermute | solution.py:34
  8.2 1.2 %collective-permute-start = (f32[8,128]{1,0:T(8,128)S(1)}, f32[8,128]{1,0:T(8,128)S(1)}, u32[]{:S(2)}, u32[]{:S(2)}) collective-permute-start(f32[8,128]{1,0:T(8,128)S(1)} %get-tuple-element.11.params_ref), channel_id=1, source_target_pairs={{0,1},{1,0},{2,3},{3,2},{4,5},{5,4},{6,7},{7,6},{8,9},{9,8},{10,11... | collective-permute-start | bytes 12296 | tf_op jit(solution)/shard_map/ppermute | solution.py:34
  21.6 1.4 %collective-permute-start.5 = (bf16[2,144,256]{2,1,0:T(8,128)(2,1)S(1)}, bf16[2,144,256]{2,1,0:T(8,128)(2,1)S(1)}, u32[]{:S(2)}, u32[]{:S(2)}) collective-permute-start(bf16[2,144,256]{2,1,0:T(8,128)(2,1)S(1)} %get-tuple-element.16), channel_id=1, source_target_pairs={{0,1},{1,0},{2,3},{3,2},{4,5},{5,4},{6,7},{7,6},{8,9},{9,8},{10,11... | collective-permute-start | bytes 442376 | tf_op jit(solution)/shard_map/ppermute | solution.py:34
  23.8 4.5 %collective-permute-start.6 = (f32[8,256]{1,0:T(8,128)S(1)}, f32[8,256]{1,0:T(8,128)S(1)}, u32[]{:S(2)}, u32[]{:S(2)}) collective-permute-start(f32[8,256]{1,0:T(8,128)S(1)} %get-tuple-element.19), channel_id=1, source_target_pairs={{0,2},{1,0},{2,4},{3,1},{4,6},{5,3},{6,8},{7,5},{8,10},{9,7},{10,1... | collective-permute-start | bytes 24584 | tf_op jit(solution)/shard_map/ppermute | solution.py:43

commit v2 on v1

v2 whole, which is shorter than its diff:
```python
import functools

import jax
import jax.numpy as jnp
from jax import lax
from jax.experimental import pallas as pl
from jax.experimental.pallas import tpu as pltpu
from jax.sharding import PartitionSpec as P


REACH = 4
LOOK = 8
SHIFT_MAX = 16
F32 = jnp.float32
BF16 = jnp.bfloat16

SIN = (1.0, -0.16666658222675323, 0.008333050645887852, -0.0001980901142815128, 2.605078407214023e-06)
COS = (1.0, -0.5, 0.04166663438081741, -0.0013888359535485506, 2.476008012308739e-05, -2.605002862310357e-07)
PI_HI = 3.140625
PI_LO = 0.0009676536
INV_PI = 0.3183098861837907


SLOTS = ((2, 0), (4, 0), (4, 1))
DIAGONAL = (2, 1)
PARAMS = pltpu.CompilerParams(vmem_limit_bytes=16 * 2**20)


def neighbour(i, by, odd, devices):
    up = (i // by) % 2 == (1 if odd else 0)
    j = i + by if up else i - by
    return j if 0 <= j < devices else i ^ 1


def swap(array, by, odd):
    devices = lax.axis_size("seg")
    return lax.ppermute(array, "seg", [(i, neighbour(i, by, odd, devices)) for i in range(devices)])


def beside(array):
    devices = lax.axis_size("seg")
    return lax.ppermute(array, "seg", [(i, (i + 1 if i % 2 else i - 1) % devices) for i in range(devices)])


def column(row):
    return jnp.transpose(jnp.broadcast_to(row, (8, row.shape[1])))[:, :1]


def migrate_kernel(*refs):
    inputs, (out_ref, params_ref), held, sems = refs[:7], refs[7:9], refs[9:16], refs[16]
    copies = [pltpu.make_async_copy(src, dst, sems.at[k]) for k, (src, dst) in enumerate(zip(inputs, held))]
    for copy in copies:
        copy.start()
    for copy in copies[1:]:
        copy.wait()
    pulses_ref, fraction_ref, shift_ref, start_ref, end_ref, doppler_ref, chirp_ref = held
    gates = pulses_ref.shape[2]
    count = pulses_ref.shape[1]
    shape = (count, gates)
    params_ref[0:1, :] = start_ref[...].astype(F32)
    params_ref[1:2, :] = end_ref[...].astype(F32)
    params_ref[2:3, :] = doppler_ref[...]
    params_ref[3:4, :] = chirp_ref[...]
    params_ref[4:8, :] = jnp.zeros((4, params_ref.shape[1]), F32)
    fraction = jnp.broadcast_to(column(fraction_ref[...]), shape)
    shift = jnp.broadcast_to(column(shift_ref[...].astype(F32)), shape).astype(jnp.int32)
    reach = lax.broadcasted_iota(jnp.int32, shape, 1) + shift
    first = jnp.where(reach < gates, 1.0 - fraction, 0.0)
    second = jnp.where(reach + 1 < gates, fraction, 0.0)
    copies[0].wait()
    for part in range(2):
        moved = pulses_ref[part].astype(F32)
        bit = 1
        while bit < SHIFT_MAX:
            moved = jnp.where((shift & bit) != 0, pltpu.roll(moved, gates - bit, 1), moved)
            bit *= 2
        out_ref[part] = (first * moved + second * pltpu.roll(moved, gates - 1, 1)).astype(BF16)


def poly(coefs, z):
    total = coefs[-1] * z + coefs[-2]
    for c in coefs[-3::-1]:
        total = total * z + c
    return total


def spread(refs, cols):
    for at, ref in enumerate(refs):
        waves = ref.shape[1]
        start, end = ref[0:1, :], ref[1:2, :]
        center = jnp.floor((start + end) * 0.5)
        scale = lax.rsqrt(end - start)
        stack = jnp.concatenate([center, start, end, ref[2:3, :], ref[3:4, :], scale, scale, scale], 0)
        turned = jnp.transpose(stack)
        for k in range(6):
            cols[k, at * waves : (at + 1) * waves, :] = jnp.broadcast_to(turned[:, k : k + 1], (waves, 128))


def weigh(cols, base, pulse_count, rows, put):
    total_rows = cols.shape[1]

    def step(k, carry):
        r = pl.multiple_of(k * rows, rows)
        center, start, end, doppler, chirp, scale = (cols[j, pl.ds(r, rows), :] for j in range(6))
        for lane in range(0, pulse_count, 128):
            pulse = (lax.broadcasted_iota(jnp.int32, (rows, 128), 1) + (base + lane)).astype(F32)
            relative = (pulse - center) * (1.0 / (REACH * pulse_count))
            phase = chirp * relative * relative + doppler * relative
            turns = jnp.round(phase * INV_PI)
            rest = (phase - turns * PI_HI) - turns * PI_LO
            square = rest * rest
            signed = jnp.where((turns.astype(jnp.int32) & 1) != 0, -scale, scale)
            signed = jnp.where((pulse >= start) & (pulse < end), signed, 0.0)
            put(r, lane, signed * poly(COS, square), signed * rest * poly(SIN, square))
        return carry

    lax.fori_loop(0, total_rows // rows, step, 0, unroll=2)


def partner(device, by, odd):
    return jnp.where((device // by) % 2 == odd, device + by, device - by)


dot = functools.partial(jnp.dot, preferred_element_type=F32)


def into(ref, at):
    def put(r, lane, re, im):
        ref[0, pl.ds(r, 16), at + lane : at + lane + 128] = re.astype(BF16)
        ref[1, pl.ds(r, 16), at + lane : at + lane + 128] = im.astype(BF16)

    return put


def lend_kernel(target_ref, own_ref, mate_ref, out_ref, cols, w):
    device = lax.axis_index("seg")
    count = own_ref.shape[1]
    mate = device + 1 - 2 * (device % 2)
    spread((target_ref,), cols)
    weigh(cols, device * count, count, 16, into(w, 0))
    weigh(cols, mate * count, count, 16, into(w, count))
    re, im = w[0], w[1]
    a = dot(re[:, :count], own_ref[0]) + dot(re[:, count:], mate_ref[0])
    b = dot(im[:, :count], own_ref[1]) + dot(im[:, count:], mate_ref[1])
    c = dot(re[:, :count], own_ref[1]) + dot(re[:, count:], mate_ref[1])
    d = dot(im[:, :count], own_ref[0]) + dot(im[:, count:], mate_ref[0])
    out_ref[0] = (a - b).astype(BF16)
    out_ref[1] = (c + d).astype(BF16)


def weights_kernel(params_ref, other_ref, own_ref, partial_ref, weights_ref, cols, own_w):
    device = lax.axis_index("seg")
    count = own_ref.shape[1]
    spread((params_ref, other_ref), cols)
    weigh(cols, device * count, count, 16, into(own_w, 0))
    partial_ref[0] = dot(own_w[0], own_ref[0]) - dot(own_w[1], own_ref[1])
    partial_ref[1] = dot(own_w[0], own_ref[1]) + dot(own_w[1], own_ref[0])
    for slot, (by, odd) in enumerate(SLOTS):
        weigh(cols, partner(device, by, odd) * count, count, 16, into(weights_ref, slot * count))


def focus_kernel(partial_ref, weights_ref, *refs):
    blocks, (keep_ref, message_ref) = refs[:-2], refs[-2:]
    count = blocks[0].shape[1]
    waves = keep_ref.shape[1]
    re, im = partial_ref[0], partial_ref[1]
    minus = jnp.zeros_like(re)
    for slot, ref in enumerate(blocks):
        w_re = weights_ref[0, :, slot * count : (slot + 1) * count]
        w_im = weights_ref[1, :, slot * count : (slot + 1) * count]
        re += dot(w_re, ref[0])
        minus += dot(w_im, ref[1])
        im += dot(w_re, ref[1])
        im += dot(w_im, ref[0])
    re = re - minus
    for part, value in enumerate((re, im)):
        keep_ref[part] = value[:waves]
        message_ref[part] = value[waves:].astype(BF16)


def total_of(device, devices, rows, keep_ref, got_ref, lent_ref):
    by_chip = partner(device, *DIAGONAL)
    known = (by_chip >= 0) & (by_chip < devices)
    lent = jnp.where(known, lent_ref[:, rows].astype(F32), 0.0)
    return keep_ref[:, rows] + got_ref[:, rows].astype(F32) + lent


def ends_kernel(devices, keep_ref, got_ref, lent_ref, near_ref, far_ref):
    device = lax.axis_index("seg")
    waves = keep_ref.shape[1]
    powers = []
    for rows in (slice(0, 2 * LOOK), slice(waves - 2 * LOOK, waves)):
        total = total_of(device, devices, rows, keep_ref, got_ref, lent_ref)
        powers.append(total[0] * total[0] + total[1] * total[1])
    initial, last = powers[0][:LOOK], powers[1][LOOK:]
    core = device % 2
    near_ref[...] = jnp.where(core == 0, last, initial)
    far_ref[...] = jnp.where(core == 0, initial, last)


def power_kernel(devices, keep_ref, got_ref, lent_ref, focused_ref, looked_ref, ends_ref, ext):
    waves = focused_ref.shape[1]
    total = total_of(lax.axis_index("seg"), devices, slice(0, waves), keep_ref, got_ref, lent_ref)
    focused_ref[...] = total.astype(BF16)
    ext[:LOOK] = jnp.zeros((LOOK, ext.shape[1]), F32)
    ext[LOOK : LOOK + waves] = total[0] * total[0] + total[1] * total[1]
    ext[LOOK + waves :] = jnp.zeros((LOOK, ext.shape[1]), F32)
    rows = waves + 2 * LOOK
    span, window = 1, ext[...]
    while span < 2 * LOOK:
        rows -= span
        window = window[:rows] + window[span : span + rows]
        span *= 2
    looked = (window[:waves] + ext[2 * LOOK :]) * (1.0 / (2 * LOOK + 1))
    looked_ref[...] = looked
    ends_ref[:LOOK] = looked[:LOOK]
    ends_ref[LOOK:] = looked[waves - LOOK :]


def edge_kernel(devices, looked_ref, ends_ref, near_ref, far_ref, out_ref, rows, sems):
    device = lax.axis_index("seg")
    core = device % 2
    beside = device + 2 * core - 1
    scale = 1.0 / (2 * LOOK + 1)
    near = near_ref[...] * scale
    far = far_ref[...] * jnp.where((beside >= 0) & (beside < devices), scale, 0.0)
    row = lax.broadcasted_iota(jnp.int32, near.shape, 0)
    before, after = jnp.where(core == 0, far, near), jnp.where(core == 0, near, far)
    top, bottom = ends_ref[:LOOK], ends_ref[LOOK:]
    for h in range(LOOK):
        top += jnp.where(row <= h, before[h : h + 1, :], 0.0)
        bottom += jnp.where(row >= h, after[h : h + 1, :], 0.0)
    rows[0] = top
    rows[1] = bottom
    waves = out_ref.shape[0]
    copies = [
        pltpu.make_async_copy(rows.at[k], out_ref.at[pl.ds(at, LOOK)], sems.at[k])
        for k, at in enumerate((0, waves - LOOK))
    ]
    for copy in copies:
        copy.start()
    for copy in copies:
        copy.wait()


def shards(pulses, fraction, gate_shift, aperture_start, aperture_end, doppler, chirp_rate):
    _, count, gates = pulses.shape
    waves = aperture_start.shape[0]
    devices = lax.axis_size("seg")
    shape = jax.ShapeDtypeStruct
    vmem = pl.BlockSpec(memory_space=pltpu.VMEM)
    hbm = pl.BlockSpec(memory_space=pltpu.HBM)

    inputs = (
        pulses,
        fraction.reshape(1, count),
        gate_shift.reshape(1, count),
        aperture_start.reshape(1, waves),
        aperture_end.reshape(1, waves),
        doppler.reshape(1, waves),
        chirp_rate.reshape(1, waves),
    )
    migrated, params = pl.pallas_call(
        migrate_kernel,
        out_shape=(shape((2, count, gates), BF16), shape((8, waves), F32)),
        in_specs=[hbm] * 7,
        out_specs=(vmem, vmem),
        scratch_shapes=[pltpu.VMEM(a.shape, a.dtype) for a in inputs] + [pltpu.SemaphoreType.DMA((7,))],
        compiler_params=PARAMS,
        name="migrate",
    )(*(pltpu.with_memory_space_constraint(a, pltpu.HBM) for a in inputs))
    blocks = [swap(migrated, by, odd) for by, odd in SLOTS]
    target = swap(params, *DIAGONAL)
    mate = swap(migrated, 1, 0)
    other = swap(params, 1, 0)
    lending = pl.pallas_call(
        lend_kernel,
        out_shape=shape((2, waves, gates), BF16),
        in_specs=[vmem] * 3,
        out_specs=vmem,
        scratch_shapes=[pltpu.VMEM((6, waves, 128), F32), pltpu.VMEM((2, waves, 2 * count), BF16)],
        compiler_params=PARAMS,
        name="lend",
    )(target, migrated, mate)
    lent = swap(lending, *DIAGONAL)
    partial, weights = pl.pallas_call(
        weights_kernel,
        out_shape=(shape((2, 2 * waves, gates), F32), shape((2, 2 * waves, len(SLOTS) * count), BF16)),
        in_specs=[vmem] * 3,
        out_specs=(vmem, vmem),
        scratch_shapes=[pltpu.VMEM((6, 2 * waves, 128), F32), pltpu.VMEM((2, 2 * waves, count), BF16)],
        compiler_params=PARAMS,
        name="weights",
    )(params, other, migrated)
    keep, message = pl.pallas_call(
        focus_kernel,
        out_shape=(shape((2, waves, gates), F32), shape((2, waves, gates), BF16)),
        in_specs=[vmem] * (2 + len(blocks)),
        out_specs=(vmem, vmem),
        compiler_params=PARAMS,
        name="focus",
    )(partial, weights, *blocks)
    got = swap(message, 1, 0)
    near, far = pl.pallas_call(
        functools.partial(ends_kernel, devices),
        out_shape=(shape((LOOK, gates), F32),) * 2,
        in_specs=[vmem] * 3,
        out_specs=(vmem, vmem),
        compiler_params=PARAMS,
        name="ends",
    )(keep, got, lent)
    far = beside(far)
    near = swap(near, 1, 0)
    focused, looked, ends = pl.pallas_call(
        functools.partial(power_kernel, devices),
        out_shape=(shape((2, waves, gates), BF16), shape((waves, gates), F32), shape((2 * LOOK, gates), F32)),
        in_specs=[vmem] * 3,
        out_specs=(vmem, vmem, vmem),
        scratch_shapes=[pltpu.VMEM((waves + 2 * LOOK, gates), F32)],
        compiler_params=PARAMS,
        name="power",
    )(keep, got, lent)
    multilook = pl.pallas_call(
        functools.partial(edge_kernel, devices),
        out_shape=shape((waves, gates), F32),
        in_specs=[hbm, vmem, vmem, vmem],
        out_specs=hbm,
        scratch_shapes=[pltpu.VMEM((2, LOOK, gates), F32), pltpu.SemaphoreType.DMA((2,))],
        input_output_aliases={0: 0},
        compiler_params=PARAMS,
        name="edge",
    )(looked, ends, near, far)
    return (focused, multilook)


def solution(mesh):
    part = P(("arcs", "seg"))
    return jax.shard_map(
        shards,
        mesh=mesh,
        in_specs=(P(None, ("arcs", "seg"), None),) + (part,) * 6,
        out_specs=(P(None, ("arcs", "seg"), None), P(("arcs", "seg"), None)),
        check_vma=False,
    )
```

time: 29.9 us -> 25.7 us (0.86)
  waiting for transfers between devices: 14.5 us -> 11 us
  local copies, waits for them, and re-layouts: 1.65 us -> 0 us
  Pallas kernels: 6.93 us -> 7.59 us
  starting transfers between devices: 5.87 us -> 6.2 us
    ppermute x6 -> x9, waiting for transfers between devices: 11 us -> 8.22 us  [swap(): lax.ppermute(array, 'seg', [(i, neighbour(i, by, odd, devices)) for i in...]
    unnamed x14 -> x0, local copies, waits for them, and re-layouts: 1.65 us -> none
    ppermute x6 -> x9, starting transfers between devices: 4.83 us -> 5.76 us  [swap(): lax.ppermute(array, 'seg', [(i, neighbour(i, by, odd, devices)) for i in...]
    pallas_call x1, Pallas kernels: 1.13 us -> 1.99 us  [shards(): pl.pallas_call(migrate_kernel, out_shape=(shape((2, count, gates), BF16),...]
    ppermute x1, waiting for transfers between devices: 3.51 us -> 2.81 us  [beside(): lax.ppermute(array, 'seg', [(i, (i + 1 if i % 2 else i - 1) % devices) fo...]
    ppermute x1, starting transfers between devices: 1.04 us -> 0.45 us  [beside(): lax.ppermute(array, 'seg', [(i, (i + 1 if i % 2 else i - 1) % devices) fo...]
    pallas_call x1, Pallas kernels: 2.98 us -> 2.52 us  [shards(): pl.pallas_call(weights_kernel, out_shape=(shape((2, 2 * waves, gates), F3...]
    pallas_call x3 -> x5, Pallas kernels: 2.82 us -> 3.08 us  [the longest x1 1.07 us: shards(): pl.pallas_call(lend_kernel, out_shape=shape((2, waves, gates), BF16), in_...]
  transfers between devices with their start and end apart: 7 -> 10, of which waited for: 7 -> 4; matrix products, arithmetic and copies ran while one was open for 0% -> 0% of each run, Pallas kernels for 10% -> 19%
where the time goes in v2:
time: 25.7 us; the launch traced here: 25.5 us
  waiting for transfers between devices  11 us (43%)
  Pallas kernels  7.59 us (30%)
  starting transfers between devices  6.2 us (24%)
  between operations  0.7 us (3%)
    ppermute x9, waiting for transfers between devices, swap(): lax.ppermute(array, 'seg', [(i, neighbour(i, by, odd, devices)) for i in...  8.22 us
    ppermute x9, starting transfers between devices, swap(): lax.ppermute(array, 'seg', [(i, neighbour(i, by, odd, devices)) for i in...  5.76 us
    ppermute x1, waiting for transfers between devices, beside(): lax.ppermute(array, 'seg', [(i, (i + 1 if i % 2 else i - 1) % devices) fo...  2.81 us
    pallas_call x1, Pallas kernels, shards(): pl.pallas_call(weights_kernel, out_shape=(shape((2, 2 * waves, gates), F3...  2.52 us
    pallas_call x1, Pallas kernels, shards(): pl.pallas_call(migrate_kernel, out_shape=(shape((2, count, gates), BF16),...  1.99 us
    pallas_call x1, Pallas kernels, shards(): pl.pallas_call(lend_kernel, out_shape=shape((2, waves, gates), BF16), in_...  1.07 us
    pallas_call x1, Pallas kernels, shards(): pl.pallas_call(functools.partial(power_kernel, devices), out_shape=(shape...  0.78 us
    pallas_call x1, Pallas kernels, shards(): pl.pallas_call(functools.partial(edge_kernel, devices), out_shape=shape((...  0.64 us
  transfers between devices with their start and end apart: 10, of which 4 were waited for; matrix products, arithmetic and copies ran while one was open for 0% of the time, Pallas kernels for 19%

profile of v2, /device:TPU:8, one launch (start us, length us, event | category | flops | bytes accessed | tf_op | source)
XLA Modules:
  0.0 25.5 jit_solution(6743202046929562062)
XLA Ops:
  0.6 2.0 %migrate.1 = (bf16[2,256,256]{2,1,0:T(8,128)(2,1)S(1)}, f32[8,128]{1,0:T(8,128)S(1)}) custom-call(bf16[2,256,256]{2,1,0:T(8,128)(2,1)} %refs_0_.1, f32[1,256]{1,0:T(1,128)} %bitcast.6, s32[1,256]{1,0:T(1,128)} %bitcast.7, s32[1,128]{1,0:T(1,128)} %bitcast.8, s32[1,128]{1,0:T(1,128)} %bitcast.9, f32[1,128]{1,0:T(1,128)} %bitcast.10, f32[1,128]{1,0:T(1,128)} %bitcast.11), custom_call_target="tpu_custom_call" | custom-call | tf_op jit(solution)/shard_map/migrate/pallas_call | solution.py:263
  2.6 0.1 collective-permute-start.6
  2.7 1.6 %collective-permute-start.3 = (bf16[2,256,256]{2,1,0:T(8,128)(2,1)S(1)}, bf16[2,256,256]{2,1,0:T(8,128)(2,1)S(1)}, u32[]{:S(2)}, u32[]{:S(2)}) collective-permute-start(bf16[2,256,256]{2,1,0:T(8,128)(2,1)S(1)} %get-tuple-element.14.own_ref), channel_id=1, source_target_pairs={{0,1},{1,0},{2,3},{3,2},{4,8},{5,9},{6,10},{7,11},{8,4},{9,5},{10,... | collective-permute-start | bytes 786440 | tf_op jit(solution)/shard_map/ppermute | solution.py:37
  4.4 0.0 collective-permute-start.2
  4.4 1.5 %collective-permute-start.1 = (bf16[2,256,256]{2,1,0:T(8,128)(2,1)S(1)}, bf16[2,256,256]{2,1,0:T(8,128)(2,1)S(1)}, u32[]{:S(2)}, u32[]{:S(2)}) collective-permute-start(bf16[2,256,256]{2,1,0:T(8,128)(2,1)S(1)} %get-tuple-element.14.own_ref), channel_id=1, source_target_pairs={{0,2},{1,3},{2,0},{3,1},{4,6},{5,7},{6,4},{7,5},{8,10},{9,11},{10,... | collective-permute-start | bytes 786440 | tf_op jit(solution)/shard_map/ppermute | solution.py:37
  5.8 0.0 collective-permute-start
  5.9 1.2 %collective-permute-done.other_ref = f32[8,128]{1,0:T(8,128)S(1)} collective-permute-done((f32[8,128]{1,0:T(8,128)S(1)}, f32[8,128]{1,0:T(8,128)S(1)}, u32[]{:S(2)}, u32[]{:S(2)}) %collective-permute-start) | collective-permute-done | bytes 4128 | tf_op jit(solution)/shard_map/ppermute | solution.py:37
  7.0 2.0 %collective-permute-start.5 = (f32[8,128]{1,0:T(8,128)S(1)}, f32[8,128]{1,0:T(8,128)S(1)}, u32[]{:S(2)}, u32[]{:S(2)}) collective-permute-start(f32[8,128]{1,0:T(8,128)S(1)} %get-tuple-element.13.params_ref), channel_id=1, source_target_pairs={{0,1},{1,0},{2,4},{3,5},{4,2},{5,3},{6,8},{7,9},{8,6},{9,7},{10,12... | collective-permute-start | bytes 12296 | tf_op jit(solution)/shard_map/ppermute | solution.py:37
  9.0 2.5 %weights.1 = (f32[2,256,256]{2,1,0:T(8,128)S(1)}, bf16[2,256,768]{2,1,0:T(8,128)(2,1)S(1)}) custom-call(f32[8,128]{1,0:T(8,128)S(1)} %get-tuple-element.13.params_ref, f32[8,128]{1,0:T(8,128)S(1)} %collective-permute-done.other_ref, bf16[2,256,256]{2,1,0:T(8,128)(2,1)S(1)} %get-tuple-element.14.own_ref), custom_call_target="tpu_custom_call" | custom-call | tf_op jit(solution)/shard_map/weights/pallas_call | solution.py:286
  11.5 2.2 %collective-permute-done.5.target_ref = f32[8,128]{1,0:T(8,128)S(1)} collective-permute-done((f32[8,128]{1,0:T(8,128)S(1)}, f32[8,128]{1,0:T(8,128)S(1)}, u32[]{:S(2)}, u32[]{:S(2)}) %collective-permute-start.5) | collective-permute-done | bytes 4128 | tf_op jit(solution)/shard_map/ppermute | solution.py:37
  13.7 0.0 collective-permute-done.6.mate_ref
  13.7 1.1 %lend.1 = bf16[2,128,256]{2,1,0:T(8,128)(2,1)S(1)} custom-call(f32[8,128]{1,0:T(8,128)S(1)} %collective-permute-done.5.target_ref, bf16[2,256,256]{2,1,0:T(8,128)(2,1)S(1)} %get-tuple-element.14.own_ref, bf16[2,256,256]{2,1,0:T(8,128)(2,1)S(1)} %collective-permute-done.6.mate_ref), custom_call_target="tpu_custom_call" | custom-call | tf_op jit(solution)/shard_map/lend/pallas_call | solution.py:276
  14.8 0.4 %collective-permute-start.7 = (bf16[2,128,256]{2,1,0:T(8,128)(2,1)S(1)}, bf16[2,128,256]{2,1,0:T(8,128)(2,1)S(1)}, u32[]{:S(2)}, u32[]{:S(2)}) collective-permute-start(bf16[2,128,256]{2,1,0:T(8,128)(2,1)S(1)} %lend.1), channel_id=1, source_target_pairs={{0,1},{1,0},{2,4},{3,5},{4,2},{5,3},{6,8},{7,9},{8,6},{9,7},{10,12... | collective-permute-start | bytes 393224 | tf_op jit(solution)/shard_map/ppermute | solution.py:37
  15.2 0.0 collective-permute-done.3.refs_2_
  15.2 0.0 collective-permute-done.2.refs_1_
  15.2 0.0 collective-permute-done.1.refs_0_
  15.2 0.6 %focus.1 = (f32[2,128,256]{2,1,0:T(8,128)S(1)}, bf16[2,128,256]{2,1,0:T(8,128)(2,1)S(1)}) custom-call(f32[2,256,256]{2,1,0:T(8,128)S(1)} %get-tuple-element.15.partial_ref, bf16[2,256,768]{2,1,0:T(8,128)(2,1)S(1)} %get-tuple-element.16.weights_ref, bf16[2,256,256]{2,1,0:T(8,128)(2,1)S(1)} %collective-permute-done.1.refs_0_, ...), custom_call_target="tpu_custom_call" | custom-call | tf_op jit(solution)/shard_map/focus/pallas_call | solution.py:295
  15.8 0.1 collective-permute-start.4
  15.9 4.8 %collective-permute-done.7.lent_ref = bf16[2,128,256]{2,1,0:T(8,128)(2,1)S(1)} collective-permute-done((bf16[2,128,256]{2,1,0:T(8,128)(2,1)S(1)}, bf16[2,128,256]{2,1,0:T(8,128)(2,1)S(1)}, u32[]{:S(2)}, u32[]{:S(2)}) %collective-permute-start.7) | collective-permute-done | bytes 131104 | tf_op jit(solution)/shard_map/ppermute | solution.py:37
  20.7 0.0 collective-permute-done.4.got_ref
  20.8 0.1 collective-permute-start.8
  20.8 0.4 %collective-permute-start.9 = (f32[8,256]{1,0:T(8,128)S(1)}, f32[8,256]{1,0:T(8,128)S(1)}, u32[]{:S(2)}, u32[]{:S(2)}) collective-permute-start(f32[8,256]{1,0:T(8,128)S(1)} %get-tuple-element.23), channel_id=1, source_target_pairs={{0,15},{1,2},{2,1},{3,4},{4,3},{5,6},{6,5},{7,8},{8,7},{9,10},{10,... | collective-permute-start | bytes 24584 | tf_op jit(solution)/shard_map/ppermute | solution.py:42
  21.3 0.8 %power.1 = (bf16[2,128,256]{2,1,0:T(8,128)(2,1)}, f32[128,256]{1,0:T(8,128)}, f32[16,256]{1,0:T(8,128)S(1)}) custom-call(f32[2,128,256]{2,1,0:T(8,128)S(1)} %get-tuple-element.17.keep_ref, bf16[2,128,256]{2,1,0:T(8,128)(2,1)S(1)} %collective-permute-done.4.got_ref, bf16[2,128,256]{2,1,0:T(8,128)(2,1)S(1)} %collective-permute-done.7.lent_ref), custom_call_target="tpu_custom_call" | custom-call | tf_op jit(solution)/shard_map/power/pallas_call | solution.py:314
  22.1 0.0 collective-permute-done.8.near_ref
  22.1 2.8 %collective-permute-done.9.far_ref = f32[8,256]{1,0:T(8,128)S(1)} collective-permute-done((f32[8,256]{1,0:T(8,128)S(1)}, f32[8,256]{1,0:T(8,128)S(1)}, u32[]{:S(2)}, u32[]{:S(2)}) %collective-permute-start.9) | collective-permute-done | bytes 8224 | tf_op jit(solution)/shard_map/ppermute | solution.py:42
  24.9 0.6 %edge.1 = f32[128,256]{1,0:T(8,128)} custom-call(f32[128,256]{1,0:T(8,128)} %get-tuple-element.20.looked_ref, f32[16,256]{1,0:T(8,128)S(1)} %get-tuple-element.21.ends_ref, f32[8,256]{1,0:T(8,128)S(1)} %collective-permute-done.8.near_ref, f32[8,256]{1,0:T(8,128)S(1)} %collective-permute-done.9.far_ref), custom_call_target="tpu_custom_call", output_to_operand_aliasing={{}: (0, {})} | custom-call | tf_op jit(solution)/shard_map/edge/pallas_call | solution.py:323
  (1 shorter events, 0.0 us)
Async XLA Ops:
  2.6 11.1 %collective-permute-start.6 = (bf16[2,256,256]{2,1,0:T(8,128)(2,1)S(1)}, bf16[2,256,256]{2,1,0:T(8,128)(2,1)S(1)}, u32[]{:S(2)}, u32[]{:S(2)}) collective-permute-start(bf16[2,256,256]{2,1,0:T(8,128)(2,1)S(1)} %get-tuple-element.14.own_ref), channel_id=1, source_target_pairs={{0,1},{1,0},{2,3},{3,2},{4,5},{5,4},{6,7},{7,6},{8,9},{9,8},{10,11... | collective-permute-start | bytes 786440 | tf_op jit(solution)/shard_map/ppermute | solution.py:37
  2.7 12.5 %collective-permute-start.3 = (bf16[2,256,256]{2,1,0:T(8,128)(2,1)S(1)}, bf16[2,256,256]{2,1,0:T(8,128)(2,1)S(1)}, u32[]{:S(2)}, u32[]{:S(2)}) collective-permute-start(bf16[2,256,256]{2,1,0:T(8,128)(2,1)S(1)} %get-tuple-element.14.own_ref), channel_id=1, source_target_pairs={{0,1},{1,0},{2,3},{3,2},{4,8},{5,9},{6,10},{7,11},{8,4},{9,5},{10,... | collective-permute-start | bytes 786440 | tf_op jit(solution)/shard_map/ppermute | solution.py:37
  4.4 10.9 %collective-permute-start.2 = (bf16[2,256,256]{2,1,0:T(8,128)(2,1)S(1)}, bf16[2,256,256]{2,1,0:T(8,128)(2,1)S(1)}, u32[]{:S(2)}, u32[]{:S(2)}) collective-permute-start(bf16[2,256,256]{2,1,0:T(8,128)(2,1)S(1)} %get-tuple-element.14.own_ref), channel_id=1, source_target_pairs={{0,4},{1,5},{2,6},{3,7},{4,0},{5,1},{6,2},{7,3},{8,12},{9,13},{10,... | collective-permute-start | bytes 786440 | tf_op jit(solution)/shard_map/ppermute | solution.py:37
  4.4 10.9 %collective-permute-start.1 = (bf16[2,256,256]{2,1,0:T(8,128)(2,1)S(1)}, bf16[2,256,256]{2,1,0:T(8,128)(2,1)S(1)}, u32[]{:S(2)}, u32[]{:S(2)}) collective-permute-start(bf16[2,256,256]{2,1,0:T(8,128)(2,1)S(1)} %get-tuple-element.14.own_ref), channel_id=1, source_target_pairs={{0,2},{1,3},{2,0},{3,1},{4,6},{5,7},{6,4},{7,5},{8,10},{9,11},{10,... | collective-permute-start | bytes 786440 | tf_op jit(solution)/shard_map/ppermute | solution.py:37
  5.8 1.2 %collective-permute-start = (f32[8,128]{1,0:T(8,128)S(1)}, f32[8,128]{1,0:T(8,128)S(1)}, u32[]{:S(2)}, u32[]{:S(2)}) collective-permute-start(f32[8,128]{1,0:T(8,128)S(1)} %get-tuple-element.13.params_ref), channel_id=1, source_target_pairs={{0,1},{1,0},{2,3},{3,2},{4,5},{5,4},{6,7},{7,6},{8,9},{9,8},{10,11... | collective-permute-start | bytes 12296 | tf_op jit(solution)/shard_map/ppermute | solution.py:37
  7.0 6.7 %collective-permute-start.5 = (f32[8,128]{1,0:T(8,128)S(1)}, f32[8,128]{1,0:T(8,128)S(1)}, u32[]{:S(2)}, u32[]{:S(2)}) collective-permute-start(f32[8,128]{1,0:T(8,128)S(1)} %get-tuple-element.13.params_ref), channel_id=1, source_target_pairs={{0,1},{1,0},{2,4},{3,5},{4,2},{5,3},{6,8},{7,9},{8,6},{9,7},{10,12... | collective-permute-start | bytes 12296 | tf_op jit(solution)/shard_map/ppermute | solution.py:37
  14.8 5.9 %collective-permute-start.7 = (bf16[2,128,256]{2,1,0:T(8,128)(2,1)S(1)}, bf16[2,128,256]{2,1,0:T(8,128)(2,1)S(1)}, u32[]{:S(2)}, u32[]{:S(2)}) collective-permute-start(bf16[2,128,256]{2,1,0:T(8,128)(2,1)S(1)} %lend.1), channel_id=1, source_target_pairs={{0,1},{1,0},{2,4},{3,5},{4,2},{5,3},{6,8},{7,9},{8,6},{9,7},{10,12... | collective-permute-start | bytes 393224 | tf_op jit(solution)/shard_map/ppermute | solution.py:37
  15.8 4.9 %collective-permute-start.4 = (bf16[2,128,256]{2,1,0:T(8,128)(2,1)S(1)}, bf16[2,128,256]{2,1,0:T(8,128)(2,1)S(1)}, u32[]{:S(2)}, u32[]{:S(2)}) collective-permute-start(bf16[2,128,256]{2,1,0:T(8,128)(2,1)S(1)} %get-tuple-element.18), channel_id=1, source_target_pairs={{0,1},{1,0},{2,3},{3,2},{4,5},{5,4},{6,7},{7,6},{8,9},{9,8},{10,11... | collective-permute-start | bytes 393224 | tf_op jit(solution)/shard_map/ppermute | solution.py:37
  20.8 1.3 %collective-permute-start.8 = (f32[8,256]{1,0:T(8,128)S(1)}, f32[8,256]{1,0:T(8,128)S(1)}, u32[]{:S(2)}, u32[]{:S(2)}) collective-permute-start(f32[8,256]{1,0:T(8,128)S(1)} %get-tuple-element.22), channel_id=1, source_target_pairs={{0,1},{1,0},{2,3},{3,2},{4,5},{5,4},{6,7},{7,6},{8,9},{9,8},{10,11... | collective-permute-start | bytes 24584 | tf_op jit(solution)/shard_map/ppermute | solution.py:37
  20.8 4.0 %collective-permute-start.9 = (f32[8,256]{1,0:T(8,128)S(1)}, f32[8,256]{1,0:T(8,128)S(1)}, u32[]{:S(2)}, u32[]{:S(2)}) collective-permute-start(f32[8,256]{1,0:T(8,128)S(1)} %get-tuple-element.23), channel_id=1, source_target_pairs={{0,15},{1,2},{2,1},{3,4},{4,3},{5,6},{6,5},{7,8},{8,7},{9,10},{10,... | collective-permute-start | bytes 24584 | tf_op jit(solution)/shard_map/ppermute | solution.py:42

commit v3 on v2

--- a/solution.py
+++ b/solution.py
@@ -1,4 +1,5 @@
 import functools
+import math
 
 import jax
 import jax.numpy as jnp
@@ -10,17 +11,11 @@
 
 REACH = 4
 LOOK = 8
-SHIFT_MAX = 16
 F32 = jnp.float32
 BF16 = jnp.bfloat16
 
-SIN = (1.0, -0.16666658222675323, 0.008333050645887852, -0.0001980901142815128, 2.605078407214023e-06)
-COS = (1.0, -0.5, 0.04166663438081741, -0.0013888359535485506, 2.476008012308739e-05, -2.605002862310357e-07)
-PI_HI = 3.140625
-PI_LO = 0.0009676536
-INV_PI = 0.3183098861837907
-
-
+SIN = (3.1415927410125732, -5.167710304260254, 2.550077438354492, -0.5982902646064758, 0.07765503972768784)
+COS = (0.9999999403953552, -4.934792995452881, 4.058411121368408, -1.3318735361099243, 0.21968165040016174)
 SLOTS = ((2, 0), (4, 0), (4, 1))
 DIAGONAL = (2, 1)
 PARAMS = pltpu.CompilerParams(vmem_limit_bytes=16 * 2**20)
@@ -38,43 +33,50 @@
 
 
 def beside(array):
-    devices = lax.axis_size("seg")
-    return lax.ppermute(array, "seg", [(i, (i + 1 if i % 2 else i - 1) % devices) for i in range(devices)])
-
-
-def column(row):
-    return jnp.transpose(jnp.broadcast_to(row, (8, row.shape[1])))[:, :1]
+    arcs, devices = lax.axis_size("arcs"), lax.axis_size("seg")
+    pairs = []
+    for arc in range(arcs):
+        for i in range(devices):
+            j = i + 1 if i % 2 else i - 1
+            to = (arc, j) if 0 <= j < devices else (arc ^ 1, i) if arcs % 2 == 0 else (arc, j % devices)
+            pairs.append((arc * devices + i, to[0] * devices + to[1]))
+    return lax.ppermute(array, ("arcs", "seg"), pairs)
 
 
 def migrate_kernel(*refs):
-    inputs, (out_ref, params_ref), held, sems = refs[:7], refs[7:9], refs[9:16], refs[16]
+    inputs, (out_ref, params_ref), held, (turned, sems) = refs[:7], refs[7:9], refs[9:16], refs[16:]
     copies = [pltpu.make_async_copy(src, dst, sems.at[k]) for k, (src, dst) in enumerate(zip(inputs, held))]
     for copy in copies:
         copy.start()
     for copy in copies[1:]:
         copy.wait()
     pulses_ref, fraction_ref, shift_ref, start_ref, end_ref, doppler_ref, chirp_ref = held
-    gates = pulses_ref.shape[2]
-    count = pulses_ref.shape[1]
-    shape = (count, gates)
+    _, count, gates = pulses_ref.shape
     params_ref[0:1, :] = start_ref[...].astype(F32)
     params_ref[1:2, :] = end_ref[...].astype(F32)
     params_ref[2:3, :] = doppler_ref[...]
     params_ref[3:4, :] = chirp_ref[...]
     params_ref[4:8, :] = jnp.zeros((4, params_ref.shape[1]), F32)
-    fraction = jnp.broadcast_to(column(fraction_ref[...]), shape)
-    shift = jnp.broadcast_to(column(shift_ref[...].astype(F32)), shape).astype(jnp.int32)
-    reach = lax.broadcasted_iota(jnp.int32, shape, 1) + shift
-    first = jnp.where(reach < gates, 1.0 - fraction, 0.0)
-    second = jnp.where(reach + 1 < gates, fraction, 0.0)
+    spare = jnp.zeros((6, count), F32)
+    turned[...] = jnp.transpose(jnp.concatenate([fraction_ref[...], shift_ref[...].astype(F32), spare], 0))
     copies[0].wait()
-    for part in range(2):
-        moved = pulses_ref[part].astype(F32)
-        bit = 1
-        while bit < SHIFT_MAX:
-            moved = jnp.where((shift & bit) != 0, pltpu.roll(moved, gates - bit, 1), moved)
-            bit *= 2
-        out_ref[part] = (first * moved + second * pltpu.roll(moved, gates - 1, 1)).astype(BF16)
+    rows = 64
+    lane = lax.broadcasted_iota(jnp.int32, (rows, 128), 1)
+    pick = functools.partial(jnp.take_along_axis, axis=1, mode="promise_in_bounds")
+    for r in range(0, count, rows):
+        fraction = jnp.broadcast_to(turned[r : r + rows, 0:1], (rows, 128))
+        shift = jnp.broadcast_to(turned[r : r + rows, 1:2], (rows, 128)).astype(jnp.int32)
+        terms = [(by, (lane + by) & 127, part) for by, part in ((shift, 1.0 - fraction), (shift + 1, fraction))]
+        for part in range(2):
+            tiles = [pulses_ref[part, r : r + rows, at : at + 128].astype(F32) for at in range(0, gates, 128)]
+            total = [0.0] * len(tiles)
+            for by, at, scale in terms:
+                inside = lane + by < 128
+                moved = [pick(t, at) for t in tiles] + [0.0]
+                for j in range(len(tiles)):
+                    total[j] += scale * jnp.where(inside, moved[j], moved[j + 1])
+            for j, value in enumerate(total):
+                out_ref[part, r : r + rows, j * 128 : (j + 1) * 128] = value.astype(BF16)
 
 
 def poly(coefs, z):
@@ -84,37 +86,39 @@
     return total
 
 
-def spread(refs, cols):
-    for at, ref in enumerate(refs):
-        waves = ref.shape[1]
-        start, end = ref[0:1, :], ref[1:2, :]
-        center = jnp.floor((start + end) * 0.5)
-        scale = lax.rsqrt(end - start)
-        stack = jnp.concatenate([center, start, end, ref[2:3, :], ref[3:4, :], scale, scale, scale], 0)
-        turned = jnp.transpose(stack)
-        for k in range(6):
-            cols[k, at * waves : (at + 1) * waves, :] = jnp.broadcast_to(turned[:, k : k + 1], (waves, 128))
-
-
-def weigh(cols, base, pulse_count, rows, put):
-    total_rows = cols.shape[1]
+def spread(ref, reach, cols):
+    waves = ref.shape[1]
+    start, end = ref[0:1, :], ref[1:2, :]
+    center = jnp.floor((start + end) * 0.5)
+    linear = ref[2:3, :] * (1.0 / (math.pi * reach))
+    square = ref[3:4, :] * (1.0 / (math.pi * reach * reach))
+    scale = lax.rsqrt(end - start)
+    turned = jnp.transpose(jnp.concatenate([center, start, end, linear, square, scale, scale, scale], 0))
+    for k in range(6):
+        cols[k] = jnp.broadcast_to(turned[:, k : k + 1], (waves, 128))
+
+
+def weigh(cols, base, pulse_count, put, rows=16, unroll=2):
+    lanes = range(0, pulse_count, 128)
+    at = lax.broadcasted_iota(jnp.int32, (rows, 128), 1) + base
+    pulses = [(at + lane).astype(F32) for lane in lanes]
 
     def step(k, carry):
         r = pl.multiple_of(k * rows, rows)
-        center, start, end, doppler, chirp, scale = (cols[j, pl.ds(r, rows), :] for j in range(6))
-        for lane in range(0, pulse_count, 128):
-            pulse = (lax.broadcasted_iota(jnp.int32, (rows, 128), 1) + (base + lane)).astype(F32)
-            relative = (pulse - center) * (1.0 / (REACH * pulse_count))
-            phase = chirp * relative * relative + doppler * relative
-            turns = jnp.round(phase * INV_PI)
-            rest = (phase - turns * PI_HI) - turns * PI_LO
-            square = rest * rest
-            signed = jnp.where((turns.astype(jnp.int32) & 1) != 0, -scale, scale)
+        center, start, end, linear, square, scale = (cols[j, pl.ds(r, rows), :] for j in range(6))
+        minus = -scale
+        for lane, pulse in zip(lanes, pulses):
+            u = pulse - center
+            halves = (square * u + linear) * u
+            near = jnp.round(halves)
+            rest = halves - near
+            z = rest * rest
+            signed = jnp.where((near.astype(jnp.int32) & 1) != 0, minus, scale)
             signed = jnp.where((pulse >= start) & (pulse < end), signed, 0.0)
-            put(r, lane, signed * poly(COS, square), signed * rest * poly(SIN, square))
+            put(r, lane, signed * poly(COS, z), signed * rest * poly(SIN, z))
         return carry
 
-    lax.fori_loop(0, total_rows // rows, step, 0, unroll=2)
+    lax.fori_loop(0, cols.shape[1] // rows, step, 0, unroll=unroll)
 
 
 def partner(device, by, odd):
@@ -136,9 +140,9 @@
     device = lax.axis_index("seg")
     count = own_ref.shape[1]
     mate = device + 1 - 2 * (device % 2)
-    spread((target_ref,), cols)
-    weigh(cols, device * count, count, 16, into(w, 0))
-    weigh(cols, mate * count, count, 16, into(w, count))
+    spread(target_ref, REACH * count, cols)
+    weigh(cols, device * count, count, into(w, 0))
+    weigh(cols, mate * count, count, into(w, count))
     re, im = w[0], w[1]
     a = dot(re[:, :count], own_ref[0]) + dot(re[:, count:], mate_ref[0])
     b = dot(im[:, :count], own_ref[1]) + dot(im[:, count:], mate_ref[1])
@@ -148,34 +152,32 @@
     out_ref[1] = (c + d).astype(BF16)
 
 
-def weights_kernel(params_ref, other_ref, own_ref, partial_ref, weights_ref, cols, own_w):
+def weights_kernel(params_ref, own_ref, partial_ref, weights_ref, cols, own_w):
     device = lax.axis_index("seg")
     count = own_ref.shape[1]
-    spread((params_ref, other_ref), cols)
-    weigh(cols, device * count, count, 16, into(own_w, 0))
+    spread(params_ref, REACH * count, cols)
+    weigh(cols, device * count, count, into(own_w, 0))
     partial_ref[0] = dot(own_w[0], own_ref[0]) - dot(own_w[1], own_ref[1])
     partial_ref[1] = dot(own_w[0], own_ref[1]) + dot(own_w[1], own_ref[0])
     for slot, (by, odd) in enumerate(SLOTS):
-        weigh(cols, partner(device, by, odd) * count, count, 16, into(weights_ref, slot * count))
-
-
-def focus_kernel(partial_ref, weights_ref, *refs):
+        weigh(cols, partner(device, by, odd) * count, count, into(weights_ref, slot * count))
+
+
+def focus_kernel(partial_ref, weights_ref, partial2_ref, weights2_ref, *refs):
     blocks, (keep_ref, message_ref) = refs[:-2], refs[-2:]
     count = blocks[0].shape[1]
-    waves = keep_ref.shape[1]
-    re, im = partial_ref[0], partial_ref[1]
-    minus = jnp.zeros_like(re)
-    for slot, ref in enumerate(blocks):
-        w_re = weights_ref[0, :, slot * count : (slot + 1) * count]
-        w_im = weights_ref[1, :, slot * count : (slot + 1) * count]
-        re += dot(w_re, ref[0])
-        minus += dot(w_im, ref[1])
-        im += dot(w_re, ref[1])
-        im += dot(w_im, ref[0])
-    re = re - minus
-    for part, value in enumerate((re, im)):
-        keep_ref[part] = value[:waves]
-        message_ref[part] = value[waves:].astype(BF16)
+    for p_ref, w_ref, out in ((partial2_ref, weights2_ref, message_ref), (partial_ref, weights_ref, keep_ref)):
+        re, im = p_ref[0], p_ref[1]
+        minus = jnp.zeros_like(re)
+        for slot, ref in enumerate(blocks):
+            w_re = w_ref[0, :, slot * count : (slot + 1) * count]
+            w_im = w_ref[1, :, slot * count : (slot + 1) * count]
+            re += dot(w_re, ref[0])
+            minus += dot(w_im, ref[1])
+            im += dot(w_re, ref[1])
+            im += dot(w_im, ref[0])
+        out[0] = (re - minus).astype(out.dtype)
+        out[1] = im.astype(out.dtype)
 
 
 def total_of(device, devices, rows, keep_ref, got_ref, lent_ref):
@@ -265,7 +267,7 @@
         out_shape=(shape((2, count, gates), BF16), shape((8, waves), F32)),
         in_specs=[hbm] * 7,
         out_specs=(vmem, vmem),
-        scratch_shapes=[pltpu.VMEM(a.shape, a.dtype) for a in inputs] + [pltpu.SemaphoreType.DMA((7,))],
+        scratch_shapes=[pltpu.VMEM(a.shape, a.dtype) for a in inputs] + [pltpu.VMEM((count, 8), F32), pltpu.SemaphoreType.DMA((7,))],
         compiler_params=PARAMS,
         name="migrate",
     )(*(pltpu.with_memory_space_constraint(a, pltpu.HBM) for a in inputs))
@@ -283,23 +285,24 @@
         name="lend",
     )(target, migrated, mate)
     lent = swap(lending, *DIAGONAL)
-    partial, weights = pl.pallas_call(
+    weigh_call = lambda: pl.pallas_call(
         weights_kernel,
-        out_shape=(shape((2, 2 * waves, gates), F32), shape((2, 2 * waves, len(SLOTS) * count), BF16)),
-        in_specs=[vmem] * 3,
+        out_shape=(shape((2, waves, gates), F32), shape((2, waves, len(SLOTS) * count), BF16)),
+        in_specs=[vmem] * 2,
         out_specs=(vmem, vmem),
-        scratch_shapes=[pltpu.VMEM((6, 2 * waves, 128), F32), pltpu.VMEM((2, 2 * waves, count), BF16)],
-        compiler_params=PARAMS,
-        name="weights",
-    )(params, other, migrated)
+        scratch_shapes=[pltpu.VMEM((6, waves, 128), F32), pltpu.VMEM((2, waves, count), BF16)],
+        compiler_params=PARAMS,
+    )
+    partial, weights = weigh_call()(params, migrated)
+    partial2, weights2 = weigh_call()(other, migrated)
     keep, message = pl.pallas_call(
         focus_kernel,
         out_shape=(shape((2, waves, gates), F32), shape((2, waves, gates), BF16)),
-        in_specs=[vmem] * (2 + len(blocks)),
+        in_specs=[vmem] * (4 + len(blocks)),
         out_specs=(vmem, vmem),
         compiler_params=PARAMS,
         name="focus",
-    )(partial, weights, *blocks)
+    )(partial, weights, partial2, weights2, *blocks)
     got = swap(message, 1, 0)
     near, far = pl.pallas_call(
         functools.partial(ends_kernel, devices),

time: 25.7 us -> 25.3 us (0.984)
  Pallas kernels: 7.59 us -> 7.22 us
    pallas_call x1, Pallas kernels: 1.99 us -> 1.68 us  [shards(): pl.pallas_call(migrate_kernel, out_shape=(shape((2, count, gates), BF16),...]
    pallas_call x1 -> x2, Pallas kernels: 2.52 us -> 2.54 us  [the longest x1 1.27 us: shards(): partial2, weights2 = weigh_call()(other, migrated)]
where the time goes in v3:
time: 25.3 us; the launch traced here: 25.1 us
  waiting for transfers between devices  11 us (43%)
  Pallas kernels  7.22 us (29%)
  starting transfers between devices  6.23 us (25%)
  between operations  0.71 us (3%)
    ppermute x9, waiting for transfers between devices, swap(): lax.ppermute(array, 'seg', [(i, neighbour(i, by, odd, devices)) for i in...  8.16 us
    ppermute x9, starting transfers between devices, swap(): lax.ppermute(array, 'seg', [(i, neighbour(i, by, odd, devices)) for i in...  5.77 us
    ppermute x1, waiting for transfers between devices, beside(): return lax.ppermute(array, ('arcs', 'seg'), pairs)  2.79 us
    pallas_call x1, Pallas kernels, shards(): pl.pallas_call(migrate_kernel, out_shape=(shape((2, count, gates), BF16),...  1.68 us
    pallas_call x1, Pallas kernels, shards(): partial2, weights2 = weigh_call()(other, migrated)  1.27 us
    pallas_call x1, Pallas kernels, shards(): partial, weights = weigh_call()(params, migrated)  1.27 us
    pallas_call x1, Pallas kernels, shards(): pl.pallas_call(lend_kernel, out_shape=shape((2, waves, gates), BF16), in_...  0.96 us
    pallas_call x1, Pallas kernels, shards(): pl.pallas_call(functools.partial(power_kernel, devices), out_shape=(shape...  0.78 us
  transfers between devices with their start and end apart: 10, of which 4 were waited for; matrix products, arithmetic and copies ran while one was open for 0% of the time, Pallas kernels for 19%

profile of v3, /device:TPU:8, one launch (start us, length us, event | category | flops | bytes accessed | tf_op | source)
XLA Modules:
  0.0 25.1 jit_solution(7219503652080307192)
XLA Ops:
  0.6 1.7 %migrate.1 = (bf16[2,256,256]{2,1,0:T(8,128)(2,1)S(1)}, f32[8,128]{1,0:T(8,128)S(1)}) custom-call(bf16[2,256,256]{2,1,0:T(8,128)(2,1)} %refs_0_.1, f32[1,256]{1,0:T(1,128)} %bitcast.6, s32[1,256]{1,0:T(1,128)} %bitcast.7, s32[1,128]{1,0:T(1,128)} %bitcast.8, s32[1,128]{1,0:T(1,128)} %bitcast.9, f32[1,128]{1,0:T(1,128)} %bitcast.10, f32[1,128]{1,0:T(1,128)} %bitcast.11), custom_call_target="tpu_custom_call" | custom-call | tf_op jit(solution)/shard_map/migrate/pallas_call | solution.py:265
  2.3 0.1 collective-permute-start.6
  2.4 1.6 %collective-permute-start.3 = (bf16[2,256,256]{2,1,0:T(8,128)(2,1)S(1)}, bf16[2,256,256]{2,1,0:T(8,128)(2,1)S(1)}, u32[]{:S(2)}, u32[]{:S(2)}) collective-permute-start(bf16[2,256,256]{2,1,0:T(8,128)(2,1)S(1)} %get-tuple-element.16.own_ref), channel_id=1, source_target_pairs={{0,1},{1,0},{2,3},{3,2},{4,8},{5,9},{6,10},{7,11},{8,4},{9,5},{10,... | collective-permute-start | bytes 786440 | tf_op jit(solution)/shard_map/ppermute | solution.py:32
  4.0 0.0 collective-permute-start.2
  4.0 1.5 %collective-permute-start.1 = (bf16[2,256,256]{2,1,0:T(8,128)(2,1)S(1)}, bf16[2,256,256]{2,1,0:T(8,128)(2,1)S(1)}, u32[]{:S(2)}, u32[]{:S(2)}) collective-permute-start(bf16[2,256,256]{2,1,0:T(8,128)(2,1)S(1)} %get-tuple-element.16.own_ref), channel_id=1, source_target_pairs={{0,2},{1,3},{2,0},{3,1},{4,6},{5,7},{6,4},{7,5},{8,10},{9,11},{10,... | collective-permute-start | bytes 786440 | tf_op jit(solution)/shard_map/ppermute | solution.py:32
  5.5 0.0 collective-permute-start
  5.5 1.2 %collective-permute-done.params_ref = f32[8,128]{1,0:T(8,128)S(1)} collective-permute-done((f32[8,128]{1,0:T(8,128)S(1)}, f32[8,128]{1,0:T(8,128)S(1)}, u32[]{:S(2)}, u32[]{:S(2)}) %collective-permute-start) | collective-permute-done | bytes 4128 | tf_op jit(solution)/shard_map/ppermute | solution.py:32
  6.7 2.0 %collective-permute-start.5 = (f32[8,128]{1,0:T(8,128)S(1)}, f32[8,128]{1,0:T(8,128)S(1)}, u32[]{:S(2)}, u32[]{:S(2)}) collective-permute-start(f32[8,128]{1,0:T(8,128)S(1)} %get-tuple-element.15.params_ref), channel_id=1, source_target_pairs={{0,1},{1,0},{2,4},{3,5},{4,2},{5,3},{6,8},{7,9},{8,6},{9,7},{10,12... | collective-permute-start | bytes 12296 | tf_op jit(solution)/shard_map/ppermute | solution.py:32
  8.7 1.3 %shard_map.86 = (f32[2,128,256]{2,1,0:T(8,128)S(1)}, bf16[2,128,768]{2,1,0:T(8,128)(2,1)S(1)}) custom-call(f32[8,128]{1,0:T(8,128)S(1)} %get-tuple-element.15.params_ref, bf16[2,256,256]{2,1,0:T(8,128)(2,1)S(1)} %get-tuple-element.16.own_ref), custom_call_target="tpu_custom_call" | custom-call | tf_op jit(solution)/shard_map/pallas_call | solution.py:296
  10.0 1.3 %shard_map.87 = (f32[2,128,256]{2,1,0:T(8,128)S(1)}, bf16[2,128,768]{2,1,0:T(8,128)(2,1)S(1)}) custom-call(f32[8,128]{1,0:T(8,128)S(1)} %collective-permute-done.params_ref, bf16[2,256,256]{2,1,0:T(8,128)(2,1)S(1)} %get-tuple-element.16.own_ref), custom_call_target="tpu_custom_call" | custom-call | tf_op jit(solution)/shard_map/pallas_call | solution.py:297
  11.3 2.2 %collective-permute-done.5.target_ref = f32[8,128]{1,0:T(8,128)S(1)} collective-permute-done((f32[8,128]{1,0:T(8,128)S(1)}, f32[8,128]{1,0:T(8,128)S(1)}, u32[]{:S(2)}, u32[]{:S(2)}) %collective-permute-start.5) | collective-permute-done | bytes 4128 | tf_op jit(solution)/shard_map/ppermute | solution.py:32
  13.4 0.0 collective-permute-done.6.mate_ref
  13.4 1.0 %lend.1 = bf16[2,128,256]{2,1,0:T(8,128)(2,1)S(1)} custom-call(f32[8,128]{1,0:T(8,128)S(1)} %collective-permute-done.5.target_ref, bf16[2,256,256]{2,1,0:T(8,128)(2,1)S(1)} %get-tuple-element.16.own_ref, bf16[2,256,256]{2,1,0:T(8,128)(2,1)S(1)} %collective-permute-done.6.mate_ref), custom_call_target="tpu_custom_call" | custom-call | tf_op jit(solution)/shard_map/lend/pallas_call | solution.py:278
  14.4 0.4 %collective-permute-start.7 = (bf16[2,128,256]{2,1,0:T(8,128)(2,1)S(1)}, bf16[2,128,256]{2,1,0:T(8,128)(2,1)S(1)}, u32[]{:S(2)}, u32[]{:S(2)}) collective-permute-start(bf16[2,128,256]{2,1,0:T(8,128)(2,1)S(1)} %lend.1), channel_id=1, source_target_pairs={{0,1},{1,0},{2,4},{3,5},{4,2},{5,3},{6,8},{7,9},{8,6},{9,7},{10,12... | collective-permute-start | bytes 393224 | tf_op jit(solution)/shard_map/ppermute | solution.py:32
  14.8 0.0 collective-permute-done.3.refs_2_
  14.8 0.0 collective-permute-done.2.refs_1_
  14.8 0.0 collective-permute-done.1.refs_0_
  14.8 0.6 %focus.1 = (f32[2,128,256]{2,1,0:T(8,128)S(1)}, bf16[2,128,256]{2,1,0:T(8,128)(2,1)S(1)}) custom-call(f32[2,128,256]{2,1,0:T(8,128)S(1)} %get-tuple-element.17.partial_ref, bf16[2,128,768]{2,1,0:T(8,128)(2,1)S(1)} %get-tuple-element.18.weights_ref, f32[2,128,256]{2,1,0:T(8,128)S(1)} %get-tuple-element.19.partial2_ref, ...), custom_call_target="tpu_custom_call" | custom-call | tf_op jit(solution)/shard_map/focus/pallas_call | solution.py:298
  15.4 0.1 collective-permute-start.4
  15.5 4.8 %collective-permute-done.7.lent_ref = bf16[2,128,256]{2,1,0:T(8,128)(2,1)S(1)} collective-permute-done((bf16[2,128,256]{2,1,0:T(8,128)(2,1)S(1)}, bf16[2,128,256]{2,1,0:T(8,128)(2,1)S(1)}, u32[]{:S(2)}, u32[]{:S(2)}) %collective-permute-start.7) | collective-permute-done | bytes 131104 | tf_op jit(solution)/shard_map/ppermute | solution.py:32
  20.3 0.0 collective-permute-done.4.got_ref
  20.4 0.1 collective-permute-start.8
  20.4 0.5 %collective-permute-start.9 = (f32[8,256]{1,0:T(8,128)S(1)}, f32[8,256]{1,0:T(8,128)S(1)}, u32[]{:S(2)}, u32[]{:S(2)}) collective-permute-start(f32[8,256]{1,0:T(8,128)S(1)} %get-tuple-element.27), channel_id=1, source_target_pairs={{0,16},{1,2},{2,1},{3,4},{4,3},{5,6},{6,5},{7,8},{8,7},{9,10},{10,... | collective-permute-start | bytes 24584 | tf_op jit(solution)/shard_map/ppermute | solution.py:43
  20.9 0.8 %power.1 = (bf16[2,128,256]{2,1,0:T(8,128)(2,1)}, f32[128,256]{1,0:T(8,128)}, f32[16,256]{1,0:T(8,128)S(1)}) custom-call(f32[2,128,256]{2,1,0:T(8,128)S(1)} %get-tuple-element.21.keep_ref, bf16[2,128,256]{2,1,0:T(8,128)(2,1)S(1)} %collective-permute-done.4.got_ref, bf16[2,128,256]{2,1,0:T(8,128)(2,1)S(1)} %collective-permute-done.7.lent_ref), custom_call_target="tpu_custom_call" | custom-call | tf_op jit(solution)/shard_map/power/pallas_call | solution.py:317
  21.7 0.0 collective-permute-done.8.near_ref
  21.7 2.8 %collective-permute-done.9.far_ref = f32[8,256]{1,0:T(8,128)S(1)} collective-permute-done((f32[8,256]{1,0:T(8,128)S(1)}, f32[8,256]{1,0:T(8,128)S(1)}, u32[]{:S(2)}, u32[]{:S(2)}) %collective-permute-start.9) | collective-permute-done | bytes 8224 | tf_op jit(solution)/shard_map/ppermute | solution.py:43
  24.5 0.6 %edge.1 = f32[128,256]{1,0:T(8,128)} custom-call(f32[128,256]{1,0:T(8,128)} %get-tuple-element.24.looked_ref, f32[16,256]{1,0:T(8,128)S(1)} %get-tuple-element.25.ends_ref, f32[8,256]{1,0:T(8,128)S(1)} %collective-permute-done.8.near_ref, f32[8,256]{1,0:T(8,128)S(1)} %collective-permute-done.9.far_ref), custom_call_target="tpu_custom_call", output_to_operand_aliasing={{}: (0, {})} | custom-call | tf_op jit(solution)/shard_map/edge/pallas_call | solution.py:326
  (1 shorter events, 0.0 us)
Async XLA Ops:
  2.3 11.1 %collective-permute-start.6 = (bf16[2,256,256]{2,1,0:T(8,128)(2,1)S(1)}, bf16[2,256,256]{2,1,0:T(8,128)(2,1)S(1)}, u32[]{:S(2)}, u32[]{:S(2)}) collective-permute-start(bf16[2,256,256]{2,1,0:T(8,128)(2,1)S(1)} %get-tuple-element.16.own_ref), channel_id=1, source_target_pairs={{0,1},{1,0},{2,3},{3,2},{4,5},{5,4},{6,7},{7,6},{8,9},{9,8},{10,11... | collective-permute-start | bytes 786440 | tf_op jit(solution)/shard_map/ppermute | solution.py:32
  2.4 12.4 %collective-permute-start.3 = (bf16[2,256,256]{2,1,0:T(8,128)(2,1)S(1)}, bf16[2,256,256]{2,1,0:T(8,128)(2,1)S(1)}, u32[]{:S(2)}, u32[]{:S(2)}) collective-permute-start(bf16[2,256,256]{2,1,0:T(8,128)(2,1)S(1)} %get-tuple-element.16.own_ref), channel_id=1, source_target_pairs={{0,1},{1,0},{2,3},{3,2},{4,8},{5,9},{6,10},{7,11},{8,4},{9,5},{10,... | collective-permute-start | bytes 786440 | tf_op jit(solution)/shard_map/ppermute | solution.py:32
  4.0 10.8 %collective-permute-start.2 = (bf16[2,256,256]{2,1,0:T(8,128)(2,1)S(1)}, bf16[2,256,256]{2,1,0:T(8,128)(2,1)S(1)}, u32[]{:S(2)}, u32[]{:S(2)}) collective-permute-start(bf16[2,256,256]{2,1,0:T(8,128)(2,1)S(1)} %get-tuple-element.16.own_ref), channel_id=1, source_target_pairs={{0,4},{1,5},{2,6},{3,7},{4,0},{5,1},{6,2},{7,3},{8,12},{9,13},{10,... | collective-permute-start | bytes 786440 | tf_op jit(solution)/shard_map/ppermute | solution.py:32
  4.0 10.8 %collective-permute-start.1 = (bf16[2,256,256]{2,1,0:T(8,128)(2,1)S(1)}, bf16[2,256,256]{2,1,0:T(8,128)(2,1)S(1)}, u32[]{:S(2)}, u32[]{:S(2)}) collective-permute-start(bf16[2,256,256]{2,1,0:T(8,128)(2,1)S(1)} %get-tuple-element.16.own_ref), channel_id=1, source_target_pairs={{0,2},{1,3},{2,0},{3,1},{4,6},{5,7},{6,4},{7,5},{8,10},{9,11},{10,... | collective-permute-start | bytes 786440 | tf_op jit(solution)/shard_map/ppermute | solution.py:32
  5.5 1.2 %collective-permute-start = (f32[8,128]{1,0:T(8,128)S(1)}, f32[8,128]{1,0:T(8,128)S(1)}, u32[]{:S(2)}, u32[]{:S(2)}) collective-permute-start(f32[8,128]{1,0:T(8,128)S(1)} %get-tuple-element.15.params_ref), channel_id=1, source_target_pairs={{0,1},{1,0},{2,3},{3,2},{4,5},{5,4},{6,7},{7,6},{8,9},{9,8},{10,11... | collective-permute-start | bytes 12296 | tf_op jit(solution)/shard_map/ppermute | solution.py:32
  6.7 6.7 %collective-permute-start.5 = (f32[8,128]{1,0:T(8,128)S(1)}, f32[8,128]{1,0:T(8,128)S(1)}, u32[]{:S(2)}, u32[]{:S(2)}) collective-permute-start(f32[8,128]{1,0:T(8,128)S(1)} %get-tuple-element.15.params_ref), channel_id=1, source_target_pairs={{0,1},{1,0},{2,4},{3,5},{4,2},{5,3},{6,8},{7,9},{8,6},{9,7},{10,12... | collective-permute-start | bytes 12296 | tf_op jit(solution)/shard_map/ppermute | solution.py:32
  14.4 5.9 %collective-permute-start.7 = (bf16[2,128,256]{2,1,0:T(8,128)(2,1)S(1)}, bf16[2,128,256]{2,1,0:T(8,128)(2,1)S(1)}, u32[]{:S(2)}, u32[]{:S(2)}) collective-permute-start(bf16[2,128,256]{2,1,0:T(8,128)(2,1)S(1)} %lend.1), channel_id=1, source_target_pairs={{0,1},{1,0},{2,4},{3,5},{4,2},{5,3},{6,8},{7,9},{8,6},{9,7},{10,12... | collective-permute-start | bytes 393224 | tf_op jit(solution)/shard_map/ppermute | solution.py:32
  15.4 4.9 %collective-permute-start.4 = (bf16[2,128,256]{2,1,0:T(8,128)(2,1)S(1)}, bf16[2,128,256]{2,1,0:T(8,128)(2,1)S(1)}, u32[]{:S(2)}, u32[]{:S(2)}) collective-permute-start(bf16[2,128,256]{2,1,0:T(8,128)(2,1)S(1)} %get-tuple-element.22), channel_id=1, source_target_pairs={{0,1},{1,0},{2,3},{3,2},{4,5},{5,4},{6,7},{7,6},{8,9},{9,8},{10,11... | collective-permute-start | bytes 393224 | tf_op jit(solution)/shard_map/ppermute | solution.py:32
  20.4 1.3 %collective-permute-start.8 = (f32[8,256]{1,0:T(8,128)S(1)}, f32[8,256]{1,0:T(8,128)S(1)}, u32[]{:S(2)}, u32[]{:S(2)}) collective-permute-start(f32[8,256]{1,0:T(8,128)S(1)} %get-tuple-element.26), channel_id=1, source_target_pairs={{0,1},{1,0},{2,3},{3,2},{4,5},{5,4},{6,7},{7,6},{8,9},{9,8},{10,11... | collective-permute-start | bytes 24584 | tf_op jit(solution)/shard_map/ppermute | solution.py:32
  20.4 4.0 %collective-permute-start.9 = (f32[8,256]{1,0:T(8,128)S(1)}, f32[8,256]{1,0:T(8,128)S(1)}, u32[]{:S(2)}, u32[]{:S(2)}) collective-permute-start(f32[8,256]{1,0:T(8,128)S(1)} %get-tuple-element.27), channel_id=1, source_target_pairs={{0,16},{1,2},{2,1},{3,4},{4,3},{5,6},{6,5},{7,8},{8,7},{9,10},{10,... | collective-permute-start | bytes 24584 | tf_op jit(solution)/shard_map/ppermute | solution.py:43

commit v4 on v3

--- a/solution.py
+++ b/solution.py
@@ -98,7 +98,7 @@
         cols[k] = jnp.broadcast_to(turned[:, k : k + 1], (waves, 128))
 
 
-def weigh(cols, base, pulse_count, put, rows=16, unroll=2):
+def weigh(cols, base, pulse_count, put, rows=16, unroll=8):
     lanes = range(0, pulse_count, 128)
     at = lax.broadcasted_iota(jnp.int32, (rows, 128), 1) + base
     pulses = [(at + lane).astype(F32) for lane in lanes]
@@ -136,20 +136,26 @@
     return put
 
 
-def lend_kernel(target_ref, own_ref, mate_ref, out_ref, cols, w):
+def lend_weights_kernel(target_ref, out_ref, cols):
     device = lax.axis_index("seg")
-    count = own_ref.shape[1]
+    count = out_ref.shape[2] // 2
     mate = device + 1 - 2 * (device % 2)
     spread(target_ref, REACH * count, cols)
-    weigh(cols, device * count, count, into(w, 0))
-    weigh(cols, mate * count, count, into(w, count))
-    re, im = w[0], w[1]
+    weigh(cols, device * count, count, into(out_ref, 0))
+    weigh(cols, mate * count, count, into(out_ref, count))
+
+
+def lend_kernel(w_ref, own_ref, mate_ref, out_ref, ends_ref):
+    count = own_ref.shape[1]
+    waves = out_ref.shape[1]
+    re, im = w_ref[0], w_ref[1]
     a = dot(re[:, :count], own_ref[0]) + dot(re[:, count:], mate_ref[0])
     b = dot(im[:, :count], own_ref[1]) + dot(im[:, count:], mate_ref[1])
     c = dot(re[:, :count], own_ref[1]) + dot(re[:, count:], mate_ref[1])
     d = dot(im[:, :count], own_ref[0]) + dot(im[:, count:], mate_ref[0])
-    out_ref[0] = (a - b).astype(BF16)
-    out_ref[1] = (c + d).astype(BF16)
+    for part, value in enumerate((a - b, c + d)):
+        out_ref[part] = value.astype(BF16)
+        ends_ref[part] = jnp.concatenate([value[:LOOK], value[waves - LOOK :]], 0).astype(BF16)
 
 
 def weights_kernel(params_ref, own_ref, partial_ref, weights_ref, cols, own_w):
@@ -163,46 +169,46 @@
         weigh(cols, partner(device, by, odd) * count, count, into(weights_ref, slot * count))
 
 
-def focus_kernel(partial_ref, weights_ref, partial2_ref, weights2_ref, *refs):
-    blocks, (keep_ref, message_ref) = refs[:-2], refs[-2:]
+def focus_kernel(partial_ref, weights_ref, *refs):
+    blocks, out_ref = refs[:-1], refs[-1]
     count = blocks[0].shape[1]
-    for p_ref, w_ref, out in ((partial2_ref, weights2_ref, message_ref), (partial_ref, weights_ref, keep_ref)):
-        re, im = p_ref[0], p_ref[1]
-        minus = jnp.zeros_like(re)
-        for slot, ref in enumerate(blocks):
-            w_re = w_ref[0, :, slot * count : (slot + 1) * count]
-            w_im = w_ref[1, :, slot * count : (slot + 1) * count]
-            re += dot(w_re, ref[0])
-            minus += dot(w_im, ref[1])
-            im += dot(w_re, ref[1])
-            im += dot(w_im, ref[0])
-        out[0] = (re - minus).astype(out.dtype)
-        out[1] = im.astype(out.dtype)
-
-
-def total_of(device, devices, rows, keep_ref, got_ref, lent_ref):
-    by_chip = partner(device, *DIAGONAL)
+    re, im = partial_ref[0], partial_ref[1]
+    minus = jnp.zeros_like(re)
+    for slot, ref in enumerate(blocks):
+        w_re = weights_ref[0, :, slot * count : (slot + 1) * count]
+        w_im = weights_ref[1, :, slot * count : (slot + 1) * count]
+        re += dot(w_re, ref[0])
+        minus += dot(w_im, ref[1])
+        im += dot(w_re, ref[1])
+        im += dot(w_im, ref[0])
+    out_ref[0] = (re - minus).astype(out_ref.dtype)
+    out_ref[1] = im.astype(out_ref.dtype)
+
+
+def total_of(devices, keep, got, lent):
+    by_chip = partner(lax.axis_index("seg"), *DIAGONAL)
     known = (by_chip >= 0) & (by_chip < devices)
-    lent = jnp.where(known, lent_ref[:, rows].astype(F32), 0.0)
-    return keep_ref[:, rows] + got_ref[:, rows].astype(F32) + lent
+    return keep + got.astype(F32) + jnp.where(known, lent.astype(F32), 0.0)
 
 
 def ends_kernel(devices, keep_ref, got_ref, lent_ref, near_ref, far_ref):
-    device = lax.axis_index("seg")
     waves = keep_ref.shape[1]
-    powers = []
-    for rows in (slice(0, 2 * LOOK), slice(waves - 2 * LOOK, waves)):
-        total = total_of(device, devices, rows, keep_ref, got_ref, lent_ref)
-        powers.append(total[0] * total[0] + total[1] * total[1])
-    initial, last = powers[0][:LOOK], powers[1][LOOK:]
-    core = device % 2
+    pair = slice(0, 2 * LOOK), slice(waves - 2 * LOOK, waves)
+    keep, got = (
+        jnp.concatenate([ref[:, pair[0]].astype(F32)[:, :LOOK], ref[:, pair[1]].astype(F32)[:, LOOK:]], 1)
+        for ref in (keep_ref, got_ref)
+    )
+    total = total_of(devices, keep, got, lent_ref[...])
+    power = total[0] * total[0] + total[1] * total[1]
+    initial, last = power[:LOOK], power[LOOK:]
+    core = lax.axis_index("seg") % 2
     near_ref[...] = jnp.where(core == 0, last, initial)
     far_ref[...] = jnp.where(core == 0, initial, last)
 
 
 def power_kernel(devices, keep_ref, got_ref, lent_ref, focused_ref, looked_ref, ends_ref, ext):
     waves = focused_ref.shape[1]
-    total = total_of(lax.axis_index("seg"), devices, slice(0, waves), keep_ref, got_ref, lent_ref)
+    total = total_of(devices, keep_ref[...], got_ref[...], lent_ref[...])
     focused_ref[...] = total.astype(BF16)
     ext[:LOOK] = jnp.zeros((LOOK, ext.shape[1]), F32)
     ext[LOOK : LOOK + waves] = total[0] * total[0] + total[1] * total[1]
@@ -275,15 +281,24 @@
     target = swap(params, *DIAGONAL)
     mate = swap(migrated, 1, 0)
     other = swap(params, 1, 0)
-    lending = pl.pallas_call(
+    lend_weights = pl.pallas_call(
+        lend_weights_kernel,
+        out_shape=shape((2, waves, 2 * count), BF16),
+        in_specs=[vmem],
+        out_specs=vmem,
+        scratch_shapes=[pltpu.VMEM((6, waves, 128), F32)],
+        compiler_params=PARAMS,
+        name="lend_weights",
+    )(target)
+    lending, lending_ends = pl.pallas_call(
         lend_kernel,
-        out_shape=shape((2, waves, gates), BF16),
+        out_shape=(shape((2, waves, gates), BF16), shape((2, 2 * LOOK, gates), BF16)),
         in_specs=[vmem] * 3,
-        out_specs=vmem,
-        scratch_shapes=[pltpu.VMEM((6, waves, 128), F32), pltpu.VMEM((2, waves, 2 * count), BF16)],
+        out_specs=(vmem, vmem),
         compiler_params=PARAMS,
         name="lend",
-    )(target, migrated, mate)
+    )(lend_weights, migrated, mate)
+    lent_ends = swap(lending_ends, *DIAGONAL)
     lent = swap(lending, *DIAGONAL)
     weigh_call = lambda: pl.pallas_call(
         weights_kernel,
@@ -295,14 +310,15 @@
     )
     partial, weights = weigh_call()(params, migrated)
     partial2, weights2 = weigh_call()(other, migrated)
-    keep, message = pl.pallas_call(
+    focus_call = lambda dtype: pl.pallas_call(
         focus_kernel,
-        out_shape=(shape((2, waves, gates), F32), shape((2, waves, gates), BF16)),
-        in_specs=[vmem] * (4 + len(blocks)),
-        out_specs=(vmem, vmem),
-        compiler_params=PARAMS,
-        name="focus",
-    )(partial, weights, partial2, weights2, *blocks)
+        out_shape=shape((2, waves, gates), dtype),
+        in_specs=[vmem] * (2 + len(blocks)),
+        out_specs=vmem,
+        compiler_params=PARAMS,
+    )
+    message = focus_call(BF16)(partial2, weights2, *blocks)
+    keep = focus_call(F32)(partial, weights, *blocks)
     got = swap(message, 1, 0)
     near, far = pl.pallas_call(
         functools.partial(ends_kernel, devices),
@@ -311,7 +327,7 @@
         out_specs=(vmem, vmem),
         compiler_params=PARAMS,
         name="ends",
-    )(keep, got, lent)
+    )(keep, got, lent_ends)
     far = beside(far)
     near = swap(near, 1, 0)
     focused, looked, ends = pl.pallas_call(

time: 25.3 us -> 30.6 us (1.21)
  the two profiles are of different devices: /device:TPU:8 before, /device:TPU:3 now
where the time goes in v4:
time: 30.6 us; the launch traced here: 30.4 us
  starting transfers between devices  12.7 us (42%)
  waiting for transfers between devices  10.5 us (34%)
  Pallas kernels  6.6 us (22%)
  between operations  0.71 us (2%)
    ppermute x10, starting transfers between devices, swap(): lax.ppermute(array, 'seg', [(i, neighbour(i, by, odd, devices)) for i in...  11.5 us
    ppermute x10, waiting for transfers between devices, swap(): lax.ppermute(array, 'seg', [(i, neighbour(i, by, odd, devices)) for i in...  8.49 us
    ppermute x1, waiting for transfers between devices, beside(): return lax.ppermute(array, ('arcs', 'seg'), pairs)  1.98 us
    pallas_call x1, Pallas kernels, shards(): pl.pallas_call(migrate_kernel, out_shape=(shape((2, count, gates), BF16),...  1.68 us
    ppermute x1, starting transfers between devices, beside(): return lax.ppermute(array, ('arcs', 'seg'), pairs)  1.2 us
    pallas_call x1, Pallas kernels, shards(): partial2, weights2 = weigh_call()(other, migrated)  0.93 us
    pallas_call x1, Pallas kernels, shards(): partial, weights = weigh_call()(params, migrated)  0.93 us
    pallas_call x1, Pallas kernels, shards(): pl.pallas_call(functools.partial(power_kernel, devices), out_shape=(shape...  0.78 us
  transfers between devices with their start and end apart: 11, of which 6 were waited for; matrix products, arithmetic and copies ran while one was open for 0% of the time, Pallas kernels for 14%

profile of v4, /device:TPU:3, one launch (start us, length us, event | category | flops | bytes accessed | tf_op | source)
XLA Modules:
  0.0 30.4 jit_solution(12727592249062299491)
XLA Ops:
  0.6 1.7 %migrate.1 = (bf16[2,256,256]{2,1,0:T(8,128)(2,1)S(1)}, f32[8,128]{1,0:T(8,128)S(1)}) custom-call(bf16[2,256,256]{2,1,0:T(8,128)(2,1)} %refs_0_.1, f32[1,256]{1,0:T(1,128)} %bitcast.6, s32[1,256]{1,0:T(1,128)} %bitcast.7, s32[1,128]{1,0:T(1,128)} %bitcast.8, s32[1,128]{1,0:T(1,128)} %bitcast.9, f32[1,128]{1,0:T(1,128)} %bitcast.10, f32[1,128]{1,0:T(1,128)} %bitcast.11), custom_call_target="tpu_custom_call" | custom-call | tf_op jit(solution)/shard_map/migrate/pallas_call | solution.py:271
  2.3 0.7 %collective-permute-start.2 = (bf16[2,256,256]{2,1,0:T(8,128)(2,1)S(1)}, bf16[2,256,256]{2,1,0:T(8,128)(2,1)S(1)}, u32[]{:S(2)}, u32[]{:S(2)}) collective-permute-start(bf16[2,256,256]{2,1,0:T(8,128)(2,1)S(1)} %get-tuple-element.16.own_ref), channel_id=1, source_target_pairs={{0,1},{1,0},{2,3},{3,2},{4,8},{5,9},{6,10},{7,11},{8,4},{9,5},{10,... | collective-permute-start | bytes 786440 | tf_op jit(solution)/shard_map/ppermute | solution.py:32
  3.1 1.9 %collective-permute-start.1 = (bf16[2,256,256]{2,1,0:T(8,128)(2,1)S(1)}, bf16[2,256,256]{2,1,0:T(8,128)(2,1)S(1)}, u32[]{:S(2)}, u32[]{:S(2)}) collective-permute-start(bf16[2,256,256]{2,1,0:T(8,128)(2,1)S(1)} %get-tuple-element.16.own_ref), channel_id=1, source_target_pairs={{0,4},{1,5},{2,6},{3,7},{4,0},{5,1},{6,2},{7,3},{8,12},{9,13},{10,... | collective-permute-start | bytes 786440 | tf_op jit(solution)/shard_map/ppermute | solution.py:32
  5.0 0.3 collective-permute-start
  5.2 1.5 %collective-permute-start.6 = (bf16[2,256,256]{2,1,0:T(8,128)(2,1)S(1)}, bf16[2,256,256]{2,1,0:T(8,128)(2,1)S(1)}, u32[]{:S(2)}, u32[]{:S(2)}) collective-permute-start(bf16[2,256,256]{2,1,0:T(8,128)(2,1)S(1)} %get-tuple-element.16.own_ref), channel_id=1, source_target_pairs={{0,1},{1,0},{2,3},{3,2},{4,5},{5,4},{6,7},{7,6},{8,9},{9,8},{10,11... | collective-permute-start | bytes 786440 | tf_op jit(solution)/shard_map/ppermute | solution.py:32
  6.8 0.0 collective-permute-start.3
  6.8 1.2 %collective-permute-done.3.params_ref = f32[8,128]{1,0:T(8,128)S(1)} collective-permute-done((f32[8,128]{1,0:T(8,128)S(1)}, f32[8,128]{1,0:T(8,128)S(1)}, u32[]{:S(2)}, u32[]{:S(2)}) %collective-permute-start.3) | collective-permute-done | bytes 4128 | tf_op jit(solution)/shard_map/ppermute | solution.py:32
  7.9 0.9 %shard_map.88 = (f32[2,128,256]{2,1,0:T(8,128)S(1)}, bf16[2,128,768]{2,1,0:T(8,128)(2,1)S(1)}) custom-call(f32[8,128]{1,0:T(8,128)S(1)} %collective-permute-done.3.params_ref, bf16[2,256,256]{2,1,0:T(8,128)(2,1)S(1)} %get-tuple-element.16.own_ref), custom_call_target="tpu_custom_call" | custom-call | tf_op jit(solution)/shard_map/pallas_call | solution.py:312
  8.9 0.0 collective-permute-done.2.refs_2_
  8.9 1.8 %collective-permute-done.1.refs_1_ = bf16[2,256,256]{2,1,0:T(8,128)(2,1)S(1)} collective-permute-done((bf16[2,256,256]{2,1,0:T(8,128)(2,1)S(1)}, bf16[2,256,256]{2,1,0:T(8,128)(2,1)S(1)}, u32[]{:S(2)}, u32[]{:S(2)}) %collective-permute-start.1) | collective-permute-done | bytes 262176 | tf_op jit(solution)/shard_map/ppermute | solution.py:32
  10.7 0.9 %collective-permute-done.refs_0_ = bf16[2,256,256]{2,1,0:T(8,128)(2,1)S(1)} collective-permute-done((bf16[2,256,256]{2,1,0:T(8,128)(2,1)S(1)}, bf16[2,256,256]{2,1,0:T(8,128)(2,1)S(1)}, u32[]{:S(2)}, u32[]{:S(2)}) %collective-permute-start) | collective-permute-done | bytes 262176 | tf_op jit(solution)/shard_map/ppermute | solution.py:32
  11.6 0.4 %shard_map.89 = bf16[2,128,256]{2,1,0:T(8,128)(2,1)S(1)} custom-call(f32[2,128,256]{2,1,0:T(8,128)S(1)} %get-tuple-element.19.partial_ref, bf16[2,128,768]{2,1,0:T(8,128)(2,1)S(1)} %get-tuple-element.20.weights_ref, bf16[2,256,256]{2,1,0:T(8,128)(2,1)S(1)} %collective-permute-done.refs_0_, bf16[2,256,256]{2,1,0:T(8,128)(2,1)S(1)} %collective-permute-done.1.refs_1_, ...), custom_call_target="tpu_custom_call" | custom-call | tf_op jit(solution)/shard_map/pallas_call | solution.py:320
  12.0 2.2 %collective-permute-start.4 = (bf16[2,128,256]{2,1,0:T(8,128)(2,1)S(1)}, bf16[2,128,256]{2,1,0:T(8,128)(2,1)S(1)}, u32[]{:S(2)}, u32[]{:S(2)}) collective-permute-start(bf16[2,128,256]{2,1,0:T(8,128)(2,1)S(1)} %shard_map.89), channel_id=1, source_target_pairs={{0,1},{1,0},{2,3},{3,2},{4,5},{5,4},{6,7},{7,6},{8,9},{9,8},{10,11... | collective-permute-start | bytes 393224 | tf_op jit(solution)/shard_map/ppermute | solution.py:32
  14.2 0.0 collective-permute-start.5
  14.2 3.4 %collective-permute-done.5.target_ref = f32[8,128]{1,0:T(8,128)S(1)} collective-permute-done((f32[8,128]{1,0:T(8,128)S(1)}, f32[8,128]{1,0:T(8,128)S(1)}, u32[]{:S(2)}, u32[]{:S(2)}) %collective-permute-start.5) | collective-permute-done | bytes 4128 | tf_op jit(solution)/shard_map/ppermute | solution.py:32
  17.5 0.5 %lend_weights.1.w_ref = bf16[2,128,512]{2,1,0:T(8,128)(2,1)S(1)} custom-call(f32[8,128]{1,0:T(8,128)S(1)} %collective-permute-done.5.target_ref), custom_call_target="tpu_custom_call" | custom-call | tf_op jit(solution)/shard_map/lend_weights/pallas_call | solution.py:284
  18.1 0.0 collective-permute-done.6.mate_ref
  18.1 0.3 %lend.1 = (bf16[2,128,256]{2,1,0:T(8,128)(2,1)S(1)}, bf16[2,16,256]{2,1,0:T(8,128)(2,1)S(1)}) custom-call(bf16[2,128,512]{2,1,0:T(8,128)(2,1)S(1)} %lend_weights.1.w_ref, bf16[2,256,256]{2,1,0:T(8,128)(2,1)S(1)} %get-tuple-element.16.own_ref, bf16[2,256,256]{2,1,0:T(8,128)(2,1)S(1)} %collective-permute-done.6.mate_ref), custom_call_target="tpu_custom_call" | custom-call | tf_op jit(solution)/shard_map/lend/pallas_call | solution.py:293
  18.4 0.1 collective-permute-start.7
  18.5 2.4 %collective-permute-start.8 = (bf16[2,16,256]{2,1,0:T(8,128)(2,1)S(1)}, bf16[2,16,256]{2,1,0:T(8,128)(2,1)S(1)}, u32[]{:S(2)}, u32[]{:S(2)}) collective-permute-start(bf16[2,16,256]{2,1,0:T(8,128)(2,1)S(1)} %get-tuple-element.25), channel_id=1, source_target_pairs={{0,1},{1,0},{2,4},{3,5},{4,2},{5,3},{6,8},{7,9},{8,6},{9,7},{10,12... | collective-permute-start | bytes 49160 | tf_op jit(solution)/shard_map/ppermute | solution.py:32
  20.8 0.9 %shard_map.86 = (f32[2,128,256]{2,1,0:T(8,128)S(1)}, bf16[2,128,768]{2,1,0:T(8,128)(2,1)S(1)}) custom-call(f32[8,128]{1,0:T(8,128)S(1)} %get-tuple-element.15.params_ref, bf16[2,256,256]{2,1,0:T(8,128)(2,1)S(1)} %get-tuple-element.16.own_ref), custom_call_target="tpu_custom_call" | custom-call | tf_op jit(solution)/shard_map/pallas_call | solution.py:311
  21.8 0.4 %shard_map.87.keep_ref = f32[2,128,256]{2,1,0:T(8,128)S(1)} custom-call(f32[2,128,256]{2,1,0:T(8,128)S(1)} %get-tuple-element.17.partial_ref, bf16[2,128,768]{2,1,0:T(8,128)(2,1)S(1)} %get-tuple-element.18.weights_ref, bf16[2,256,256]{2,1,0:T(8,128)(2,1)S(1)} %collective-permute-done.refs_0_, bf16[2,256,256]{2,1,0:T(8,128)(2,1)S(1)} %collective-permute-done.1.refs_1_, ...), custom_call_target="tpu_custom_call" | custom-call | tf_op jit(solution)/shard_map/pallas_call | solution.py:321
  22.1 1.2 %collective-permute-done.8.lent_ref = bf16[2,16,256]{2,1,0:T(8,128)(2,1)S(1)} collective-permute-done((bf16[2,16,256]{2,1,0:T(8,128)(2,1)S(1)}, bf16[2,16,256]{2,1,0:T(8,128)(2,1)S(1)}, u32[]{:S(2)}, u32[]{:S(2)}) %collective-permute-start.8) | collective-permute-done | bytes 16416 | tf_op jit(solution)/shard_map/ppermute | solution.py:32
  23.4 0.0 collective-permute-done.4.got_ref
  23.4 2.4 %collective-permute-start.9 = (f32[8,256]{1,0:T(8,128)S(1)}, f32[8,256]{1,0:T(8,128)S(1)}, u32[]{:S(2)}, u32[]{:S(2)}) collective-permute-start(f32[8,256]{1,0:T(8,128)S(1)} %get-tuple-element.26), channel_id=1, source_target_pairs={{0,1},{1,0},{2,3},{3,2},{4,5},{5,4},{6,7},{7,6},{8,9},{9,8},{10,11... | collective-permute-start | bytes 24584 | tf_op jit(solution)/shard_map/ppermute | solution.py:32
  25.8 1.2 %collective-permute-start.10 = (f32[8,256]{1,0:T(8,128)S(1)}, f32[8,256]{1,0:T(8,128)S(1)}, u32[]{:S(2)}, u32[]{:S(2)}) collective-permute-start(f32[8,256]{1,0:T(8,128)S(1)} %get-tuple-element.27), channel_id=1, source_target_pairs={{0,16},{1,2},{2,1},{3,4},{4,3},{5,6},{6,5},{7,8},{8,7},{9,10},{10,... | collective-permute-start | bytes 24584 | tf_op jit(solution)/shard_map/ppermute | solution.py:43
  27.0 0.0 collective-permute-done.7.lent_ref
  27.0 0.8 %power.1 = (bf16[2,128,256]{2,1,0:T(8,128)(2,1)}, f32[128,256]{1,0:T(8,128)}, f32[16,256]{1,0:T(8,128)S(1)}) custom-call(f32[2,128,256]{2,1,0:T(8,128)S(1)} %shard_map.87.keep_ref, bf16[2,128,256]{2,1,0:T(8,128)(2,1)S(1)} %collective-permute-done.4.got_ref, bf16[2,128,256]{2,1,0:T(8,128)(2,1)S(1)} %collective-permute-done.7.lent_ref), custom_call_target="tpu_custom_call" | custom-call | tf_op jit(solution)/shard_map/power/pallas_call | solution.py:333
  27.8 0.0 collective-permute-done.9.near_ref
  27.8 2.0 %collective-permute-done.10.far_ref = f32[8,256]{1,0:T(8,128)S(1)} collective-permute-done((f32[8,256]{1,0:T(8,128)S(1)}, f32[8,256]{1,0:T(8,128)S(1)}, u32[]{:S(2)}, u32[]{:S(2)}) %collective-permute-start.10) | collective-permute-done | bytes 8224 | tf_op jit(solution)/shard_map/ppermute | solution.py:43
  29.8 0.6 %edge.1 = f32[128,256]{1,0:T(8,128)} custom-call(f32[128,256]{1,0:T(8,128)} %get-tuple-element.23.looked_ref, f32[16,256]{1,0:T(8,128)S(1)} %get-tuple-element.24.ends_ref, f32[8,256]{1,0:T(8,128)S(1)} %collective-permute-done.9.near_ref, f32[8,256]{1,0:T(8,128)S(1)} %collective-permute-done.10.far_ref), custom_call_target="tpu_custom_call", output_to_operand_aliasing={{}: (0, {})} | custom-call | tf_op jit(solution)/shard_map/edge/pallas_call | solution.py:342
  (1 shorter events, 0.0 us)
Async XLA Ops:
  2.3 6.5 %collective-permute-start.2 = (bf16[2,256,256]{2,1,0:T(8,128)(2,1)S(1)}, bf16[2,256,256]{2,1,0:T(8,128)(2,1)S(1)}, u32[]{:S(2)}, u32[]{:S(2)}) collective-permute-start(bf16[2,256,256]{2,1,0:T(8,128)(2,1)S(1)} %get-tuple-element.16.own_ref), channel_id=1, source_target_pairs={{0,1},{1,0},{2,3},{3,2},{4,8},{5,9},{6,10},{7,11},{8,4},{9,5},{10,... | collective-permute-start | bytes 786440 | tf_op jit(solution)/shard_map/ppermute | solution.py:32
  3.1 7.6 %collective-permute-start.1 = (bf16[2,256,256]{2,1,0:T(8,128)(2,1)S(1)}, bf16[2,256,256]{2,1,0:T(8,128)(2,1)S(1)}, u32[]{:S(2)}, u32[]{:S(2)}) collective-permute-start(bf16[2,256,256]{2,1,0:T(8,128)(2,1)S(1)} %get-tuple-element.16.own_ref), channel_id=1, source_target_pairs={{0,4},{1,5},{2,6},{3,7},{4,0},{5,1},{6,2},{7,3},{8,12},{9,13},{10,... | collective-permute-start | bytes 786440 | tf_op jit(solution)/shard_map/ppermute | solution.py:32
  5.0 6.6 %collective-permute-start = (bf16[2,256,256]{2,1,0:T(8,128)(2,1)S(1)}, bf16[2,256,256]{2,1,0:T(8,128)(2,1)S(1)}, u32[]{:S(2)}, u32[]{:S(2)}) collective-permute-start(bf16[2,256,256]{2,1,0:T(8,128)(2,1)S(1)} %get-tuple-element.16.own_ref), channel_id=1, source_target_pairs={{0,2},{1,3},{2,0},{3,1},{4,6},{5,7},{6,4},{7,5},{8,10},{9,11},{10,... | collective-permute-start | bytes 786440 | tf_op jit(solution)/shard_map/ppermute | solution.py:32
  5.2 12.8 %collective-permute-start.6 = (bf16[2,256,256]{2,1,0:T(8,128)(2,1)S(1)}, bf16[2,256,256]{2,1,0:T(8,128)(2,1)S(1)}, u32[]{:S(2)}, u32[]{:S(2)}) collective-permute-start(bf16[2,256,256]{2,1,0:T(8,128)(2,1)S(1)} %get-tuple-element.16.own_ref), channel_id=1, source_target_pairs={{0,1},{1,0},{2,3},{3,2},{4,5},{5,4},{6,7},{7,6},{8,9},{9,8},{10,11... | collective-permute-start | bytes 786440 | tf_op jit(solution)/shard_map/ppermute | solution.py:32
  6.8 1.2 %collective-permute-start.3 = (f32[8,128]{1,0:T(8,128)S(1)}, f32[8,128]{1,0:T(8,128)S(1)}, u32[]{:S(2)}, u32[]{:S(2)}) collective-permute-start(f32[8,128]{1,0:T(8,128)S(1)} %get-tuple-element.15.params_ref), channel_id=1, source_target_pairs={{0,1},{1,0},{2,3},{3,2},{4,5},{5,4},{6,7},{7,6},{8,9},{9,8},{10,11... | collective-permute-start | bytes 12296 | tf_op jit(solution)/shard_map/ppermute | solution.py:32
  12.0 11.4 %collective-permute-start.4 = (bf16[2,128,256]{2,1,0:T(8,128)(2,1)S(1)}, bf16[2,128,256]{2,1,0:T(8,128)(2,1)S(1)}, u32[]{:S(2)}, u32[]{:S(2)}) collective-permute-start(bf16[2,128,256]{2,1,0:T(8,128)(2,1)S(1)} %shard_map.89), channel_id=1, source_target_pairs={{0,1},{1,0},{2,3},{3,2},{4,5},{5,4},{6,7},{7,6},{8,9},{9,8},{10,11... | collective-permute-start | bytes 393224 | tf_op jit(solution)/shard_map/ppermute | solution.py:32
  14.2 3.4 %collective-permute-start.5 = (f32[8,128]{1,0:T(8,128)S(1)}, f32[8,128]{1,0:T(8,128)S(1)}, u32[]{:S(2)}, u32[]{:S(2)}) collective-permute-start(f32[8,128]{1,0:T(8,128)S(1)} %get-tuple-element.15.params_ref), channel_id=1, source_target_pairs={{0,1},{1,0},{2,4},{3,5},{4,2},{5,3},{6,8},{7,9},{8,6},{9,7},{10,12... | collective-permute-start | bytes 12296 | tf_op jit(solution)/shard_map/ppermute | solution.py:32
  18.4 8.6 %collective-permute-start.7 = (bf16[2,128,256]{2,1,0:T(8,128)(2,1)S(1)}, bf16[2,128,256]{2,1,0:T(8,128)(2,1)S(1)}, u32[]{:S(2)}, u32[]{:S(2)}) collective-permute-start(bf16[2,128,256]{2,1,0:T(8,128)(2,1)S(1)} %get-tuple-element.21), channel_id=1, source_target_pairs={{0,1},{1,0},{2,4},{3,5},{4,2},{5,3},{6,8},{7,9},{8,6},{9,7},{10,12... | collective-permute-start | bytes 393224 | tf_op jit(solution)/shard_map/ppermute | solution.py:32
  18.5 4.9 %collective-permute-start.8 = (bf16[2,16,256]{2,1,0:T(8,128)(2,1)S(1)}, bf16[2,16,256]{2,1,0:T(8,128)(2,1)S(1)}, u32[]{:S(2)}, u32[]{:S(2)}) collective-permute-start(bf16[2,16,256]{2,1,0:T(8,128)(2,1)S(1)} %get-tuple-element.25), channel_id=1, source_target_pairs={{0,1},{1,0},{2,4},{3,5},{4,2},{5,3},{6,8},{7,9},{8,6},{9,7},{10,12... | collective-permute-start | bytes 49160 | tf_op jit(solution)/shard_map/ppermute | solution.py:32
  23.4 4.4 %collective-permute-start.9 = (f32[8,256]{1,0:T(8,128)S(1)}, f32[8,256]{1,0:T(8,128)S(1)}, u32[]{:S(2)}, u32[]{:S(2)}) collective-permute-start(f32[8,256]{1,0:T(8,128)S(1)} %get-tuple-element.26), channel_id=1, source_target_pairs={{0,1},{1,0},{2,3},{3,2},{4,5},{5,4},{6,7},{7,6},{8,9},{9,8},{10,11... | collective-permute-start | bytes 24584 | tf_op jit(solution)/shard_map/ppermute | solution.py:32
  25.8 4.0 %collective-permute-start.10 = (f32[8,256]{1,0:T(8,128)S(1)}, f32[8,256]{1,0:T(8,128)S(1)}, u32[]{:S(2)}, u32[]{:S(2)}) collective-permute-start(f32[8,256]{1,0:T(8,128)S(1)} %get-tuple-element.27), channel_id=1, source_target_pairs={{0,16},{1,2},{2,1},{3,4},{4,3},{5,6},{6,5},{7,8},{8,7},{9,10},{10,... | collective-permute-start | bytes 24584 | tf_op jit(solution)/shard_map/ppermute | solution.py:43

commit v5 on v4

--- a/solution.py
+++ b/solution.py
@@ -59,22 +59,23 @@
     params_ref[4:8, :] = jnp.zeros((4, params_ref.shape[1]), F32)
     spare = jnp.zeros((6, count), F32)
     turned[...] = jnp.transpose(jnp.concatenate([fraction_ref[...], shift_ref[...].astype(F32), spare], 0))
-    copies[0].wait()
     rows = 64
     lane = lax.broadcasted_iota(jnp.int32, (rows, 128), 1)
     pick = functools.partial(jnp.take_along_axis, axis=1, mode="promise_in_bounds")
+    plans = []
     for r in range(0, count, rows):
         fraction = jnp.broadcast_to(turned[r : r + rows, 0:1], (rows, 128))
         shift = jnp.broadcast_to(turned[r : r + rows, 1:2], (rows, 128)).astype(jnp.int32)
-        terms = [(by, (lane + by) & 127, part) for by, part in ((shift, 1.0 - fraction), (shift + 1, fraction))]
+        plans.append((r, [(lane + shift, 1.0 - fraction), (lane + shift + 1, fraction)]))
+    copies[0].wait()
+    for r, terms in plans:
         for part in range(2):
             tiles = [pulses_ref[part, r : r + rows, at : at + 128].astype(F32) for at in range(0, gates, 128)]
             total = [0.0] * len(tiles)
-            for by, at, scale in terms:
-                inside = lane + by < 128
-                moved = [pick(t, at) for t in tiles] + [0.0]
+            for at, scale in terms:
+                moved = [pick(t, at & 127) for t in tiles] + [0.0]
                 for j in range(len(tiles)):
-                    total[j] += scale * jnp.where(inside, moved[j], moved[j + 1])
+                    total[j] += scale * jnp.where(at < 128, moved[j], moved[j + 1])
             for j, value in enumerate(total):
                 out_ref[part, r : r + rows, j * 128 : (j + 1) * 128] = value.astype(BF16)
 

time: 30.6 us -> 30.6 us (level)
  no operation moved by 1% of the time
where the time goes in v5:
time: 30.6 us; the launch traced here: 30.4 us
  starting transfers between devices  12.7 us (42%)
  waiting for transfers between devices  10.5 us (34%)
  Pallas kernels  6.56 us (21%)
  between operations  0.71 us (2%)
    ppermute x10, starting transfers between devices, swap(): lax.ppermute(array, 'seg', [(i, neighbour(i, by, odd, devices)) for i in...  11.5 us
    ppermute x10, waiting for transfers between devices, swap(): lax.ppermute(array, 'seg', [(i, neighbour(i, by, odd, devices)) for i in...  8.49 us
    ppermute x1, waiting for transfers between devices, beside(): return lax.ppermute(array, ('arcs', 'seg'), pairs)  1.98 us
    pallas_call x1, Pallas kernels, shards(): pl.pallas_call(migrate_kernel, out_shape=(shape((2, count, gates), BF16),...  1.65 us
    ppermute x1, starting transfers between devices, beside(): return lax.ppermute(array, ('arcs', 'seg'), pairs)  1.2 us
    pallas_call x1, Pallas kernels, shards(): partial2, weights2 = weigh_call()(other, migrated)  0.93 us
    pallas_call x1, Pallas kernels, shards(): partial, weights = weigh_call()(params, migrated)  0.93 us
    pallas_call x1, Pallas kernels, shards(): pl.pallas_call(functools.partial(power_kernel, devices), out_shape=(shape...  0.78 us
  transfers between devices with their start and end apart: 11, of which 6 were waited for; matrix products, arithmetic and copies ran while one was open for 0% of the time, Pallas kernels for 14%

profile of v5, /device:TPU:3, one launch (start us, length us, event | category | flops | bytes accessed | tf_op | source)
XLA Modules:
  0.0 30.4 jit_solution(17936494171109109511)
XLA Ops:
  0.6 1.7 %migrate.1 = (bf16[2,256,256]{2,1,0:T(8,128)(2,1)S(1)}, f32[8,128]{1,0:T(8,128)S(1)}) custom-call(bf16[2,256,256]{2,1,0:T(8,128)(2,1)} %refs_0_.1, f32[1,256]{1,0:T(1,128)} %bitcast.6, s32[1,256]{1,0:T(1,128)} %bitcast.7, s32[1,128]{1,0:T(1,128)} %bitcast.8, s32[1,128]{1,0:T(1,128)} %bitcast.9, f32[1,128]{1,0:T(1,128)} %bitcast.10, f32[1,128]{1,0:T(1,128)} %bitcast.11), custom_call_target="tpu_custom_call" | custom-call | tf_op jit(solution)/shard_map/migrate/pallas_call | solution.py:272
  2.3 0.7 %collective-permute-start.2 = (bf16[2,256,256]{2,1,0:T(8,128)(2,1)S(1)}, bf16[2,256,256]{2,1,0:T(8,128)(2,1)S(1)}, u32[]{:S(2)}, u32[]{:S(2)}) collective-permute-start(bf16[2,256,256]{2,1,0:T(8,128)(2,1)S(1)} %get-tuple-element.16.own_ref), channel_id=1, source_target_pairs={{0,1},{1,0},{2,3},{3,2},{4,8},{5,9},{6,10},{7,11},{8,4},{9,5},{10,... | collective-permute-start | bytes 786440 | tf_op jit(solution)/shard_map/ppermute | solution.py:32
  3.0 1.9 %collective-permute-start.1 = (bf16[2,256,256]{2,1,0:T(8,128)(2,1)S(1)}, bf16[2,256,256]{2,1,0:T(8,128)(2,1)S(1)}, u32[]{:S(2)}, u32[]{:S(2)}) collective-permute-start(bf16[2,256,256]{2,1,0:T(8,128)(2,1)S(1)} %get-tuple-element.16.own_ref), channel_id=1, source_target_pairs={{0,4},{1,5},{2,6},{3,7},{4,0},{5,1},{6,2},{7,3},{8,12},{9,13},{10,... | collective-permute-start | bytes 786440 | tf_op jit(solution)/shard_map/ppermute | solution.py:32
  5.0 0.3 collective-permute-start
  5.2 1.5 %collective-permute-start.6 = (bf16[2,256,256]{2,1,0:T(8,128)(2,1)S(1)}, bf16[2,256,256]{2,1,0:T(8,128)(2,1)S(1)}, u32[]{:S(2)}, u32[]{:S(2)}) collective-permute-start(bf16[2,256,256]{2,1,0:T(8,128)(2,1)S(1)} %get-tuple-element.16.own_ref), channel_id=1, source_target_pairs={{0,1},{1,0},{2,3},{3,2},{4,5},{5,4},{6,7},{7,6},{8,9},{9,8},{10,11... | collective-permute-start | bytes 786440 | tf_op jit(solution)/shard_map/ppermute | solution.py:32
  6.7 0.0 collective-permute-start.3
  6.7 1.2 %collective-permute-done.3.params_ref = f32[8,128]{1,0:T(8,128)S(1)} collective-permute-done((f32[8,128]{1,0:T(8,128)S(1)}, f32[8,128]{1,0:T(8,128)S(1)}, u32[]{:S(2)}, u32[]{:S(2)}) %collective-permute-start.3) | collective-permute-done | bytes 4128 | tf_op jit(solution)/shard_map/ppermute | solution.py:32
  7.9 0.9 %shard_map.88 = (f32[2,128,256]{2,1,0:T(8,128)S(1)}, bf16[2,128,768]{2,1,0:T(8,128)(2,1)S(1)}) custom-call(f32[8,128]{1,0:T(8,128)S(1)} %collective-permute-done.3.params_ref, bf16[2,256,256]{2,1,0:T(8,128)(2,1)S(1)} %get-tuple-element.16.own_ref), custom_call_target="tpu_custom_call" | custom-call | tf_op jit(solution)/shard_map/pallas_call | solution.py:313
  8.8 0.0 collective-permute-done.2.refs_2_
  8.8 1.8 %collective-permute-done.1.refs_1_ = bf16[2,256,256]{2,1,0:T(8,128)(2,1)S(1)} collective-permute-done((bf16[2,256,256]{2,1,0:T(8,128)(2,1)S(1)}, bf16[2,256,256]{2,1,0:T(8,128)(2,1)S(1)}, u32[]{:S(2)}, u32[]{:S(2)}) %collective-permute-start.1) | collective-permute-done | bytes 262176 | tf_op jit(solution)/shard_map/ppermute | solution.py:32
  10.7 0.9 %collective-permute-done.refs_0_ = bf16[2,256,256]{2,1,0:T(8,128)(2,1)S(1)} collective-permute-done((bf16[2,256,256]{2,1,0:T(8,128)(2,1)S(1)}, bf16[2,256,256]{2,1,0:T(8,128)(2,1)S(1)}, u32[]{:S(2)}, u32[]{:S(2)}) %collective-permute-start) | collective-permute-done | bytes 262176 | tf_op jit(solution)/shard_map/ppermute | solution.py:32
  11.6 0.4 %shard_map.89 = bf16[2,128,256]{2,1,0:T(8,128)(2,1)S(1)} custom-call(f32[2,128,256]{2,1,0:T(8,128)S(1)} %get-tuple-element.19.partial_ref, bf16[2,128,768]{2,1,0:T(8,128)(2,1)S(1)} %get-tuple-element.20.weights_ref, bf16[2,256,256]{2,1,0:T(8,128)(2,1)S(1)} %collective-permute-done.refs_0_, bf16[2,256,256]{2,1,0:T(8,128)(2,1)S(1)} %collective-permute-done.1.refs_1_, ...), custom_call_target="tpu_custom_call" | custom-call | tf_op jit(solution)/shard_map/pallas_call | solution.py:321
  12.0 2.2 %collective-permute-start.4 = (bf16[2,128,256]{2,1,0:T(8,128)(2,1)S(1)}, bf16[2,128,256]{2,1,0:T(8,128)(2,1)S(1)}, u32[]{:S(2)}, u32[]{:S(2)}) collective-permute-start(bf16[2,128,256]{2,1,0:T(8,128)(2,1)S(1)} %shard_map.89), channel_id=1, source_target_pairs={{0,1},{1,0},{2,3},{3,2},{4,5},{5,4},{6,7},{7,6},{8,9},{9,8},{10,11... | collective-permute-start | bytes 393224 | tf_op jit(solution)/shard_map/ppermute | solution.py:32
  14.1 0.0 collective-permute-start.5
  14.1 3.4 %collective-permute-done.5.target_ref = f32[8,128]{1,0:T(8,128)S(1)} collective-permute-done((f32[8,128]{1,0:T(8,128)S(1)}, f32[8,128]{1,0:T(8,128)S(1)}, u32[]{:S(2)}, u32[]{:S(2)}) %collective-permute-start.5) | collective-permute-done | bytes 4128 | tf_op jit(solution)/shard_map/ppermute | solution.py:32
  17.5 0.5 %lend_weights.1.w_ref = bf16[2,128,512]{2,1,0:T(8,128)(2,1)S(1)} custom-call(f32[8,128]{1,0:T(8,128)S(1)} %collective-permute-done.5.target_ref), custom_call_target="tpu_custom_call" | custom-call | tf_op jit(solution)/shard_map/lend_weights/pallas_call | solution.py:285
  18.0 0.0 collective-permute-done.6.mate_ref
  18.0 0.3 %lend.1 = (bf16[2,128,256]{2,1,0:T(8,128)(2,1)S(1)}, bf16[2,16,256]{2,1,0:T(8,128)(2,1)S(1)}) custom-call(bf16[2,128,512]{2,1,0:T(8,128)(2,1)S(1)} %lend_weights.1.w_ref, bf16[2,256,256]{2,1,0:T(8,128)(2,1)S(1)} %get-tuple-element.16.own_ref, bf16[2,256,256]{2,1,0:T(8,128)(2,1)S(1)} %collective-permute-done.6.mate_ref), custom_call_target="tpu_custom_call" | custom-call | tf_op jit(solution)/shard_map/lend/pallas_call | solution.py:294
  18.4 0.1 collective-permute-start.7
  18.4 2.4 %collective-permute-start.8 = (bf16[2,16,256]{2,1,0:T(8,128)(2,1)S(1)}, bf16[2,16,256]{2,1,0:T(8,128)(2,1)S(1)}, u32[]{:S(2)}, u32[]{:S(2)}) collective-permute-start(bf16[2,16,256]{2,1,0:T(8,128)(2,1)S(1)} %get-tuple-element.25), channel_id=1, source_target_pairs={{0,1},{1,0},{2,4},{3,5},{4,2},{5,3},{6,8},{7,9},{8,6},{9,7},{10,12... | collective-permute-start | bytes 49160 | tf_op jit(solution)/shard_map/ppermute | solution.py:32
  20.8 0.9 %shard_map.86 = (f32[2,128,256]{2,1,0:T(8,128)S(1)}, bf16[2,128,768]{2,1,0:T(8,128)(2,1)S(1)}) custom-call(f32[8,128]{1,0:T(8,128)S(1)} %get-tuple-element.15.params_ref, bf16[2,256,256]{2,1,0:T(8,128)(2,1)S(1)} %get-tuple-element.16.own_ref), custom_call_target="tpu_custom_call" | custom-call | tf_op jit(solution)/shard_map/pallas_call | solution.py:312
  21.7 0.4 %shard_map.87.keep_ref = f32[2,128,256]{2,1,0:T(8,128)S(1)} custom-call(f32[2,128,256]{2,1,0:T(8,128)S(1)} %get-tuple-element.17.partial_ref, bf16[2,128,768]{2,1,0:T(8,128)(2,1)S(1)} %get-tuple-element.18.weights_ref, bf16[2,256,256]{2,1,0:T(8,128)(2,1)S(1)} %collective-permute-done.refs_0_, bf16[2,256,256]{2,1,0:T(8,128)(2,1)S(1)} %collective-permute-done.1.refs_1_, ...), custom_call_target="tpu_custom_call" | custom-call | tf_op jit(solution)/shard_map/pallas_call | solution.py:322
  22.1 1.2 %collective-permute-done.8.lent_ref = bf16[2,16,256]{2,1,0:T(8,128)(2,1)S(1)} collective-permute-done((bf16[2,16,256]{2,1,0:T(8,128)(2,1)S(1)}, bf16[2,16,256]{2,1,0:T(8,128)(2,1)S(1)}, u32[]{:S(2)}, u32[]{:S(2)}) %collective-permute-start.8) | collective-permute-done | bytes 16416 | tf_op jit(solution)/shard_map/ppermute | solution.py:32
  23.3 0.0 collective-permute-done.4.got_ref
  23.3 2.4 %collective-permute-start.9 = (f32[8,256]{1,0:T(8,128)S(1)}, f32[8,256]{1,0:T(8,128)S(1)}, u32[]{:S(2)}, u32[]{:S(2)}) collective-permute-start(f32[8,256]{1,0:T(8,128)S(1)} %get-tuple-element.26), channel_id=1, source_target_pairs={{0,1},{1,0},{2,3},{3,2},{4,5},{5,4},{6,7},{7,6},{8,9},{9,8},{10,11... | collective-permute-start | bytes 24584 | tf_op jit(solution)/shard_map/ppermute | solution.py:32
  25.8 1.2 %collective-permute-start.10 = (f32[8,256]{1,0:T(8,128)S(1)}, f32[8,256]{1,0:T(8,128)S(1)}, u32[]{:S(2)}, u32[]{:S(2)}) collective-permute-start(f32[8,256]{1,0:T(8,128)S(1)} %get-tuple-element.27), channel_id=1, source_target_pairs={{0,16},{1,2},{2,1},{3,4},{4,3},{5,6},{6,5},{7,8},{8,7},{9,10},{10,... | collective-permute-start | bytes 24584 | tf_op jit(solution)/shard_map/ppermute | solution.py:43
  27.0 0.0 collective-permute-done.7.lent_ref
  27.0 0.8 %power.1 = (bf16[2,128,256]{2,1,0:T(8,128)(2,1)}, f32[128,256]{1,0:T(8,128)}, f32[16,256]{1,0:T(8,128)S(1)}) custom-call(f32[2,128,256]{2,1,0:T(8,128)S(1)} %shard_map.87.keep_ref, bf16[2,128,256]{2,1,0:T(8,128)(2,1)S(1)} %collective-permute-done.4.got_ref, bf16[2,128,256]{2,1,0:T(8,128)(2,1)S(1)} %collective-permute-done.7.lent_ref), custom_call_target="tpu_custom_call" | custom-call | tf_op jit(solution)/shard_map/power/pallas_call | solution.py:334
  27.8 0.0 collective-permute-done.9.near_ref
  27.8 2.0 %collective-permute-done.10.far_ref = f32[8,256]{1,0:T(8,128)S(1)} collective-permute-done((f32[8,256]{1,0:T(8,128)S(1)}, f32[8,256]{1,0:T(8,128)S(1)}, u32[]{:S(2)}, u32[]{:S(2)}) %collective-permute-start.10) | collective-permute-done | bytes 8224 | tf_op jit(solution)/shard_map/ppermute | solution.py:43
  29.8 0.6 %edge.1 = f32[128,256]{1,0:T(8,128)} custom-call(f32[128,256]{1,0:T(8,128)} %get-tuple-element.23.looked_ref, f32[16,256]{1,0:T(8,128)S(1)} %get-tuple-element.24.ends_ref, f32[8,256]{1,0:T(8,128)S(1)} %collective-permute-done.9.near_ref, f32[8,256]{1,0:T(8,128)S(1)} %collective-permute-done.10.far_ref), custom_call_target="tpu_custom_call", output_to_operand_aliasing={{}: (0, {})} | custom-call | tf_op jit(solution)/shard_map/edge/pallas_call | solution.py:343
  (1 shorter events, 0.0 us)
Async XLA Ops:
  2.3 6.5 %collective-permute-start.2 = (bf16[2,256,256]{2,1,0:T(8,128)(2,1)S(1)}, bf16[2,256,256]{2,1,0:T(8,128)(2,1)S(1)}, u32[]{:S(2)}, u32[]{:S(2)}) collective-permute-start(bf16[2,256,256]{2,1,0:T(8,128)(2,1)S(1)} %get-tuple-element.16.own_ref), channel_id=1, source_target_pairs={{0,1},{1,0},{2,3},{3,2},{4,8},{5,9},{6,10},{7,11},{8,4},{9,5},{10,... | collective-permute-start | bytes 786440 | tf_op jit(solution)/shard_map/ppermute | solution.py:32
  3.0 7.6 %collective-permute-start.1 = (bf16[2,256,256]{2,1,0:T(8,128)(2,1)S(1)}, bf16[2,256,256]{2,1,0:T(8,128)(2,1)S(1)}, u32[]{:S(2)}, u32[]{:S(2)}) collective-permute-start(bf16[2,256,256]{2,1,0:T(8,128)(2,1)S(1)} %get-tuple-element.16.own_ref), channel_id=1, source_target_pairs={{0,4},{1,5},{2,6},{3,7},{4,0},{5,1},{6,2},{7,3},{8,12},{9,13},{10,... | collective-permute-start | bytes 786440 | tf_op jit(solution)/shard_map/ppermute | solution.py:32
  5.0 6.6 %collective-permute-start = (bf16[2,256,256]{2,1,0:T(8,128)(2,1)S(1)}, bf16[2,256,256]{2,1,0:T(8,128)(2,1)S(1)}, u32[]{:S(2)}, u32[]{:S(2)}) collective-permute-start(bf16[2,256,256]{2,1,0:T(8,128)(2,1)S(1)} %get-tuple-element.16.own_ref), channel_id=1, source_target_pairs={{0,2},{1,3},{2,0},{3,1},{4,6},{5,7},{6,4},{7,5},{8,10},{9,11},{10,... | collective-permute-start | bytes 786440 | tf_op jit(solution)/shard_map/ppermute | solution.py:32
  5.2 12.8 %collective-permute-start.6 = (bf16[2,256,256]{2,1,0:T(8,128)(2,1)S(1)}, bf16[2,256,256]{2,1,0:T(8,128)(2,1)S(1)}, u32[]{:S(2)}, u32[]{:S(2)}) collective-permute-start(bf16[2,256,256]{2,1,0:T(8,128)(2,1)S(1)} %get-tuple-element.16.own_ref), channel_id=1, source_target_pairs={{0,1},{1,0},{2,3},{3,2},{4,5},{5,4},{6,7},{7,6},{8,9},{9,8},{10,11... | collective-permute-start | bytes 786440 | tf_op jit(solution)/shard_map/ppermute | solution.py:32
  6.7 1.2 %collective-permute-start.3 = (f32[8,128]{1,0:T(8,128)S(1)}, f32[8,128]{1,0:T(8,128)S(1)}, u32[]{:S(2)}, u32[]{:S(2)}) collective-permute-start(f32[8,128]{1,0:T(8,128)S(1)} %get-tuple-element.15.params_ref), channel_id=1, source_target_pairs={{0,1},{1,0},{2,3},{3,2},{4,5},{5,4},{6,7},{7,6},{8,9},{9,8},{10,11... | collective-permute-start | bytes 12296 | tf_op jit(solution)/shard_map/ppermute | solution.py:32
  12.0 11.4 %collective-permute-start.4 = (bf16[2,128,256]{2,1,0:T(8,128)(2,1)S(1)}, bf16[2,128,256]{2,1,0:T(8,128)(2,1)S(1)}, u32[]{:S(2)}, u32[]{:S(2)}) collective-permute-start(bf16[2,128,256]{2,1,0:T(8,128)(2,1)S(1)} %shard_map.89), channel_id=1, source_target_pairs={{0,1},{1,0},{2,3},{3,2},{4,5},{5,4},{6,7},{7,6},{8,9},{9,8},{10,11... | collective-permute-start | bytes 393224 | tf_op jit(solution)/shard_map/ppermute | solution.py:32
  14.1 3.4 %collective-permute-start.5 = (f32[8,128]{1,0:T(8,128)S(1)}, f32[8,128]{1,0:T(8,128)S(1)}, u32[]{:S(2)}, u32[]{:S(2)}) collective-permute-start(f32[8,128]{1,0:T(8,128)S(1)} %get-tuple-element.15.params_ref), channel_id=1, source_target_pairs={{0,1},{1,0},{2,4},{3,5},{4,2},{5,3},{6,8},{7,9},{8,6},{9,7},{10,12... | collective-permute-start | bytes 12296 | tf_op jit(solution)/shard_map/ppermute | solution.py:32
  18.4 8.6 %collective-permute-start.7 = (bf16[2,128,256]{2,1,0:T(8,128)(2,1)S(1)}, bf16[2,128,256]{2,1,0:T(8,128)(2,1)S(1)}, u32[]{:S(2)}, u32[]{:S(2)}) collective-permute-start(bf16[2,128,256]{2,1,0:T(8,128)(2,1)S(1)} %get-tuple-element.21), channel_id=1, source_target_pairs={{0,1},{1,0},{2,4},{3,5},{4,2},{5,3},{6,8},{7,9},{8,6},{9,7},{10,12... | collective-permute-start | bytes 393224 | tf_op jit(solution)/shard_map/ppermute | solution.py:32
  18.4 4.9 %collective-permute-start.8 = (bf16[2,16,256]{2,1,0:T(8,128)(2,1)S(1)}, bf16[2,16,256]{2,1,0:T(8,128)(2,1)S(1)}, u32[]{:S(2)}, u32[]{:S(2)}) collective-permute-start(bf16[2,16,256]{2,1,0:T(8,128)(2,1)S(1)} %get-tuple-element.25), channel_id=1, source_target_pairs={{0,1},{1,0},{2,4},{3,5},{4,2},{5,3},{6,8},{7,9},{8,6},{9,7},{10,12... | collective-permute-start | bytes 49160 | tf_op jit(solution)/shard_map/ppermute | solution.py:32
  23.3 4.4 %collective-permute-start.9 = (f32[8,256]{1,0:T(8,128)S(1)}, f32[8,256]{1,0:T(8,128)S(1)}, u32[]{:S(2)}, u32[]{:S(2)}) collective-permute-start(f32[8,256]{1,0:T(8,128)S(1)} %get-tuple-element.26), channel_id=1, source_target_pairs={{0,1},{1,0},{2,3},{3,2},{4,5},{5,4},{6,7},{7,6},{8,9},{9,8},{10,11... | collective-permute-start | bytes 24584 | tf_op jit(solution)/shard_map/ppermute | solution.py:32
  25.8 4.0 %collective-permute-start.10 = (f32[8,256]{1,0:T(8,128)S(1)}, f32[8,256]{1,0:T(8,128)S(1)}, u32[]{:S(2)}, u32[]{:S(2)}) collective-permute-start(f32[8,256]{1,0:T(8,128)S(1)} %get-tuple-element.27), channel_id=1, source_target_pairs={{0,16},{1,2},{2,1},{3,4},{4,3},{5,6},{6,5},{7,8},{8,7},{9,10},{10,... | collective-permute-start | bytes 24584 | tf_op jit(solution)/shard_map/ppermute | solution.py:43
